TPU v7x, 128 devices: a whole 4x4x4 slice. The times are simulated.
128 devices in a mesh: lon: 16 (over z, x_lo, core), lat: 8 (over x_hi, y).
Axes of the slice: x: 4 (x_hi: 2, x_lo: 2; x = x_hi * 2 + x_lo), y: 4, z: 4, core: 2. Of those that a mesh axis runs over, the one named last changes fastest.
Arguments:
- tracers: float32 [2, 25, 512, 6144], P(None, None, 'lat', 'lon'), may hold values from -6 to 6
- east_speed: float32 [25, 512, 6144], P(None, 'lat', 'lon'), may hold values from -3 to 3
- north_speed: float32 [25, 512, 6144], P(None, 'lat', 'lon'), may hold values from -3 to 3
- wet: int32 [512, 6144], P('lat', 'lon'), may hold values 0 or 1
- fold_partner: int32 [6144], P('lon'), may hold values from 0 to 6143, as said below
- bergs: float32 [524288, 128], P(('lon', 'lat')), may hold values from -6 to 6
- berg_count: int32 [16384], P(('lon', 'lat')), may hold values from 0 to 32, as said below
- berg_cell: int32 [524288], P(('lon', 'lat')), may hold values from 0 to 24575
- melt_map: float32 [128, 50], replicated, may hold values from -0.5 to 0.5
Outputs:
- updated: float32 [2, 25, 512, 6144], P(None, None, 'lat', 'lon')
Inputs may be any that keep to these rules, and one draw needn't show every extreme that they name: fold_partner is a permutation; the partner of column i lies among the 384 columns of block 15 - i // 384, blocks of 384 columns. `berg_count`: every source has a full owner, and some owner is full from every source.
All inputs are finite; a program needn't handle non-finite values. No bound on the sum of `wet` on one device may be relied on, other than what follows from the above.
Results may differ from a plain program's by a relative error of at most 0.000067.
Values sent between devices are 32-bit elements; how exact they have to be, the bound alone decides.
No kernel may reach another device: no remote copies, remote signals or barrier semaphores. Data moves between devices by JAX's collectives and lax.ppermute only.
A program may use at most 192 MiB of HBM per device.

v0:
```python
import jax
import jax.numpy as jnp
from jax import lax
from jax.sharding import PartitionSpec as P

diffuse_h = 0.1
diffuse_v = 0.1
time_step = 0.5


def with_halo(value, sides, width, wrap):
    for axis, dim in sides:
        devices, length = (lax.axis_size(axis), value.shape[dim])
        up = [(i, (i + 1) % devices) for i in range(devices if wrap else devices - 1)]
        down = [(j, i) for i, j in up]
        last = lax.slice_in_dim(value, length - width, length, axis=dim)
        initial = lax.slice_in_dim(value, 0, width, axis=dim)
        before = lax.ppermute(last, axis, up)
        after = lax.ppermute(initial, axis, down)
        value = jnp.concatenate([before, value, after], axis=dim)
    return value


def from_partner(block, axis, distance):
    count = lax.axis_size(axis)
    route = []
    for low in range(count):
        high = low | 1 << distance
        if high != low and high < count:
            route += [(low, high), (high, low)]
    return lax.ppermute(block, axis, route)


def face_flux(value, speed, wetness, value_next, speed_next, wet_next):
    face = wetness * wet_next
    return face * (
        0.5 * (speed + speed_next) * (0.5 * (value + value_next)) - diffuse_h * (value_next - value)
    )


def vertical_mix(tracers):
    zero_level = jnp.zeros_like(tracers[:, :1])
    step_diff = tracers[:, 1:] - tracers[:, :-1]
    upper = jnp.concatenate([step_diff, zero_level], axis=1)
    lower = jnp.concatenate([zero_level, step_diff], axis=1)
    return diffuse_v * upper - diffuse_v * lower


def shards(
    tracers, east_speed, north_speed, wet, fold_partner, bergs, berg_count, berg_cell, melt_map
):
    lon_count = lax.axis_size("lon")
    lat_count = lax.axis_size("lat")
    lon_index = lax.axis_index("lon")
    lat_index = lax.axis_index("lat")
    levels = tracers.shape[1]
    rows_here = tracers.shape[2]
    cols_here = tracers.shape[3]
    wetness = wet.astype(jnp.float32)[None, None]
    wet_levels = jnp.broadcast_to(wetness, (1, levels, rows_here, cols_here))
    east_state = jnp.concatenate([tracers, east_speed[None], wet_levels], axis=0)
    east_padded = with_halo(east_state, (("lon", 3),), 1, True)
    faces_e = face_flux(
        east_padded[:2, :, :, :-1],
        east_padded[2:3, :, :, :-1],
        east_padded[3:4, :, :, :-1],
        east_padded[:2, :, :, 1:],
        east_padded[2:3, :, :, 1:],
        east_padded[3:4, :, :, 1:],
    )
    flux_w = faces_e[..., :-1]
    flux_e = faces_e[..., 1:]
    north_state = jnp.concatenate([tracers, north_speed[None], wet_levels], axis=0)
    across = north_state[:, :, rows_here - 1 :, :]
    for bit_number in range(lon_count.bit_length() - 1):
        across = from_partner(across, "lon", bit_number)
    picks = fold_partner - (lon_count - 1 - lon_index) * cols_here
    picked = jnp.take(across, picks, axis=3)
    fold_row = jnp.concatenate([picked[:2], -picked[2:3], picked[3:]], axis=0)
    north_padded = with_halo(north_state, (("lat", 2),), 1, False)
    north_ghost = jnp.where(
        lat_index == lat_count - 1, fold_row, north_padded[:, :, rows_here + 1 :, :]
    )
    north_padded = jnp.concatenate([north_padded[:, :, : rows_here + 1, :], north_ghost], axis=2)
    faces_n = face_flux(
        north_padded[:2, :, :-1],
        north_padded[2:3, :, :-1],
        north_padded[3:4, :, :-1],
        north_padded[:2, :, 1:],
        north_padded[2:3, :, 1:],
        north_padded[3:4, :, 1:],
    )
    flux_s = faces_n[:, :, :-1]
    flux_n = faces_n[:, :, 1:]
    vertical = vertical_mix(tracers)
    device_count = lon_count * lat_count
    slot_count = bergs.shape[0] // device_count
    live = (jnp.arange(slot_count, dtype=jnp.int32)[None, :] < berg_count[:, None]).astype(
        jnp.float32
    )
    loaded = bergs.reshape(device_count, slot_count, bergs.shape[1]) * live[:, :, None]
    melt = jnp.einsum(
        "psc,cm->mps",
        lax.all_to_all(loaded, ("lon", "lat"), split_axis=0, concat_axis=0, tiled=True),
        melt_map,
        precision=lax.Precision.HIGHEST,
    )
    melt = melt.reshape(melt.shape[0], device_count * slot_count)
    sources = (
        jnp.zeros((melt.shape[0], rows_here * cols_here), jnp.float32).at[:, berg_cell].add(melt)
    )
    sources = sources.reshape(tracers.shape[0], levels, rows_here, cols_here)
    tendency = vertical - (flux_e - flux_w) - (flux_n - flux_s)
    return wetness * (tracers + time_step * tendency + sources)


def solution(mesh):
    in_specs = (
        P(None, None, "lat", "lon"),
        P(None, "lat", "lon"),
        P(None, "lat", "lon"),
        P("lat", "lon"),
        P("lon"),
        P(("lon", "lat"), None),
        P(("lon", "lat")),
        P(("lon", "lat")),
        P(),
    )
    out_specs = P(None, None, "lat", "lon")
    return jax.shard_map(shards, mesh=mesh, in_specs=in_specs, out_specs=out_specs, check_vma=False)
```

profile of v0, /device:TPU:4, one launch (start us, length us, event | category | flops | bytes accessed | tf_op | source)
XLA Modules:
  0.0 179.2 jit_solution(12002425162361298436)
XLA Ops:
  1.2 5.6 %pad_maximum_fusion.1 = (f32[4,25,64,384]{3,2,1,0:T(8,128)S(1)}, f32[4,25,64,384]{3,2,1,0:T(8,128)S(1)}) fusion(f32[1,25,64,384]{3,2,1,0:T(8,128)S(1)} %broadcast_in_dim.35, f32[2,25,64,384]{3,2,1,0:T(8,128)} %param.9, f32[1,25,64,384]{3,2,1,0:T(8,128)} %bitcast.39, f32[1,25,64,384]{3,2,1,0:T(8,128)} %bitcast.36), kind=kLoop, calls=%fused_computation.3 | loop fusion | flops 9830400 | bytes 31948800 | tf_op jit(solution)/shard_map/concatenate | solution.py:61
  7.8 3.5 %collective-permute-start.2 = (f32[4,25,1,384]{3,2,1,0:T(1,128)}, f32[4,25,1,384]{3,2,1,0:T(1,128)S(1)}, u32[]{:S(2)}, u32[]{:S(2)}) collective-permute-start(f32[4,25,1,384]{3,2,1,0:T(1,128)} %get-tuple-element.17), channel_id=1, source_target_pairs={{0,1},{1,2},{2,3},{3,4},{4,5},{5,6},{6,7},{8,9},{9,10},{10,11},{11... | collective-permute-start | bytes 460808 | tf_op jit(solution)/shard_map/ppermute | solution.py:18
  11.3 4.0 %fusion.17 = (f32[4,25,64,1]{3,2,1,0:T(8,128)}, f32[4,25,64,1]{3,2,1,0:T(8,128)}) fusion(f32[4,25,64,384]{3,2,1,0:T(8,128)S(1)} %get-tuple-element.19), kind=kLoop, calls=%fused_computation.45 | loop fusion | bytes 102400 | tf_op jit(solution)/shard_map/slice | solution.py:16
  15.2 2.6 %copy.32 = f32[4,25,64,1]{2,0,3,1:T(4,128)S(1)} copy(f32[4,25,64,1]{3,2,1,0:T(8,128)} %get-tuple-element.13) | data formatting | bytes 51200 | tf_op jit(solution)/shard_map/slice | solution.py:16
  18.2 2.6 %copy.34 = f32[4,25,64,1]{2,0,3,1:T(4,128)S(1)} copy(f32[4,25,64,1]{3,2,1,0:T(8,128)} %get-tuple-element.14) | data formatting | bytes 51200 | tf_op jit(solution)/shard_map/slice | solution.py:17
  20.8 4.4 %collective-permute-start.1 = (f32[4,25,64,1]{2,0,3,1:T(4,128)S(1)}, f32[4,25,64,1]{2,0,3,1:T(4,128)S(1)}, u32[]{:S(2)}, u32[]{:S(2)}) collective-permute-start(f32[4,25,64,1]{2,0,3,1:T(4,128)S(1)} %copy.34), channel_id=1, source_target_pairs={{8,0},{16,8},{24,16},{32,24},{40,32},{48,40},{56,48},{64,56},{72,6... | collective-permute-start | bytes 76808 | tf_op jit(solution)/shard_map/ppermute | solution.py:19
  25.2 5.4 %collective-permute-start.7 = (f32[4,25,1,384]{3,2,1,0:T(1,128)}, f32[4,25,1,384]{3,2,1,0:T(1,128)}, u32[]{:S(2)}, u32[]{:S(2)}) collective-permute-start(f32[4,25,1,384]{3,2,1,0:T(1,128)} %get-tuple-element.18), channel_id=1, source_target_pairs={{1,0},{2,1},{3,2},{4,3},{5,4},{6,5},{7,6},{9,8},{10,9},{11,10},{12... | collective-permute-start | bytes 460808 | tf_op jit(solution)/shard_map/ppermute | solution.py:19
  30.7 3.6 %broadcast_multiply_fusion = f32[128,32,128]{2,1,0:T(8,128)} fusion(f32[128,32,128]{2,1,0:T(8,128)} %bitcast.46, f32[128,32]{1,0:T(8,128)S(1)} %fusion.14), kind=kLoop, calls=%fused_computation.33 | loop fusion | flops 524288 | bytes 4210688 | tf_op jit(solution)/shard_map/mul | solution.py:101
  34.2 7.0 %all-to-all-start = ((f32[128,32,128]{2,1,0:T(8,128)}), f32[128,32,128]{2,1,0:T(8,128)}, u32[]{:S(2)}, u32[]{:S(2)}) async-start(f32[128,32,128]{2,1,0:T(8,128)} %broadcast_multiply_fusion), calls=%async_computation | async-start | bytes 4194304 | tf_op jit(solution)/shard_map/all_to_all | solution.py:104
  41.3 7.1 %slice_subtract_fusion.2 = f32[2,24,64,384]{3,2,1,0:T(8,128)} fusion(f32[2,25,64,384]{3,2,1,0:T(8,128)} %param.9), kind=kLoop, calls=%fused_computation.22 | loop fusion | flops 1179648 | bytes 14155776 | tf_op jit(solution)/shard_map/sub | solution.py:43
  54.6 17.7 %maximum_maximum_fusion = (f32[4,25,64,385]{3,2,1,0:T(8,128)}, f32[4,25,64,385]{3,2,1,0:T(8,128)}) fusion(f32[1,25,64,384]{3,2,1,0:T(8,128)S(1)} %broadcast_in_dim.35, f32[1,25,64,384]{3,2,1,0:T(8,128)} %bitcast.40, f32[2,25,64,384]{3,2,1,0:T(8,128)} %param.9, f32[4,25,64,1]{3,2,1,0:T(8,128)} %copy.33, f32[4,25,64,1]{3,2,1,0:T(8,128)} %copy.35), kind=kLoop, calls=%fused_computation.4 | loop fusion | flops 14784000 | bytes 29593600 | tf_op jit(solution)/shard_map/concatenate | solution.py:20
  74.1 5.9 %fusion.10 = (f32[25,64,385]{2,1,0:T(8,128)}, f32[25,64,385]{2,1,0:T(8,128)}) fusion(f32[4,25,64,1]{3,2,1,0:T(8,128)} %copy.35, f32[1,25,64,384]{3,2,1,0:T(8,128)S(1)} %broadcast_in_dim.35, f32[1,25,64,384]{3,2,1,0:T(8,128)} %bitcast.41, f32[2,25,64,384]{3,2,1,0:T(8,128)S(1)} %bitcast.31, f32[4,25,64,1]{3,2,1,0:T(8,128)S(1)} %copy-done.1), kind=kLoop, calls=%fused_computation.27 | loop fusion | flops 9240000 | bytes 14809600 | tf_op jit(solution)/shard_map/mul | solution.py:36
  80.0 3.5 %collective-permute-start.6 = (f32[4,25,1,384]{3,2,1,0:T(1,128)S(1)}, f32[4,25,1,384]{3,2,1,0:T(1,128)}, u32[]{:S(2)}, u32[]{:S(2)}) collective-permute-start(f32[4,25,1,384]{3,2,1,0:T(1,128)S(1)} %collective-permute-done.5), channel_id=1, source_target_pairs={{0,64},{64,0},{8,72},{72,8},{16,80},{80,16},{24,88},{88,24},{32,96... | collective-permute-start | bytes 460808 | tf_op jit(solution)/shard_map/ppermute | solution.py:31
  83.4 10.6 %subtract_multiply_fusion = f32[2,25,64,385]{3,2,1,0:T(8,128)} fusion(f32[4,25,64,385]{3,2,1,0:T(8,128)} %get-tuple-element.12, f32[4,25,64,385]{3,2,1,0:T(8,128)} %get-tuple-element.11, f32[25,64,385]{2,1,0:T(8,128)} %get-tuple-element.8, f32[25,64,385]{2,1,0:T(8,128)} %get-tuple-element.7), kind=kLoop, calls=%fused_computation.10 | loop fusion | flops 7392000 | bytes 19712000 | tf_op jit(solution)/shard_map/mul | solution.py:36
  95.2 2.5 %gather_fusion = f32[384,4,25]{2,1,0:T(4,128)} fusion(f32[4,25,384]{1,0,2:T(4,128)S(1)} %bitcast.47, s32[1024]{0:T(1024)S(1)} %pad_clamp_fusion), kind=kCustom, calls=%fused_computation | custom fusion | bytes 308736 | tf_op jit(solution)/shard_map/jit(_take)/gather | solution.py:78
  100.8 3.9 %fusion.13 = (f32[25,65,384]{2,1,0:T(8,128)S(1)}, f32[25,65,384]{2,1,0:T(8,128)S(1)}) fusion(f32[4,25,1,384]{3,2,1,0:T(1,128)S(1)} %broadcast_select_fusion.1, f32[1,25,64,384]{3,2,1,0:T(8,128)S(1)} %broadcast_in_dim.35, f32[1,25,64,384]{3,2,1,0:T(8,128)} %bitcast.37, f32[2,25,64,384]{3,2,1,0:T(8,128)} %param.9, f32[4,25,1,384]{3,2,1,0:T(1,128)S(1)} %collective-permute-done.2), kind=kLoop, calls=%fused_computation.32 | loop fusion | flops 9360000 | bytes 15129600 | tf_op jit(solution)/shard_map/mul | solution.py:36
  104.7 6.0 %maximum_maximum_fusion.1 = (f32[4,25,65,384]{3,2,1,0:T(8,128)S(1)}, f32[4,25,65,384]{3,2,1,0:T(8,128)}) fusion(f32[1,25,64,384]{3,2,1,0:T(8,128)S(1)} %broadcast_in_dim.35, f32[1,25,64,384]{3,2,1,0:T(8,128)S(1)} %bitcast.38, f32[2,25,64,384]{3,2,1,0:T(8,128)S(1)} %bitcast.33, f32[4,25,1,384]{3,2,1,0:T(1,128)S(1)} %collective-permute-done.2, ...), kind=kLoop, calls=%fused_computation.8 | loop fusion | flops 14976000 | bytes 30105600 | tf_op jit(solution)/shard_map/concatenate | solution.py:20
  110.7 5.0 %subtract_multiply_fusion.1 = f32[2,25,65,384]{3,2,1,0:T(8,128)} fusion(f32[4,25,65,384]{3,2,1,0:T(8,128)} %get-tuple-element.16, f32[4,25,65,384]{3,2,1,0:T(8,128)S(1)} %get-tuple-element.15, f32[25,65,384]{2,1,0:T(8,128)S(1)} %get-tuple-element.10, f32[25,65,384]{2,1,0:T(8,128)S(1)} %get-tuple-element.9), kind=kLoop, calls=%fused_computation.13 | loop fusion | flops 7488000 | bytes 19968000 | tf_op jit(solution)/shard_map/mul | solution.py:36
  115.7 3.4 %fusion.15 = f32[128,32,50]{2,1,0:T(8,128)S(1)} fusion(f32[128,32,128]{2,1,0:T(8,128)} %all-to-all-done, f32[128,50]{0,1:T(8,128)S(1)} %copy-done), kind=kOutput, calls=%fused_computation.40 | convolution fusion | flops 314572800 | bytes 2941952 | tf_op jit(solution)/shard_map/psc,cm->mps/dot_general | solution.py:102
  119.1 27.6 %scatter_custom_fusion = f32[50,24576]{0,1:T(8,128)} fusion(s32[4096]{0:T(1024)S(1)} %compare_select_fusion, f32[4096,50]{1,0:T(8,128)S(1)} %bitcast.45, f32[]{:T(128)} %constant.14.clone.1), kind=kCustom, calls=%fused_computation.11 | custom fusion | flops 204800 | bytes 4915204 | tf_op jit(solution)/shard_map/scatter-add | solution.py:110
  146.8 9.7 %copy.42 = f32[50,24576]{1,0:T(8,128)} copy(f32[50,24576]{0,1:T(8,128)} %scatter_custom_fusion) | data formatting | bytes 9830400 | tf_op jit(solution)/shard_map/scatter-add | solution.py:110
  156.5 3.7 %copy.49 = f32[7,8,64,384]{3,2,1,0:T(8,128)S(1)} copy(f32[7,8,64,384]{3,1,2,0:T(8,128)} %bitcast.42) | data formatting | bytes 11010048
  160.2 2.6 %slice.127 = f32[50,64,384]{2,1,0:T(8,128)} slice(f32[56,64,384]{2,1,0:T(8,128)S(1)} %bitcast.43), slice={[0:50], [0:64], [0:384]} | slice | bytes 9830400
  162.8 16.4 %fusion.6 = f32[2,25,64,384]{3,2,1,0:T(8,128)} fusion(f32[2,25,64,384]{3,2,1,0:T(8,128)} %bitcast.44, f32[2,25,64,384]{3,2,1,0:T(8,128)S(1)} %bitcast.35, f32[2,25,65,384]{3,2,1,0:T(8,128)} %subtract_multiply_fusion.1, f32[2,25,64,385]{3,2,1,0:T(8,128)} %subtract_multiply_fusion, f32[2,24,64,384]{3,2,1,0:T(8,128)} %slice_subtract_fusion.2, ...), kind=kLoop, calls=%fused_computation.19 | loop fusion | flops 13516800 | bytes 39223296 | tf_op jit(solution)/shard_map/mul | solution.py:114
  (55 shorter events, 14.7 us)
Async XLA Ops:
  0.0 115.7 %copy-start = (f32[128,50]{0,1:T(8,128)S(1)}, f32[128,50]{0,1:T(8,128)}, u32[]{:S(2)}) copy-start(f32[128,50]{0,1:T(8,128)} %param.17) | copy-start | bytes 76804
  7.8 45.6 %collective-permute-start.3 = (f32[4,25,1,384]{3,2,1,0:T(1,128)}, f32[4,25,1,384]{3,2,1,0:T(1,128)}, u32[]{:S(2)}, u32[]{:S(2)}) collective-permute-start(f32[4,25,1,384]{3,2,1,0:T(1,128)} %get-tuple-element.17), channel_id=1, source_target_pairs={{0,8},{8,0},{16,24},{24,16},{32,40},{40,32},{48,56},{56,48},{64,72... | collective-permute-start | bytes 460808 | tf_op jit(solution)/shard_map/ppermute | solution.py:31
  7.8 93.0 %collective-permute-start.2 = (f32[4,25,1,384]{3,2,1,0:T(1,128)}, f32[4,25,1,384]{3,2,1,0:T(1,128)S(1)}, u32[]{:S(2)}, u32[]{:S(2)}) collective-permute-start(f32[4,25,1,384]{3,2,1,0:T(1,128)} %get-tuple-element.17), channel_id=1, source_target_pairs={{0,1},{1,2},{2,3},{3,4},{4,5},{5,6},{6,7},{8,9},{9,10},{10,11},{11... | collective-permute-start | bytes 460808 | tf_op jit(solution)/shard_map/ppermute | solution.py:18
  15.2 15.3 %copy-start.5 = (s32[128]{0:T(128)S(1)}, s32[128]{0:T(128)}, u32[]{:S(2)}) copy-start(s32[128]{0:T(128)} %param.15) | copy-start | bytes 1540
  17.9 30.6 %collective-permute-start = (f32[4,25,64,1]{2,0,3,1:T(4,128)S(1)}, f32[4,25,64,1]{2,0,3,1:T(4,128)S(1)}, u32[]{:S(2)}, u32[]{:S(2)}) collective-permute-start(f32[4,25,64,1]{2,0,3,1:T(4,128)S(1)} %copy.32), channel_id=1, source_target_pairs={{0,8},{8,16},{16,24},{24,32},{32,40},{40,48},{48,56},{56,64},{64,7... | collective-permute-start | bytes 76808 | tf_op jit(solution)/shard_map/ppermute | solution.py:18
  20.8 30.1 %collective-permute-start.1 = (f32[4,25,64,1]{2,0,3,1:T(4,128)S(1)}, f32[4,25,64,1]{2,0,3,1:T(4,128)S(1)}, u32[]{:S(2)}, u32[]{:S(2)}) collective-permute-start(f32[4,25,64,1]{2,0,3,1:T(4,128)S(1)} %copy.34), channel_id=1, source_target_pairs={{8,0},{16,8},{24,16},{32,24},{40,32},{48,40},{56,48},{64,56},{72,6... | collective-permute-start | bytes 76808 | tf_op jit(solution)/shard_map/ppermute | solution.py:19
  25.2 74.2 %collective-permute-start.7 = (f32[4,25,1,384]{3,2,1,0:T(1,128)}, f32[4,25,1,384]{3,2,1,0:T(1,128)}, u32[]{:S(2)}, u32[]{:S(2)}) collective-permute-start(f32[4,25,1,384]{3,2,1,0:T(1,128)} %get-tuple-element.18), channel_id=1, source_target_pairs={{1,0},{2,1},{3,2},{4,3},{5,4},{6,5},{7,6},{9,8},{10,9},{11,10},{12... | collective-permute-start | bytes 460808 | tf_op jit(solution)/shard_map/ppermute | solution.py:19
  34.2 81.5 %all-to-all-start = ((f32[128,32,128]{2,1,0:T(8,128)}), f32[128,32,128]{2,1,0:T(8,128)}, u32[]{:S(2)}, u32[]{:S(2)}) async-start(f32[128,32,128]{2,1,0:T(8,128)} %broadcast_multiply_fusion), calls=%async_computation | async-start | bytes 4194304 | tf_op jit(solution)/shard_map/all_to_all | solution.py:104
  41.3 7.1 %copy-start.3 = (s32[4096]{0:T(1024)S(1)}, s32[4096]{0:T(1024)}, u32[]{:S(2)}) copy-start(s32[4096]{0:T(1024)} %param.16) | copy-start | bytes 49156
  41.3 7.1 %copy-start.4 = (s32[384]{0:T(512)S(1)}, s32[384]{0:T(512)}, u32[]{:S(2)}) copy-start(s32[384]{0:T(512)} %param.13) | copy-start | bytes 4612
  50.9 23.1 %slice-start = ((s8[4915200]{0:T(1024)(128)(4,1)}), s8[720896]{0:T(1024)(128)(4,1)S(1)}, s32[]{:S(2)}) async-start(s8[4915200]{0:T(1024)(128)(4,1)} %bitcast.30), calls=%async_computation.1 | async-start | bytes 1441792
  53.4 20.7 %slice-start.1 = ((s8[4915200]{0:T(1024)(128)(4,1)}), s8[4194304]{0:T(1024)(128)(4,1)S(1)}, s32[]{:S(2)}) async-start(s8[4915200]{0:T(1024)(128)(4,1)} %bitcast.30), calls=%async_computation.2 | async-start | bytes 8388608
  53.4 20.7 %copy-start.1 = (f32[4,25,64,1]{3,2,1,0:T(8,128)S(1)}, f32[4,25,64,1]{3,2,1,0:T(8,128)}, u32[]{:S(2)}) copy-start(f32[4,25,64,1]{3,2,1,0:T(8,128)} %copy.33) | copy-start | bytes 76804
  53.4 19.0 %collective-permute-start.4 = (f32[4,25,1,384]{3,2,1,0:T(1,128)}, f32[4,25,1,384]{3,2,1,0:T(1,128)S(1)}, u32[]{:S(2)}, u32[]{:S(2)}) collective-permute-start(f32[4,25,1,384]{3,2,1,0:T(1,128)} %collective-permute-done.3), channel_id=1, source_target_pairs={{0,16},{16,0},{8,24},{24,8},{32,48},{48,32},{40,56},{56,40},{64,80... | collective-permute-start | bytes 460808 | tf_op jit(solution)/shard_map/ppermute | solution.py:31
  72.3 7.6 %collective-permute-start.5 = (f32[4,25,1,384]{3,2,1,0:T(1,128)S(1)}, f32[4,25,1,384]{3,2,1,0:T(1,128)S(1)}, u32[]{:S(2)}, u32[]{:S(2)}) collective-permute-start(f32[4,25,1,384]{3,2,1,0:T(1,128)S(1)} %collective-permute-done.4), channel_id=1, source_target_pairs={{0,32},{32,0},{8,40},{40,8},{16,48},{48,16},{24,56},{56,24},{64,96... | collective-permute-start | bytes 460808 | tf_op jit(solution)/shard_map/ppermute | solution.py:31
  80.0 14.0 %collective-permute-start.6 = (f32[4,25,1,384]{3,2,1,0:T(1,128)S(1)}, f32[4,25,1,384]{3,2,1,0:T(1,128)}, u32[]{:S(2)}, u32[]{:S(2)}) collective-permute-start(f32[4,25,1,384]{3,2,1,0:T(1,128)S(1)} %collective-permute-done.5), channel_id=1, source_target_pairs={{0,64},{64,0},{8,72},{72,8},{16,80},{80,16},{24,88},{88,24},{32,96... | collective-permute-start | bytes 460808 | tf_op jit(solution)/shard_map/ppermute | solution.py:31
  99.5 5.2 %slice-start.2 = ((s8[4915200]{0:T(1024)(128)(4,1)}), s8[4194304]{0:T(1024)(128)(4,1)S(1)}, s32[]{:S(2)}) async-start(s8[4915200]{0:T(1024)(128)(4,1)} %bitcast.32), calls=%async_computation.3 | async-start | bytes 8388608
  100.8 3.9 %slice-start.3 = ((s8[4915200]{0:T(1024)(128)(4,1)}), s8[720896]{0:T(1024)(128)(4,1)S(1)}, s32[]{:S(2)}) async-start(s8[4915200]{0:T(1024)(128)(4,1)} %bitcast.32), calls=%async_computation.4 | async-start | bytes 1441792
  100.8 3.9 %copy-start.2 = (f32[25,64,384]{2,1,0:T(8,128)S(1)}, f32[25,64,384]{2,1,0:T(8,128)}, u32[]{:S(2)}) copy-start(f32[25,64,384]{2,1,0:T(8,128)} %param.11) | copy-start | bytes 7372804
  146.8 16.0 %slice-start.4 = ((s8[4915200]{0:T(1024)(128)(4,1)}), s8[720896]{0:T(1024)(128)(4,1)S(1)}, s32[]{:S(2)}) async-start(s8[4915200]{0:T(1024)(128)(4,1)} %bitcast.34), calls=%async_computation.5 | async-start | bytes 1441792
  156.5 6.3 %slice-start.5 = ((s8[4915200]{0:T(1024)(128)(4,1)}), s8[4194304]{0:T(1024)(128)(4,1)S(1)}, s32[]{:S(2)}) async-start(s8[4915200]{0:T(1024)(128)(4,1)} %bitcast.34), calls=%async_computation.6 | async-start | bytes 8388608
where the time goes:
time: 180 us; the launch traced here: 179 us
  other arithmetic  112 us (62%)
  local copies, waits for them, and re-layouts  36.6 us (20%)
  starting transfers between devices  27 us (15%)
  matrix products  3.44 us (2%)
    scatter-add x1, other arithmetic, shards(): jnp.zeros((melt.shape[0], rows_here * cols_here), jnp.float32)  27.6 us
    mul x4, other arithmetic, face_flux(): face * (0.5 * (speed + speed_next) * (0.5 * (value + value_next)) - diffu...  25.3 us
    concatenate x2, other arithmetic, with_halo(): value = jnp.concatenate([before, value, after], axis=dim)  23.7 us
    mul x1, other arithmetic, shards(): return wetness * (tracers + time_step * tendency + sources)  16.4 us
    ppermute x2, starting transfers between devices, with_halo(): after = lax.ppermute(initial, axis, down)  9.73 us
    scatter-add x1, local copies, waits for them, and re-layouts, shards(): jnp.zeros((melt.shape[0], rows_here * cols_here), jnp.float32)  9.72 us
    slice x3, local copies, waits for them, and re-layouts, with_halo(): last = lax.slice_in_dim(value, length - width, length, axis=dim)  7.57 us
    sub x1, other arithmetic, vertical_mix(): step_diff = tracers[:, 1:] - tracers[:, :-1]  7.09 us
  transfers between devices with their start and end apart: 9, of which 0 were waited for; matrix products, arithmetic and copies ran while one was open for 45% of the time, Pallas kernels for 0%

commit v1 on v0

v1 whole, which is shorter than its diff:
```python
import functools

import jax
import jax.numpy as jnp
from jax import lax
from jax.experimental import pallas as pl
from jax.experimental.pallas import tpu as pltpu
from jax.sharding import PartitionSpec as P

diffuse_h = 0.1
diffuse_v = 0.1
time_step = 0.5

F32 = jnp.float32
BF16 = jnp.bfloat16
VM = pltpu.VMEM
VMEM_SPEC = pl.BlockSpec(memory_space=pltpu.VMEM)
SMEM_SPEC = pl.BlockSpec(memory_space=pltpu.SMEM)
ANY_SPEC = pl.BlockSpec(memory_space=pl.ANY)
LIMIT = 48 << 20

TR_LANES = 32
HALF = 64
WET_LANE = 127
ROW_LANE = 50
COL_LANE = 51
GROUP = 8


def split(value):
    high = value.astype(BF16)
    low = (value - high.astype(F32)).astype(BF16)
    return high, low


def dot_nt(a, b):
    return lax.dot_general(a, b, (((1,), (1,)), ((), ())), preferred_element_type=F32)


def dot_nn(a, b):
    return lax.dot_general(a, b, (((1,), (0,)), ((), ())), preferred_element_type=F32)


def melt_kernel(count_ref, berg_ref, map_ref, out_ref, weight_ref):
    maps = map_ref.shape[0]
    width = berg_ref.shape[1]
    owners = out_ref.shape[0]
    pairs = out_ref.shape[1]
    rows = owners * pairs
    weight_ref[...] = jnp.zeros_like(weight_ref)
    weight_ref[0:maps, 0:width] = map_ref[...]
    weight_ref[HALF : HALF + maps, width : 2 * width] = map_ref[...]
    w_high, w_low = split(weight_ref[...])
    even = berg_ref[pl.ds(0, rows, stride=2), :]
    odd = berg_ref[pl.ds(1, rows, stride=2), :]
    both = jnp.concatenate([even, odd], axis=1)
    b_high, b_low = split(both)
    made = dot_nt(b_high, w_high) + (dot_nt(b_high, w_low) + dot_nt(b_low, w_high))
    lane = lax.broadcasted_iota(jnp.int32, (pairs, 128), 1)
    slot = 2 * lax.broadcasted_iota(jnp.int32, (pairs, 128), 0) + (lane >= HALF).astype(jnp.int32)
    first = pl.program_id(0) * owners
    for o in range(owners):
        out_ref[o] = jnp.where(
            slot < count_ref[first + o], made[o * pairs : (o + 1) * pairs], 0.0
        )


def melt_rows(bergs, berg_count, melt_map):
    owners = berg_count.shape[0]
    slots = bergs.shape[0] // owners
    width = bergs.shape[1]
    steps = 4
    per = owners // steps
    return pl.pallas_call(
        melt_kernel,
        grid=(steps,),
        out_shape=jax.ShapeDtypeStruct((owners, slots // 2, 128), F32),
        in_specs=[
            SMEM_SPEC,
            pl.BlockSpec((per * slots, width), lambda i: (i, 0)),
            pl.BlockSpec(melt_map.shape[::-1], lambda i: (0, 0)),
        ],
        out_specs=pl.BlockSpec((per, slots // 2, 128), lambda i: (i, 0, 0)),
        scratch_shapes=[VM((128, 2 * width), F32)],
        compiler_params=pltpu.CompilerParams(vmem_limit_bytes=LIMIT),
        name="melt",
    )(berg_count, bergs, melt_map.T)


def stencil_kernel(
    tr_hbm, ea_hbm, no_hbm, wet_ref,
    part_hbm, ew_a, ew_b, ns_a, ns_b,
    tv, ev, nv, ov, m_e, m_n, wetf, west, east, sem_t, sem_e, sem_n, sem_o,
):
    levels, rows, cols = ea_hbm.shape
    strips = rows // 8

    def copies(k):
        return (
            pltpu.make_async_copy(tr_hbm.at[:, k], tv.at[:, k], sem_t.at[k]),
            pltpu.make_async_copy(ea_hbm.at[k], ev.at[k], sem_e.at[k]),
            pltpu.make_async_copy(no_hbm.at[k], nv.at[k], sem_n.at[k]),
        )

    def start_level(k, _):
        for c in copies(k):
            c.start()
        return _

    lax.fori_loop(0, levels, start_level, 0)

    odd_lon = lax.rem(lax.axis_index("lon"), 2)
    odd_lat = lax.rem(lax.axis_index("lat"), 2)
    row_a = odd_lat * (rows - 1)
    row_b = (1 - odd_lat) * (rows - 1)

    wet = wet_ref[...].astype(F32)
    wetf[...] = wet
    col = lax.broadcasted_iota(jnp.int32, (rows, cols), 1)
    row = lax.broadcasted_iota(jnp.int32, (rows, cols), 0)
    m_e[...] = jnp.where(col == cols - 1, 0.0, wet * pltpu.roll(wet, cols - 1, 1))
    m_n[...] = jnp.where(row == rows - 1, 0.0, wet * pltpu.roll(wet, rows - 1, 0))
    lane_all = lax.broadcasted_iota(jnp.int32, (rows, 128), 1)
    west[...] = jnp.where(lane_all == WET_LANE, wet[:, 0:1], 0.0)
    east[...] = jnp.where(lane_all == WET_LANE, wet[:, cols - 1 : cols], 0.0)
    ns_a[...] = jnp.zeros_like(ns_a)
    ns_b[...] = jnp.zeros_like(ns_b)
    ns_a[3 * levels : 3 * levels + 1, :] = wetf[pl.ds(row_a, 1), :]
    ns_b[3 * levels : 3 * levels + 1, :] = wetf[pl.ds(row_b, 1), :]

    lane = lax.broadcasted_iota(jnp.int32, (8, 128), 1)
    top = lax.broadcasted_iota(jnp.int32, (8, cols), 0) == 0

    def next_row(ref, lead, s):
        if s < strips - 1:
            return ref[lead + (pl.ds(8 * s + 1, 8), slice(None))]
        return pltpu.roll(ref[lead + (pl.ds(8 * s, 8), slice(None))], 7, 0)

    for c in copies(0):
        c.wait()

    def level(k, _):
        above = jnp.minimum(k + 1, levels - 1)
        below = jnp.maximum(k - 1, 0)

        @pl.when(k + 1 < levels)
        def _wait():
            for c in copies(k + 1):
                c.wait()

        in_0 = lane == k
        in_1 = lane == TR_LANES + k
        in_s = (lane == HALF + k) | (lane == HALF + TR_LANES + k)
        carried = [None, None]
        for s in range(strips):
            here = pl.ds(8 * s, 8)
            u = ev[k, here, :]
            v = nv[k, here, :]
            me = m_e[here, :]
            mn = m_n[here, :]
            w = wetf[here, :]
            s_e = (0.25 * time_step * me) * (u + pltpu.roll(u, cols - 1, 1))
            s_n = (0.25 * time_step * mn) * (v + next_row(nv, (k,), s))
            d_e = (diffuse_h * time_step) * me
            d_n = (diffuse_h * time_step) * mn
            a_e, b_e, a_n, b_n = s_e + d_e, s_e - d_e, s_n + d_n, s_n - d_n
            q_both = []
            for t in range(2):
                q = tv[t, k, here, :]
                q_both.append(q)
                up = tv[t, above, here, :]
                dn = tv[t, below, here, :]
                fe = q * a_e + pltpu.roll(q, cols - 1, 1) * b_e
                fn = q * a_n + next_row(tv, (t, k), s) * b_n
                fw = pltpu.roll(fe, 1, 1)
                turned = pltpu.roll(fn, 1, 0)
                last = jnp.zeros_like(turned) if carried[t] is None else carried[t]
                fs = jnp.where(top, last, turned)
                carried[t] = turned
                mix = (diffuse_v * time_step) * ((up - q) - (q - dn))
                ov[t, k, here, :] = w * (q + ((mix - (fe - fw)) - (fn - fs)))
            for ref, at in ((west, 0), (east, cols - 1)):
                old = ref[here, :]
                old = jnp.where(in_0, q_both[0][:, at : at + 1], old)
                old = jnp.where(in_1, q_both[1][:, at : at + 1], old)
                ref[here, :] = jnp.where(in_s, u[:, at : at + 1], old)
        for ref, at in ((ns_a, row_a), (ns_b, row_b)):
            ref[pl.ds(k, 1), :] = tv[0, k, pl.ds(at, 1), :]
            ref[pl.ds(levels + k, 1), :] = tv[1, k, pl.ds(at, 1), :]
            ref[pl.ds(2 * levels + k, 1), :] = nv[k, pl.ds(at, 1), :]
        pltpu.make_async_copy(ov.at[:, k], part_hbm.at[:, k], sem_o.at[k]).start()
        return _

    lax.fori_loop(0, levels, level, 0)
    is_odd = odd_lon == 1
    ew_a[...] = jnp.where(is_odd, west[...], east[...])
    ew_b[...] = jnp.where(is_odd, east[...], west[...])

    def finish(k, _):
        pltpu.make_async_copy(ov.at[:, k], part_hbm.at[:, k], sem_o.at[k]).wait()
        return _

    lax.fori_loop(0, levels, finish, 0)


def stencil(tracers, east_speed, north_speed, wet):
    count, levels, rows, cols = tracers.shape
    edge_rows = -(-(3 * levels + 1) // 8) * 8
    dma = pltpu.SemaphoreType.DMA((levels,))
    return pl.pallas_call(
        stencil_kernel,
        out_shape=(
            jax.ShapeDtypeStruct(tracers.shape, F32),
            jax.ShapeDtypeStruct((rows, 128), F32),
            jax.ShapeDtypeStruct((rows, 128), F32),
            jax.ShapeDtypeStruct((edge_rows, cols), F32),
            jax.ShapeDtypeStruct((edge_rows, cols), F32),
        ),
        in_specs=[ANY_SPEC, ANY_SPEC, ANY_SPEC, VMEM_SPEC],
        out_specs=(ANY_SPEC, VMEM_SPEC, VMEM_SPEC, VMEM_SPEC, VMEM_SPEC),
        scratch_shapes=[
            VM(tracers.shape, F32),
            VM(east_speed.shape, F32),
            VM(north_speed.shape, F32),
            VM(tracers.shape, F32),
            VM((rows, cols), F32),
            VM((rows, cols), F32),
            VM((rows, cols), F32),
            VM((rows, 128), F32),
            VM((rows, 128), F32),
            dma,
            dma,
            dma,
            dma,
        ],
        compiler_params=pltpu.CompilerParams(vmem_limit_bytes=LIMIT),
        name="stencil",
    )(tracers, east_speed, north_speed, wet)


def fix_kernel(
    fold_ref, ew_a, ew_b, ns_a, ns_b, ew_a_in, ew_b_in, ns_a_in, ns_b_in,
    fix_e, fix_w, fix_n, fix_s, north, south,
):
    levels = fix_n.shape[0] // 2
    cols = ns_a.shape[1]
    lon_count, lat_count = lax.axis_size("lon"), lax.axis_size("lat")
    lon_index, lat_index = lax.axis_index("lon"), lax.axis_index("lat")
    odd_lon = lax.rem(lon_index, 2) == 1
    odd_lat = lax.rem(lat_index, 2) == 1

    def faces(q, s, w, q_next, s_next, w_next):
        face = w * w_next
        speed = (0.25 * time_step) * face * (s + s_next)
        spread = (diffuse_h * time_step) * face
        return q * (speed + spread) + q_next * (speed - spread)

    def pick(odd, a, b):
        return jnp.where(odd, a, b)

    def column(value):
        return value, pltpu.roll(value, HALF, 1), value[:, WET_LANE : WET_LANE + 1]

    east_own = column(pick(odd_lon, ew_b[...], ew_a[...]))
    west_own = column(pick(odd_lon, ew_a[...], ew_b[...]))
    east_far = column(pick(odd_lon, ew_b_in[...], ew_a_in[...]))
    west_far = column(pick(odd_lon, ew_a_in[...], ew_b_in[...]))
    fix_e[...] = -(east_own[2] * faces(*east_own, *east_far))
    fix_w[...] = west_own[2] * faces(*west_far, *west_own)

    north[...] = pick(odd_lat, ns_a_in[...], ns_b_in[...])
    south[...] = pick(odd_lat, ns_b_in[...], ns_a_in[...])

    @pl.when(lat_index == lat_count - 1)
    def _fold():
        picks = fold_ref[...] - (lon_count - 1 - lon_index) * cols
        hot = (lax.broadcasted_iota(jnp.int32, (cols, cols), 0) == picks).astype(F32).astype(BF16)
        across = north[...]
        high, low = split(across)
        least = ((across - high.astype(F32)) - low.astype(F32)).astype(BF16)
        picked = dot_nn(high, hot) + (dot_nn(low, hot) + dot_nn(least, hot))
        at = lax.broadcasted_iota(jnp.int32, picked.shape, 0)
        is_speed = (at >= 2 * levels) & (at < 3 * levels)
        north[...] = jnp.where(is_speed, -picked, picked)

    def fields(value, t):
        return (
            value[t * levels : (t + 1) * levels],
            value[2 * levels : 3 * levels],
            value[3 * levels : 3 * levels + 1],
        )

    north_own = pick(odd_lat, ns_a[...], ns_b[...])
    south_own = pick(odd_lat, ns_b[...], ns_a[...])
    north_far, south_far = north[...], south[...]
    for t in range(2):
        at = pl.ds(t * levels, levels)
        own = fields(north_own, t)
        fix_n[at, :] = -(own[2] * faces(*own, *fields(north_far, t)))
        own = fields(south_own, t)
        fix_s[at, :] = own[2] * faces(*fields(south_far, t), *own)


def fixes(fold_partner, own, far, levels):
    rows, cols = own[0].shape[0], own[2].shape[1]
    return pl.pallas_call(
        fix_kernel,
        out_shape=(
            jax.ShapeDtypeStruct((rows, 128), F32),
            jax.ShapeDtypeStruct((rows, 128), F32),
            jax.ShapeDtypeStruct((2 * levels, cols), F32),
            jax.ShapeDtypeStruct((2 * levels, cols), F32),
        ),
        in_specs=[VMEM_SPEC] * 9,
        out_specs=(VMEM_SPEC,) * 4,
        scratch_shapes=[VM(own[2].shape, F32), VM(own[2].shape, F32)],
        compiler_params=pltpu.CompilerParams(vmem_limit_bytes=LIMIT),
        name="fix",
    )(fold_partner.reshape(1, cols), *own, *far)


def order_kernel(cell_ref, place_ref, start_ref, mark_ref, wide, *, cols):
    blocks = cell_ref.shape[0]
    buckets = 2 * GROUP
    cell = cell_ref[...]
    band = cell // (8 * cols)
    odd = lax.rem(lax.broadcasted_iota(jnp.int32, cell.shape, 1), 2)
    bucket = odd * GROUP + band
    hot = jnp.concatenate([(bucket == b).astype(F32) for b in range(buckets)], axis=0)
    hot16 = hot.astype(BF16)
    before = (
        lax.broadcasted_iota(jnp.int32, (128, 128), 0) < lax.broadcasted_iota(jnp.int32, (128, 128), 1)
    ).astype(F32).astype(BF16)
    within = dot_nn(hot16, before)
    totals = dot_nn(hot16, jnp.ones((128, 128), BF16))
    n = buckets * blocks
    earlier = (
        lax.broadcasted_iota(jnp.int32, (n, n), 1) < lax.broadcasted_iota(jnp.int32, (n, n), 0)
    ).astype(F32).astype(BF16)
    base = dot_nn(earlier, totals.astype(BF16))
    place = jnp.zeros(cell.shape, F32)
    start_ref[...] = jnp.full(start_ref.shape, blocks * 128, jnp.int32)
    for b in range(buckets):
        rows = slice(b * blocks, (b + 1) * blocks)
        place = place + hot[rows] * (base[rows] + within[rows])
        start_ref[b : b + 1, :] = base[b * blocks : b * blocks + 1].astype(jnp.int32)
    place_ref[...] = place.astype(jnp.int32)
    lane = lax.broadcasted_iota(jnp.int32, (128, 128), 1)
    row_f = (cell // cols).astype(F32)
    col_f = lax.rem(cell, cols).astype(F32)
    is_row = lax.rem(lane, HALF) == ROW_LANE
    is_col = lax.rem(lane, HALF) == COL_LANE
    for i in range(blocks):
        r = jnp.broadcast_to(row_f[i : i + 1], (128, 128)).T
        c = jnp.broadcast_to(col_f[i : i + 1], (128, 128)).T
        wide[i * 128 : (i + 1) * 128, :] = jnp.where(is_row, r, jnp.where(is_col, c, 0.0))
    half = blocks * 64
    low = lax.broadcasted_iota(jnp.int32, (half, 128), 1) < HALF
    mark_ref[...] = jnp.where(low, wide[pl.ds(0, half, stride=2), :], wide[pl.ds(1, half, stride=2), :])


def order(berg_cell, cols):
    blocks = berg_cell.shape[0] // 128
    return pl.pallas_call(
        functools.partial(order_kernel, cols=cols),
        out_shape=(
            jax.ShapeDtypeStruct((blocks, 128), jnp.int32),
            jax.ShapeDtypeStruct((3 * GROUP, 128), jnp.int32),
            jax.ShapeDtypeStruct((blocks * 64, 128), F32),
        ),
        in_specs=[VMEM_SPEC],
        out_specs=(VMEM_SPEC,) * 3,
        scratch_shapes=[VM((blocks * 128, 128), F32)],
        compiler_params=pltpu.CompilerParams(vmem_limit_bytes=LIMIT),
        name="order",
    )(berg_cell.reshape(blocks, 128))


def final_kernel(
    place_ref, start_ref, recv_ref, mark_ref, part_hbm, wet_ref, fix_e, fix_w, fix_n, fix_s,
    out_hbm,
    rows_v, sorted_v, pv, wetf, acc, lhs_h, lhs_l, hot_v, sem_i, sem_o,
):
    _, levels, rows, cols = pv.shape
    groups = rows // 8
    maps = 2 * levels
    n_rows = recv_ref.shape[0]

    def load(g):
        here = pl.ds(pl.multiple_of(8 * g, 8), 8)
        return pltpu.make_async_copy(part_hbm.at[:, :, here], pv.at[:, :, here], sem_i.at[g])

    def store(g):
        here = pl.ds(pl.multiple_of(8 * g, 8), 8)
        return pltpu.make_async_copy(pv.at[:, :, here], out_hbm.at[:, :, here], sem_o.at[g])

    for g in range(groups):
        load(g).start()
    rows_v[...] = recv_ref[...] + mark_ref[...]
    wetf[...] = wet_ref[...].astype(F32)

    unroll = 16

    def spread(i, _):
        for j in range(unroll):
            r = i * unroll + j
            line = rows_v[pl.ds(r, 1), :]
            sorted_v[pl.ds(place_ref[2 * r], 1), :] = line
            sorted_v[pl.ds(place_ref[2 * r + 1], 1), :] = line
        return _

    lax.fori_loop(0, n_rows // unroll, spread, 0)

    sub = lax.broadcasted_iota(jnp.int32, (8, 128), 0)
    subf = sub.astype(F32)
    lane = lax.broadcasted_iota(jnp.int32, (8, 128), 1)
    colf = lax.broadcasted_iota(jnp.int32, (128, cols), 1).astype(F32)
    last_chunk = n_rows // 128 - 1

    def group(g, _):
        here = pl.ds(pl.multiple_of(8 * g, 8), 8)
        first = []
        for h in range(2):
            s = start_ref[h * GROUP + g, 0]
            e = start_ref[h * GROUP + g + 1, 0]
            c = lax.div(s, 128)
            first.append((c, jnp.where(e > s, lax.div(e + 127, 128) - c, 0)))
        acc[...] = jnp.zeros_like(acc)

        def chunk(j, _):
            for h in range(2):
                c, n = first[h]
                at = jnp.minimum(c + j, h * (last_chunk + 1) + last_chunk)
                lines = sorted_v[pl.ds(pl.multiple_of(at * 128, 128), 128), :]
                flipped = lines.T
                off = h * HALF
                shift = (8 * g + jnp.where(j < n, 0, 4 * rows)).astype(F32)
                hit = subf == (flipped[off + ROW_LANE : off + ROW_LANE + 1, :] - shift)
                body = flipped[off : off + 56]
                high = body.astype(BF16).astype(F32)
                low = body - high
                for m in range(0, maps, 2):
                    for ref, src in ((lhs_h, high), (lhs_l, low)):
                        a = jnp.where(hit, src[m : m + 1, :], 0.0)
                        b = jnp.where(hit, src[m + 1 : m + 2, :], 0.0)
                        ref[8 * m : 8 * m + 16, h * 128 : (h + 1) * 128] = jnp.concatenate(
                            [a, b], axis=0
                        ).astype(BF16)
                hot = colf == lines[:, off + COL_LANE : off + COL_LANE + 1]
                hot_v[h * 128 : (h + 1) * 128, :] = hot.astype(F32).astype(BF16)
            acc[...] += dot_nn(lhs_h[...], hot_v[...]) + dot_nn(lhs_l[...], hot_v[...])
            return _

        lax.fori_loop(0, jnp.maximum(first[0][1], first[1][1]), chunk, 0)

        load(g).wait()
        w = wetf[here, :]
        e_fix = fix_e[here, :]
        w_fix = fix_w[here, :]
        at_n = (sub == 7) & (g == groups - 1)
        at_s = (sub == 0) & (g == 0)
        for m in range(maps):
            t, k = m // levels, m % levels
            at = t * TR_LANES + k
            for c in range(cols // 128):
                lanes = slice(c * 128, (c + 1) * 128)
                value = pv[t, k, here, lanes] + w[:, lanes] * acc[8 * m : 8 * m + 8, lanes]
                value += jnp.where(at_n, fix_n[m : m + 1, lanes], 0.0)
                value += jnp.where(at_s, fix_s[m : m + 1, lanes], 0.0)
                if c == 0:
                    value += jnp.where(lane == 0, w_fix[:, at : at + 1], 0.0)
                if c == cols // 128 - 1:
                    value += jnp.where(lane == 127, e_fix[:, at : at + 1], 0.0)
                pv[t, k, here, lanes] = value
        store(g).start()
        return _

    lax.fori_loop(0, groups, group, 0)
    for g in range(groups):
        store(g).wait()


def finish(place, start, recv, mark, part, wet, fix):
    count, levels, rows, cols = part.shape
    maps = count * levels
    dma = pltpu.SemaphoreType.DMA((rows // 8,))
    return pl.pallas_call(
        final_kernel,
        out_shape=jax.ShapeDtypeStruct(part.shape, F32),
        in_specs=[SMEM_SPEC, SMEM_SPEC, VMEM_SPEC, VMEM_SPEC, ANY_SPEC] + [VMEM_SPEC] * 5,
        out_specs=ANY_SPEC,
        scratch_shapes=[
            VM(recv.shape, F32),
            VM((2 * recv.shape[0], 128), F32),
            VM(part.shape, F32),
            VM((rows, cols), F32),
            VM((maps * 8, cols), F32),
            VM((maps * 8, 256), BF16),
            VM((maps * 8, 256), BF16),
            VM((256, cols), BF16),
            dma,
            dma,
        ],
        compiler_params=pltpu.CompilerParams(vmem_limit_bytes=LIMIT),
        name="final",
    )(place, start, recv, mark, part, wet, *fix)


def swap(value, axes, pairs):
    return lax.ppermute(value, axes, pairs + [(b, a) for a, b in pairs])


def shards(
    tracers, east_speed, north_speed, wet, fold_partner, bergs, berg_count, berg_cell, melt_map
):
    lon_count, lat_count = lax.axis_size("lon"), lax.axis_size("lat")
    levels, cols = tracers.shape[1], tracers.shape[3]

    melt = melt_rows(bergs, berg_count, melt_map)
    recv = lax.all_to_all(melt, ("lon", "lat"), split_axis=0, concat_axis=0, tiled=True)
    part, *own = stencil(tracers, east_speed, north_speed, wet)
    ew_a, ew_b, ns_a, ns_b = own

    lon_even = [(i, i + 1) for i in range(0, lon_count, 2)]
    lon_odd = [(i, (i + 1) % lon_count) for i in range(1, lon_count, 2)]

    def place(i, j):
        return i * lat_count + j

    lat_odd = [(place(i, j), place(i, j + 1)) for i in range(lon_count) for j in range(1, lat_count - 1, 2)]
    lat_odd += [
        (place(i, lat_count - 1), place(lon_count - 1 - i, lat_count - 1))
        for i in range(lon_count // 2)
    ]
    lat_even = [(j, j + 1) for j in range(0, lat_count, 2)]
    far = (
        swap(ew_a, "lon", lon_even),
        swap(ew_b, "lon", lon_odd),
        swap(ns_a, ("lon", "lat"), lat_odd),
        swap(ns_b, "lat", lat_even),
    )
    fix = fixes(fold_partner, own, far, levels)
    spots, start, mark = order(berg_cell, cols)
    recv = recv.reshape(-1, 128)
    return finish(spots.reshape(-1), start, recv, mark, part, wet, fix)


def solution(mesh):
    in_specs = (
        P(None, None, "lat", "lon"),
        P(None, "lat", "lon"),
        P(None, "lat", "lon"),
        P("lat", "lon"),
        P("lon"),
        P(("lon", "lat"), None),
        P(("lon", "lat")),
        P(("lon", "lat")),
        P(),
    )
    out_specs = P(None, None, "lat", "lon")
    return jax.shard_map(shards, mesh=mesh, in_specs=in_specs, out_specs=out_specs, check_vma=False)
```

time: 180 us -> 78.5 us (0.44)
  other arithmetic: 112 us -> 0 us
  Pallas kernels: 0 us -> 49.4 us
  local copies, waits for them, and re-layouts: 36.6 us -> 6.62 us
  starting transfers between devices: 27 us -> 20.4 us
  matrix products: 3.44 us -> 0 us
    pallas_call x0 -> x5, Pallas kernels: none -> 49.4 us  [the longest x1 22.9 us: stencil(): pl.pallas_call(stencil_kernel, out_shape=(jax.ShapeDtypeStruct(tracers.sh...]
    mul x6 -> x0, other arithmetic: 45.2 us -> none  [the longest x4 25.3 us: face_flux(): face * (0.5 * (speed + speed_next) * (0.5 * (value + value_next)) - diffu...]
    concatenate x3 -> x0, other arithmetic: 29.4 us -> none  [the longest x2 23.7 us: with_halo(): value = jnp.concatenate([before, value, after], axis=dim)]
    scatter-add x1 -> x0, other arithmetic: 27.6 us -> none  [shards(): jnp.zeros((melt.shape[0], rows_here * cols_here), jnp.float32)]
    slice x5 -> x0, local copies, waits for them, and re-layouts: 10.2 us -> none  [the longest x3 7.57 us: with_halo(): last = lax.slice_in_dim(value, length - width, length, axis=dim)]
    ppermute x8 -> x4, starting transfers between devices: 19.9 us -> 9.94 us  [swap(): return lax.ppermute(value, axes, pairs + [(b, a) for a, b in pairs])]
    scatter-add x1 -> x0, local copies, waits for them, and re-layouts: 9.72 us -> none  [shards(): jnp.zeros((melt.shape[0], rows_here * cols_here), jnp.float32)]
    sub x1 -> x0, other arithmetic: 7.09 us -> none  [vertical_mix(): step_diff = tracers[:, 1:] - tracers[:, :-1]]
  transfers between devices with their start and end apart: 9 -> 5, of which waited for: 0 -> 1; matrix products, arithmetic and copies ran while one was open for 45% -> 0% of each run, Pallas kernels for 0% -> 32%
where the time goes in v1:
time: 78.5 us; the launch traced here: 78 us
  Pallas kernels  49.4 us (63%)
  starting transfers between devices  20.4 us (26%)
  local copies, waits for them, and re-layouts  6.62 us (8%)
  waiting for transfers between devices  1.37 us (2%)
    pallas_call x1, Pallas kernels, stencil(): pl.pallas_call(stencil_kernel, out_shape=(jax.ShapeDtypeStruct(tracers.sh...  22.9 us
    pallas_call x1, Pallas kernels, finish(): pl.pallas_call(final_kernel, out_shape=jax.ShapeDtypeStruct(part.shape, F...  21.6 us
    all_to_all x1, starting transfers between devices, shards(): lax.all_to_all(melt, ('lon', 'lat'), split_axis=0, concat_axis=0, tiled=T...  10.5 us
    ppermute x4, starting transfers between devices, swap(): return lax.ppermute(value, axes, pairs + [(b, a) for a, b in pairs])  9.94 us
    unnamed x18, local copies, waits for them, and re-layouts  6.62 us
    pallas_call x1, Pallas kernels, melt_rows(): pl.pallas_call(melt_kernel, grid=(steps,), out_shape=jax.ShapeDtypeStruct...  3.1 us
  transfers between devices with their start and end apart: 5, of which 1 were waited for; matrix products, arithmetic and copies ran while one was open for 0% of the time, Pallas kernels for 32%

profile of v1, /device:TPU:4, one launch (start us, length us, event | category | flops | bytes accessed | tf_op | source)
XLA Modules:
  0.0 78.0 jit_solution(7138029025199996977)
XLA Ops:
  0.0 1.7 %copy-done.2 = f32[4096,128]{1,0:T(8,128)S(1)} copy-done((f32[4096,128]{1,0:T(8,128)S(1)}, f32[4096,128]{1,0:T(8,128)}, u32[]{:S(2)}) %copy-start.2) | copy-done | bytes 2097176
  1.7 0.7 copy-done.5
  2.5 0.7 copy-done.7
  3.1 3.1 %melt.1 = f32[128,16,128]{2,1,0:T(8,128)} custom-call(s32[128]{0:T(128)S(1)} %copy-done.7, f32[4096,128]{1,0:T(8,128)S(1)} %copy-done.2, f32[50,128]{1,0:T(8,128)S(1)} %bitcast.5), custom_call_target="tpu_custom_call" | custom-call | tf_op jit(solution)/shard_map/melt/pallas_call | solution.py:74
  6.3 10.5 %all-to-all-start = ((f32[128,16,128]{2,1,0:T(8,128)}), f32[128,16,128]{2,1,0:T(8,128)S(1)}, u32[]{:S(2)}, u32[]{:S(2)}) async-start(f32[128,16,128]{2,1,0:T(8,128)} %melt.1), calls=%async_computation | async-start | bytes 2097152 | tf_op jit(solution)/shard_map/all_to_all | solution.py:520
  16.8 0.0 copy-done
  16.8 0.0 copy-start.1
  16.8 1.7 %copy-done.1 = f32[25,64,384]{2,1,0:T(8,128)S(1)} copy-done((f32[25,64,384]{2,1,0:T(8,128)S(1)}, f32[25,64,384]{2,1,0:T(8,128)}, u32[]{:S(2)}) %copy-start.1) | copy-done | bytes 2457624
  18.5 0.9 %copy-done.3 = s32[64,384]{1,0:T(8,128)S(1)} copy-done((s32[64,384]{1,0:T(8,128)S(1)}, s32[64,384]{1,0:T(8,128)}, u32[]{:S(2)}) %copy-start.3) | copy-done | bytes 98328
  19.4 22.9 %stencil.1 = (f32[2,25,64,384]{3,2,1,0:T(8,128)}, f32[64,128]{1,0:T(8,128)S(1)}, f32[64,128]{1,0:T(8,128)S(1)}, f32[80,384]{1,0:T(8,128)S(1)}, f32[80,384]{1,0:T(8,128)S(1)}) custom-call(f32[2,25,64,384]{3,2,1,0:T(8,128)} %tr_hbm.1, f32[25,64,384]{2,1,0:T(8,128)S(1)} %copy-done, f32[25,64,384]{2,1,0:T(8,128)S(1)} %copy-done.1, s32[64,384]{1,0:T(8,128)S(1)} %copy-done.3), custom_call_target="tpu_custom_call" | custom-call | tf_op jit(solution)/shard_map/stencil/pallas_call | solution.py:210
  42.3 4.6 %collective-permute-start.2 = (f32[80,384]{1,0:T(8,128)S(1)}, f32[80,384]{1,0:T(8,128)S(1)}, u32[]{:S(2)}, u32[]{:S(2)}) collective-permute-start(f32[80,384]{1,0:T(8,128)S(1)} %get-tuple-element.23.ns_a), channel_id=1, source_target_pairs={{1,2},{3,4},{5,6},{9,10},{11,12},{13,14},{17,18},{19,20},{21,22},{... | collective-permute-start | bytes 368648 | tf_op jit(solution)/shard_map/ppermute | solution.py:510
  46.9 0.3 collective-permute-start.3
  47.2 0.0 collective-permute-start
  47.2 5.0 %collective-permute-start.1 = (f32[64,128]{1,0:T(8,128)S(1)}, f32[64,128]{1,0:T(8,128)S(1)}, u32[]{:S(2)}, u32[]{:S(2)}) collective-permute-start(f32[64,128]{1,0:T(8,128)S(1)} %get-tuple-element.22.ew_b), channel_id=1, source_target_pairs={{8,16},{24,32},{40,48},{56,64},{72,80},{88,96},{104,112},{120,0},{... | collective-permute-start | bytes 98312 | tf_op jit(solution)/shard_map/ppermute | solution.py:510
  52.2 1.6 %order.1 = (s32[32,128]{1,0:T(8,128)S(1)}, s32[24,128]{1,0:T(8,128)S(1)}, f32[2048,128]{1,0:T(8,128)S(1)}) custom-call(s32[32,128]{1,0:T(8,128)S(1)} %bitcast.7), custom_call_target="tpu_custom_call" | custom-call | tf_op jit(solution)/shard_map/order/pallas_call | solution.py:364
  53.8 0.0 collective-permute-done.ew_a_in
  53.8 1.4 %collective-permute-done.1.ew_b_in = f32[64,128]{1,0:T(8,128)S(1)} collective-permute-done((f32[64,128]{1,0:T(8,128)S(1)}, f32[64,128]{1,0:T(8,128)S(1)}, u32[]{:S(2)}, u32[]{:S(2)}) %collective-permute-start.1) | collective-permute-done | bytes 32800 | tf_op jit(solution)/shard_map/ppermute | solution.py:510
  55.2 0.0 collective-permute-done.2.ns_a_in
  55.2 0.0 collective-permute-done.3.ns_b_in
  55.2 0.3 fix.1
  55.4 0.0 all-to-all-done
  55.4 0.0 copy-start.4
  55.5 0.9 %copy-done.4 = s32[64,384]{1,0:T(8,128)S(1)} copy-done((s32[64,384]{1,0:T(8,128)S(1)}, s32[64,384]{1,0:T(8,128)}, u32[]{:S(2)}) %copy-start.4) | copy-done | bytes 98328
  56.3 21.6 %final.1 = f32[2,25,64,384]{3,2,1,0:T(8,128)} custom-call(s32[4096]{0:T(1024)S(1)} %bitcast.6, s32[24,128]{1,0:T(8,128)S(1)} %get-tuple-element.18.start_ref, f32[2048,128]{1,0:T(8,128)S(1)} %bitcast.4, f32[2048,128]{1,0:T(8,128)S(1)} %get-tuple-element.19.mark_ref, f32[2,25,64,384]{3,2,1,0:T(8,128)} %get-tuple-element.20.part_hbm, s32[64,384]{1,0:T(8,128)S(1)} %copy-done.4, ...), custom_call_target="tpu_custom_call" | custom-call | tf_op jit(solution)/shard_map/final/pallas_call | solution.py:487
  (10 shorter events, 0.0 us)
Async XLA Ops:
  0.0 16.8 %copy-start = (f32[25,64,384]{2,1,0:T(8,128)S(1)}, f32[25,64,384]{2,1,0:T(8,128)}, u32[]{:S(2)}) copy-start(f32[25,64,384]{2,1,0:T(8,128)} %ea_hbm.1) | copy-start | bytes 7372804
  0.0 1.7 %copy-start.2 = (f32[4096,128]{1,0:T(8,128)S(1)}, f32[4096,128]{1,0:T(8,128)}, u32[]{:S(2)}) copy-start(f32[4096,128]{1,0:T(8,128)} %berg_ref.1) | copy-start | bytes 6291460
  1.7 0.7 copy-start.5
  2.5 0.7 copy-start.7
  6.3 49.2 %all-to-all-start = ((f32[128,16,128]{2,1,0:T(8,128)}), f32[128,16,128]{2,1,0:T(8,128)S(1)}, u32[]{:S(2)}, u32[]{:S(2)}) async-start(f32[128,16,128]{2,1,0:T(8,128)} %melt.1), calls=%async_computation | async-start | bytes 2097152 | tf_op jit(solution)/shard_map/all_to_all | solution.py:520
  16.8 1.7 %copy-start.1 = (f32[25,64,384]{2,1,0:T(8,128)S(1)}, f32[25,64,384]{2,1,0:T(8,128)}, u32[]{:S(2)}) copy-start(f32[25,64,384]{2,1,0:T(8,128)} %no_hbm.1) | copy-start | bytes 7372804
  18.5 0.9 %copy-start.3 = (s32[64,384]{1,0:T(8,128)S(1)}, s32[64,384]{1,0:T(8,128)}, u32[]{:S(2)}) copy-start(s32[64,384]{1,0:T(8,128)} %wet_ref.3) | copy-start | bytes 294916
  19.4 32.8 %copy-start.8 = (s32[384]{0:T(512)S(1)}, s32[384]{0:T(512)}, u32[]{:S(2)}) copy-start(s32[384]{0:T(512)} %param.13) | copy-start | bytes 4612
  19.4 32.9 %copy-start.6 = (s32[4096]{0:T(1024)S(1)}, s32[4096]{0:T(1024)}, u32[]{:S(2)}) copy-start(s32[4096]{0:T(1024)} %param.16) | copy-start | bytes 49156
  42.3 12.9 %collective-permute-start.2 = (f32[80,384]{1,0:T(8,128)S(1)}, f32[80,384]{1,0:T(8,128)S(1)}, u32[]{:S(2)}, u32[]{:S(2)}) collective-permute-start(f32[80,384]{1,0:T(8,128)S(1)} %get-tuple-element.23.ns_a), channel_id=1, source_target_pairs={{1,2},{3,4},{5,6},{9,10},{11,12},{13,14},{17,18},{19,20},{21,22},{... | collective-permute-start | bytes 368648 | tf_op jit(solution)/shard_map/ppermute | solution.py:510
  46.9 8.2 %collective-permute-start.3 = (f32[80,384]{1,0:T(8,128)S(1)}, f32[80,384]{1,0:T(8,128)S(1)}, u32[]{:S(2)}, u32[]{:S(2)}) collective-permute-start(f32[80,384]{1,0:T(8,128)S(1)} %get-tuple-element.24.ns_b), channel_id=1, source_target_pairs={{0,1},{2,3},{4,5},{6,7},{1,0},{3,2},{5,4},{7,6},{8,9},{10,11},{12,... | collective-permute-start | bytes 368648 | tf_op jit(solution)/shard_map/ppermute | solution.py:510
  47.2 6.6 %collective-permute-start = (f32[64,128]{1,0:T(8,128)S(1)}, f32[64,128]{1,0:T(8,128)S(1)}, u32[]{:S(2)}, u32[]{:S(2)}) collective-permute-start(f32[64,128]{1,0:T(8,128)S(1)} %get-tuple-element.21.ew_a), channel_id=1, source_target_pairs={{0,8},{16,24},{32,40},{48,56},{64,72},{80,88},{96,104},{112,120},{... | collective-permute-start | bytes 98312 | tf_op jit(solution)/shard_map/ppermute | solution.py:510
  47.2 7.9 %collective-permute-start.1 = (f32[64,128]{1,0:T(8,128)S(1)}, f32[64,128]{1,0:T(8,128)S(1)}, u32[]{:S(2)}, u32[]{:S(2)}) collective-permute-start(f32[64,128]{1,0:T(8,128)S(1)} %get-tuple-element.22.ew_b), channel_id=1, source_target_pairs={{8,16},{24,32},{40,48},{56,64},{72,80},{88,96},{104,112},{120,0},{... | collective-permute-start | bytes 98312 | tf_op jit(solution)/shard_map/ppermute | solution.py:510
  55.4 0.9 %copy-start.4 = (s32[64,384]{1,0:T(8,128)S(1)}, s32[64,384]{1,0:T(8,128)}, u32[]{:S(2)}) copy-start(s32[64,384]{1,0:T(8,128)} %wet_ref.3) | copy-start | bytes 294916

commit v2 on v1

v2 whole, which is shorter than its diff:
```python
import functools

import jax
import jax.numpy as jnp
from jax import lax
from jax.experimental import pallas as pl
from jax.experimental.pallas import tpu as pltpu
from jax.sharding import PartitionSpec as P

diffuse_h = 0.1
diffuse_v = 0.1
time_step = 0.5

F32 = jnp.float32
BF16 = jnp.bfloat16
VM = pltpu.VMEM
VMEM_SPEC = pl.BlockSpec(memory_space=pltpu.VMEM)
SMEM_SPEC = pl.BlockSpec(memory_space=pltpu.SMEM)
ANY_SPEC = pl.BlockSpec(memory_space=pl.ANY)
LIMIT = 12 << 20

TR_LANES = 32
HALF = 64
WET_LANE = 127
WINDOW = 128
CELL_LANE = 50


def in_hbm(*values):
    return tuple(pltpu.with_memory_space_constraint(v, pltpu.HBM) for v in values)


def split(value):
    high = value.astype(BF16)
    low = (value - high.astype(F32)).astype(BF16)
    return high, low


def dot_nt(a, b):
    return lax.dot_general(a, b, (((1,), (1,)), ((), ())), preferred_element_type=F32)


def dot_nn(a, b):
    return lax.dot_general(a, b, (((1,), (0,)), ((), ())), preferred_element_type=F32)


def melt_kernel(count_ref, berg_ref, map_ref, out_ref, weight_ref):
    maps = map_ref.shape[0]
    width = berg_ref.shape[1]
    owners = out_ref.shape[0]
    pairs = out_ref.shape[1]
    rows = owners * pairs
    weight_ref[...] = jnp.zeros_like(weight_ref)
    weight_ref[0:maps, 0:width] = map_ref[...]
    weight_ref[HALF : HALF + maps, width : 2 * width] = map_ref[...]
    w_high, w_low = split(weight_ref[...])
    w_both = jnp.concatenate([w_high, w_low], axis=0)
    slots = berg_ref[...].reshape(owners, 2, pairs, width)
    both = jnp.concatenate([slots[:, h].reshape(rows, width) for h in range(2)], axis=1)
    b_high, b_low = split(both)
    wide = dot_nt(b_high, w_both)
    made = wide[:, :128] + (wide[:, 128:] + dot_nt(b_low, w_high))
    lane = lax.broadcasted_iota(jnp.int32, (pairs, 128), 1)
    slot = lax.broadcasted_iota(jnp.int32, (pairs, 128), 0) + jnp.where(lane >= HALF, pairs, 0)
    first = pl.program_id(0) * owners
    for o in range(owners):
        out_ref[o] = jnp.where(
            slot < count_ref[first + o], made[o * pairs : (o + 1) * pairs], 0.0
        )


def melt_rows(bergs, berg_count, melt_map):
    owners = berg_count.shape[0]
    slots = bergs.shape[0] // owners
    width = bergs.shape[1]
    steps = 4
    per = owners // steps
    return pl.pallas_call(
        melt_kernel,
        grid=(steps,),
        out_shape=jax.ShapeDtypeStruct((owners, slots // 2, 128), F32),
        in_specs=[
            SMEM_SPEC,
            pl.BlockSpec((per * slots, width), lambda i: (i, 0)),
            pl.BlockSpec(melt_map.shape[::-1], lambda i: (0, 0)),
        ],
        out_specs=pl.BlockSpec((per, slots // 2, 128), lambda i: (i, 0, 0)),
        scratch_shapes=[VM((128, 2 * width), F32)],
        compiler_params=pltpu.CompilerParams(vmem_limit_bytes=LIMIT),
        name="melt",
    )(*in_hbm(berg_count, bergs, melt_map.T))


def stencil_kernel(
    tr_hbm, ea_hbm, no_hbm, wet_ref,
    part_hbm, ew_a, ew_b, ns_a, ns_b,
    tv, ev, nv, ov, m_e, m_n, wetf, sem_t, sem_e, sem_n, sem_o,
):
    levels, rows, cols = ea_hbm.shape
    strips = rows // 8

    def copies(k):
        return (
            pltpu.make_async_copy(tr_hbm.at[:, k], tv.at[:, k], sem_t.at[k]),
            pltpu.make_async_copy(ea_hbm.at[k], ev.at[k], sem_e.at[k]),
            pltpu.make_async_copy(no_hbm.at[k], nv.at[k], sem_n.at[k]),
        )

    def result(k):
        return pltpu.make_async_copy(ov.at[:, k], part_hbm.at[:, k], sem_o.at[k])

    def start_level(k, _):
        for c in copies(k):
            c.start()
        return _

    lax.fori_loop(0, levels, start_level, 0)
    odd_lon = lax.rem(lax.axis_index("lon"), 2)
    odd_lat = lax.rem(lax.axis_index("lat"), 2)
    row_a = odd_lat * (rows - 1)
    row_b = (1 - odd_lat) * (rows - 1)

    wet = wet_ref[...].astype(F32)
    wetf[...] = wet
    col = lax.broadcasted_iota(jnp.int32, (rows, cols), 1)
    row = lax.broadcasted_iota(jnp.int32, (rows, cols), 0)
    m_e[...] = jnp.where(col == cols - 1, 0.0, wet * pltpu.roll(wet, cols - 1, 1))
    m_n[...] = jnp.where(row == rows - 1, 0.0, wet * pltpu.roll(wet, rows - 1, 0))
    lane_all = lax.broadcasted_iota(jnp.int32, (rows, 128), 1)
    ns_a[...] = jnp.zeros_like(ns_a)
    ns_b[...] = jnp.zeros_like(ns_b)
    ns_a[3 * levels : 3 * levels + 1, :] = wetf[pl.ds(row_a, 1), :]
    ns_b[3 * levels : 3 * levels + 1, :] = wetf[pl.ds(row_b, 1), :]

    lane = lax.broadcasted_iota(jnp.int32, (8, 128), 1)
    top = lax.broadcasted_iota(jnp.int32, (8, cols), 0) == 0
    marks = [lane == 0, lane == TR_LANES, lane == HALF]

    def next_row(ref, lead, s):
        if s < strips - 1:
            return ref[lead + (pl.ds(8 * s + 1, 8), slice(None))]
        return pltpu.roll(ref[lead + (pl.ds(8 * s, 8), slice(None))], 7, 0)

    for c in copies(0):
        c.wait()

    def level(k, packs):
        packs = list(packs)
        above = jnp.minimum(k + 1, levels - 1)
        below = jnp.maximum(k - 1, 0)

        @pl.when(k + 1 < levels)
        def _wait():
            for c in copies(k + 1):
                c.wait()

        carried = [None, None]
        for s in range(strips):
            here = pl.ds(8 * s, 8)
            u = ev[k, here, :]
            v = nv[k, here, :]
            me = m_e[here, :]
            mn = m_n[here, :]
            w = wetf[here, :]
            s_e = (0.25 * time_step * me) * (u + pltpu.roll(u, cols - 1, 1))
            s_n = (0.25 * time_step * mn) * (v + next_row(nv, (k,), s))
            d_e = (diffuse_h * time_step) * me
            d_n = (diffuse_h * time_step) * mn
            a_e, b_e, a_n, b_n = s_e + d_e, s_e - d_e, s_n + d_n, s_n - d_n
            edge = []
            for t in range(2):
                q = tv[t, k, here, :]
                edge.append(q)
                up = tv[t, above, here, :]
                dn = tv[t, below, here, :]
                fe = q * a_e + pltpu.roll(q, cols - 1, 1) * b_e
                fn = q * a_n + next_row(tv, (t, k), s) * b_n
                fw = pltpu.roll(fe, 1, 1)
                turned = pltpu.roll(fn, 1, 0)
                last = jnp.zeros_like(turned) if carried[t] is None else carried[t]
                fs = jnp.where(top, last, turned)
                carried[t] = turned
                mix = (diffuse_v * time_step) * ((up - q) - (q - dn))
                ov[t, k, here, :] = w * (q + ((mix - (fe - fw)) - (fn - fs)))
            edge.append(u)
            for side, lanes, shift in ((0, slice(0, 128), 0), (1, slice(cols - 128, cols), 1)):
                old = pltpu.roll(packs[2 * s + side], 1, 1)
                for at, (field, mark) in enumerate(zip(edge, marks)):
                    turn = at * TR_LANES + shift
                    moved = pltpu.roll(field[:, lanes], turn, 1) if turn else field[:, lanes]
                    old = jnp.where(mark, moved, old)
                packs[2 * s + side] = old
        for ref, at in ((ns_a, row_a), (ns_b, row_b)):
            ref[pl.ds(k, 1), :] = tv[0, k, pl.ds(at, 1), :]
            ref[pl.ds(levels + k, 1), :] = tv[1, k, pl.ds(at, 1), :]
            ref[pl.ds(2 * levels + k, 1), :] = nv[k, pl.ds(at, 1), :]
        result(k).start()
        return tuple(packs)

    packs = lax.fori_loop(0, levels, level, (jnp.zeros((8, 128), F32),) * (2 * strips))
    west = jnp.concatenate(packs[0::2], axis=0)
    east = jnp.concatenate(packs[1::2], axis=0)

    def again(value, mask):
        speed = (lane_all >= HALF + TR_LANES) & (lane_all < HALF + TR_LANES + levels)
        value = jnp.where(speed, pltpu.roll(value, TR_LANES, 1), value)
        return jnp.where(lane_all == WET_LANE, mask, value)

    is_odd = odd_lon == 1
    west_all, east_all = again(west, wetf[:, 0:1]), again(east, wetf[:, cols - 1 : cols])
    ew_a[...] = jnp.where(is_odd, west_all, east_all)
    ew_b[...] = jnp.where(is_odd, east_all, west_all)

    def done(k, _):
        result(k).wait()
        return _

    lax.fori_loop(0, levels, done, 0)


def stencil(tracers, east_speed, north_speed, wet):
    count, levels, rows, cols = tracers.shape
    edge_rows = -(-(3 * levels + 1) // 8) * 8
    dma = pltpu.SemaphoreType.DMA((levels,))
    return pl.pallas_call(
        stencil_kernel,
        out_shape=(
            pltpu.HBM(tracers.shape, F32),
            jax.ShapeDtypeStruct((rows, 128), F32),
            jax.ShapeDtypeStruct((rows, 128), F32),
            jax.ShapeDtypeStruct((edge_rows, cols), F32),
            jax.ShapeDtypeStruct((edge_rows, cols), F32),
        ),
        in_specs=[ANY_SPEC] * 3 + [VMEM_SPEC],
        out_specs=(ANY_SPEC,) + (VMEM_SPEC,) * 4,
        scratch_shapes=[
            VM(tracers.shape, F32),
            VM(east_speed.shape, F32),
            VM(north_speed.shape, F32),
            VM(tracers.shape, F32),
            VM((rows, cols), F32),
            VM((rows, cols), F32),
            VM((rows, cols), F32),
            dma,
            dma,
            dma,
            dma,
        ],
        compiler_params=pltpu.CompilerParams(vmem_limit_bytes=20 << 20),
        name="stencil",
    )(*in_hbm(tracers, east_speed, north_speed, wet))


def fix_kernel(
    fold_ref, ew_a, ew_b, ns_a, ns_b, ew_a_in, ew_b_in, ns_a_in, ns_b_in,
    fix_e, fix_w, fix_n, fix_s, north, south,
):
    levels = fix_n.shape[0] // 2
    cols = ns_a.shape[1]
    lon_count, lat_count = lax.axis_size("lon"), lax.axis_size("lat")
    lon_index, lat_index = lax.axis_index("lon"), lax.axis_index("lat")
    odd_lon = lax.rem(lon_index, 2) == 1
    odd_lat = lax.rem(lat_index, 2) == 1

    def faces(q, s, w, q_next, s_next, w_next):
        face = w * w_next
        speed = (0.25 * time_step) * face * (s + s_next)
        spread = (diffuse_h * time_step) * face
        return q * (speed + spread) + q_next * (speed - spread)

    def pick(odd, a, b):
        return jnp.where(odd, a, b)

    def column(value):
        return value, pltpu.roll(value, HALF, 1), value[:, WET_LANE : WET_LANE + 1]

    east_own = column(pick(odd_lon, ew_b[...], ew_a[...]))
    west_own = column(pick(odd_lon, ew_a[...], ew_b[...]))
    east_far = column(pick(odd_lon, ew_b_in[...], ew_a_in[...]))
    west_far = column(pick(odd_lon, ew_a_in[...], ew_b_in[...]))
    fix_e[...] = -(east_own[2] * faces(*east_own, *east_far))
    fix_w[...] = west_own[2] * faces(*west_far, *west_own)

    north[...] = pick(odd_lat, ns_a_in[...], ns_b_in[...])
    south[...] = pick(odd_lat, ns_b_in[...], ns_a_in[...])

    @pl.when(lat_index == lat_count - 1)
    def _fold():
        picks = fold_ref[...] - (lon_count - 1 - lon_index) * cols
        hot = (lax.broadcasted_iota(jnp.int32, (cols, cols), 0) == picks).astype(F32).astype(BF16)
        across = north[...]
        high, low = split(across)
        least = ((across - high.astype(F32)) - low.astype(F32)).astype(BF16)
        picked = dot_nn(high, hot) + (dot_nn(low, hot) + dot_nn(least, hot))
        at = lax.broadcasted_iota(jnp.int32, picked.shape, 0)
        is_speed = (at >= 2 * levels) & (at < 3 * levels)
        north[...] = jnp.where(is_speed, -picked, picked)

    def fields(value, t):
        return (
            value[t * levels : (t + 1) * levels],
            value[2 * levels : 3 * levels],
            value[3 * levels : 3 * levels + 1],
        )

    north_own = pick(odd_lat, ns_a[...], ns_b[...])
    south_own = pick(odd_lat, ns_b[...], ns_a[...])
    north_far, south_far = north[...], south[...]
    for t in range(2):
        at = pl.ds(t * levels, levels)
        own = fields(north_own, t)
        fix_n[at, :] = -(own[2] * faces(*own, *fields(north_far, t)))
        own = fields(south_own, t)
        fix_s[at, :] = own[2] * faces(*fields(south_far, t), *own)


def fixes(fold_partner, own, far, levels):
    rows, cols = own[0].shape[0], own[2].shape[1]
    return pl.pallas_call(
        fix_kernel,
        out_shape=(
            jax.ShapeDtypeStruct((rows, 128), F32),
            jax.ShapeDtypeStruct((rows, 128), F32),
            jax.ShapeDtypeStruct((2 * levels, cols), F32),
            jax.ShapeDtypeStruct((2 * levels, cols), F32),
        ),
        in_specs=[VMEM_SPEC] * 9,
        out_specs=(VMEM_SPEC,) * 4,
        scratch_shapes=[VM(own[2].shape, F32), VM(own[2].shape, F32)],
        compiler_params=pltpu.CompilerParams(vmem_limit_bytes=LIMIT),
        name="fix",
    )(*in_hbm(fold_partner.reshape(1, cols)), *own, *far)


def order_kernel(cell_ref, place_ref, start_ref, mark_ref, base_ref, *, rows, cols, pairs):
    blocks = cell_ref.shape[0]
    count = blocks * 128
    half = count // 2
    cell = cell_ref[...].astype(F32)
    row = jnp.floor((cell + 0.5) * (1.0 / cols))
    hot = [jnp.where(row == float(r), 1.0, 0.0) for r in range(rows)]
    hot16 = jnp.concatenate([h.astype(BF16) for h in hot], axis=0)
    down = lax.broadcasted_iota(jnp.int32, (128, 128), 0)
    along = lax.broadcasted_iota(jnp.int32, (128, 128), 1)
    before = jnp.where(down < along, 1.0, 0.0).astype(BF16)
    after = jnp.where(along < down, 1.0, 0.0).astype(BF16)
    ones = jnp.ones((128, 128), BF16)
    within = dot_nn(hot16, before)
    totals = dot_nn(hot16, ones)
    carry = jnp.zeros((1, 128), F32)
    place = jnp.zeros(cell.shape, F32)
    per = 128 // blocks
    for c in range(rows // per):
        part = totals[c * 128 : (c + 1) * 128]
        base = dot_nn(after, part.astype(BF16)) + carry
        carry = base[127:128] + part[127:128]
        base_ref[c * 128 : (c + 1) * 128, :] = base
        spot = base + within[c * 128 : (c + 1) * 128]
        for j in range(per):
            place = place + hot[c * per + j] * spot[j * blocks : (j + 1) * blocks]
    place_ref[...] = place.astype(jnp.int32)
    starts = base_ref[pl.ds(0, rows, stride=blocks), :]
    high = jnp.floor(starts * (1.0 / 128))
    low = starts - 128 * high
    first = jnp.where(along[:8] == 0, 1.0, 0.0).astype(BF16)
    starts = 128 * dot_nt(first, high.astype(BF16)) + dot_nt(first, low.astype(BF16))
    start_ref[...] = jnp.full(start_ref.shape, count, jnp.int32)
    start_ref[:, 0:rows] = starts.astype(jnp.int32)
    for i in range(blocks):
        turned = jnp.broadcast_to(cell[i : i + 1], (128, 128)).T
        for j in range(128 // pairs):
            at = (j % 2) * half + (i * (128 // pairs) + j) // 2 * pairs
            mark_ref[at : at + pairs, :] = turned[j * pairs : (j + 1) * pairs]


def order(berg_cell, rows, cols, pairs):
    count = berg_cell.shape[0]
    blocks = count // 128
    return pl.pallas_call(
        functools.partial(order_kernel, rows=rows, cols=cols, pairs=pairs),
        out_shape=(
            jax.ShapeDtypeStruct((blocks, 128), jnp.int32),
            jax.ShapeDtypeStruct((8, 128), jnp.int32),
            jax.ShapeDtypeStruct((count, 128), F32),
        ),
        in_specs=[VMEM_SPEC],
        out_specs=(VMEM_SPEC,) * 3,
        scratch_shapes=[VM((blocks * rows, 128), F32)],
        compiler_params=pltpu.CompilerParams(vmem_limit_bytes=LIMIT),
        name="order",
    )(*in_hbm(berg_cell.reshape(blocks, 128)))


def final_kernel(
    place_ref, start_ref, recv_ref, mark_ref, part_hbm, wet_ref, fix_e, fix_w, fix_n, fix_s,
    out_hbm,
    rows_v, sorted_v, pv, wetf, acc, sem_i, sem_o, *, pairs,
):
    _, levels, rows, cols = pv.shape
    groups = rows // 8
    tiles = cols // 128
    maps = 2 * levels
    n_rows = recv_ref.shape[0]
    count = 2 * n_rows

    def load(g):
        here = pl.ds(pl.multiple_of(8 * g, 8), 8)
        return pltpu.make_async_copy(part_hbm.at[:, :, here], pv.at[:, :, here], sem_i.at[g])

    def store(g):
        here = pl.ds(pl.multiple_of(8 * g, 8), 8)
        return pltpu.make_async_copy(pv.at[:, :, here], out_hbm.at[:, :, here], sem_o.at[g])

    for g in range(groups):
        load(g).start()
    lane_all = lax.broadcasted_iota(jnp.int32, (128, 128), 1)
    low_half = lane_all < HALF
    cell_lane = lane_all == CELL_LANE

    def halves(i, _):
        at = pl.multiple_of(i * 128, 128)
        both = recv_ref[pl.ds(at, 128), :]
        high = both.astype(BF16).astype(F32)
        low = both - high
        for h, body in enumerate(
            (
                jnp.where(low_half, high, pltpu.roll(low, HALF, 1)),
                jnp.where(low_half, pltpu.roll(high, HALF, 1), low),
            )
        ):
            there = pl.ds(pl.multiple_of(h * n_rows + at, 128), 128)
            rows_v[there, :] = jnp.where(cell_lane, mark_ref[there, :], body)
        return _

    lax.fori_loop(0, n_rows // 128, halves, 0)
    wetf[...] = wet_ref[...].astype(F32)
    sorted_v[count:, :] = jnp.full((WINDOW, 128), -1.0, F32)

    def spread(i, _):
        first = pl.multiple_of(i * pairs, pairs)
        for j in range(pairs):
            for h in range(2):
                to = place_ref[2 * first + h * pairs + j]
                sorted_v[pl.ds(to, 1), :] = rows_v[pl.ds(h * n_rows + first + j, 1), :]
        return _

    lax.fori_loop(0, n_rows // pairs, spread, 0)

    lane = lax.broadcasted_iota(jnp.int32, (8, 128), 1)
    lanef = lax.broadcasted_iota(jnp.int32, (WINDOW, 128), 1).astype(F32)

    def row_sources(r, at):
        at = pl.multiple_of(at, 8)
        lines = sorted_v[pl.ds(at, WINDOW), :]
        lhs = lines.T.astype(BF16)
        near = lines[:, CELL_LANE : CELL_LANE + 1] - (r * cols).astype(F32)
        hot = [jnp.where(near - float(128 * c) == lanef, 1.0, 0.0).astype(BF16) for c in range(tiles)]
        both = dot_nn(lhs, jnp.concatenate(hot, axis=1))
        return both[:HALF] + both[HALF:]

    def group(g, _):
        here = pl.ds(pl.multiple_of(8 * g, 8), 8)
        firsts, windows = [], []
        for j in range(8):
            s = start_ref[0, 8 * g + j]
            e = start_ref[0, 8 * g + j + 1]
            first = lax.div(s, 8) * 8
            firsts.append(first)
            windows.append(lax.div(e - first + (WINDOW - 1), WINDOW))
        for j in range(8):
            made = row_sources(8 * g + j, firsts[j])
            for c in range(tiles):
                acc[c, j * HALF : (j + 1) * HALF, :] = made[:, c * 128 : (c + 1) * 128]
        most = functools.reduce(jnp.maximum, windows)

        @pl.when(most > 1)
        def _more():
            for j in range(8):

                def again(i, _, j=j):
                    made = row_sources(8 * g + j, firsts[j] + i * WINDOW)
                    for c in range(tiles):
                        acc[c, j * HALF : (j + 1) * HALF, :] += made[:, c * 128 : (c + 1) * 128]
                    return _

                lax.fori_loop(1, windows[j], again, 0)

        load(g).wait()
        w = wetf[here, :]
        e_fix = fix_e[here, :]
        w_fix = fix_w[here, :]

        for edge, ref, at in ((groups - 1, fix_n, rows - 1), (0, fix_s, 0)):

            @pl.when(g == edge)
            def _edge_row(ref=ref, at=at):
                for m in range(maps):
                    t, k = m // levels, m % levels
                    pv[t, k, at : at + 1, :] += ref[m : m + 1, :]

        for m in range(maps):
            t, k = m // levels, m % levels
            at = t * TR_LANES + levels - 1 - k
            for c in range(tiles):
                lanes = slice(c * 128, (c + 1) * 128)
                value = pv[t, k, here, lanes] + w[:, lanes] * acc[c, pl.ds(m, 8, stride=HALF), :]
                if c == 0:
                    value += jnp.where(lane == 0, pltpu.roll(w_fix, (128 - at) % 128, 1), 0.0)
                if c == tiles - 1:
                    value += jnp.where(lane == 127, pltpu.roll(e_fix, 127 - at, 1), 0.0)
                pv[t, k, here, lanes] = value
        store(g).start()
        return _

    lax.fori_loop(0, groups, group, 0)
    for g in range(groups):
        store(g).wait()


def finish(place, start, recv, mark, part, wet, fix, pairs):
    _, levels, rows, cols = part.shape
    dma = pltpu.SemaphoreType.DMA((rows // 8,))
    return pl.pallas_call(
        functools.partial(final_kernel, pairs=pairs),
        out_shape=jax.ShapeDtypeStruct(part.shape, F32),
        in_specs=[SMEM_SPEC] * 2 + [VMEM_SPEC] * 2 + [ANY_SPEC] + [VMEM_SPEC] * 5,
        out_specs=ANY_SPEC,
        scratch_shapes=[
            VM((2 * recv.shape[0], 128), F32),
            VM((2 * recv.shape[0] + WINDOW, 128), F32),
            VM(part.shape, F32),
            VM((rows, cols), F32),
            VM((cols // 128, 8 * HALF, 128), F32),
            dma,
            dma,
        ],
        compiler_params=pltpu.CompilerParams(vmem_limit_bytes=24 << 20),
        name="final",
    )(place, start, recv, mark, *in_hbm(part, wet), *fix)


def swap(value, axes, pairs):
    return lax.ppermute(value, axes, pairs + [(b, a) for a, b in pairs])


def shards(
    tracers, east_speed, north_speed, wet, fold_partner, bergs, berg_count, berg_cell, melt_map
):
    lon_count, lat_count = lax.axis_size("lon"), lax.axis_size("lat")
    levels, cols = tracers.shape[1], tracers.shape[3]

    melt = melt_rows(bergs, berg_count, melt_map)
    recv = lax.all_to_all(melt, ("lon", "lat"), split_axis=0, concat_axis=0, tiled=True)
    part, *own = stencil(tracers, east_speed, north_speed, wet)
    ew_a, ew_b, ns_a, ns_b = own

    lon_even = [(i, i + 1) for i in range(0, lon_count, 2)]
    lon_odd = [(i, (i + 1) % lon_count) for i in range(1, lon_count, 2)]

    def place(i, j):
        return i * lat_count + j

    lat_odd = [(place(i, j), place(i, j + 1)) for i in range(lon_count) for j in range(1, lat_count - 1, 2)]
    lat_odd += [
        (place(i, lat_count - 1), place(lon_count - 1 - i, lat_count - 1))
        for i in range(lon_count // 2)
    ]
    lat_even = [(j, j + 1) for j in range(0, lat_count, 2)]
    far = (
        swap(ew_a, "lon", lon_even),
        swap(ew_b, "lon", lon_odd),
        swap(ns_a, ("lon", "lat"), lat_odd),
        swap(ns_b, "lat", lat_even),
    )
    fix = fixes(fold_partner, own, far, levels)
    pairs = melt.shape[1]
    spots, start, mark = order(berg_cell, tracers.shape[2], cols, pairs)
    recv = recv.reshape(-1, 128)
    return finish(spots.reshape(-1), start, recv, mark, part, wet, fix, pairs)


def solution(mesh):
    in_specs = (
        P(None, None, "lat", "lon"),
        P(None, "lat", "lon"),
        P(None, "lat", "lon"),
        P("lat", "lon"),
        P("lon"),
        P(("lon", "lat"), None),
        P(("lon", "lat")),
        P(("lon", "lat")),
        P(),
    )
    out_specs = P(None, None, "lat", "lon")
    return jax.shard_map(shards, mesh=mesh, in_specs=in_specs, out_specs=out_specs, check_vma=False)
```

time: 78.5 us -> 62.1 us (0.79)
  Pallas kernels: 49.4 us -> 39.9 us
  local copies, waits for them, and re-layouts: 6.62 us -> 0.57 us
    pallas_call x3, Pallas kernels: 46.1 us -> 34.7 us  [the longest x1 17.1 us: finish(): pl.pallas_call(functools.partial(final_kernel, pairs=pairs), out_shape=ja...]
    unnamed x18 -> x2, local copies, waits for them, and re-layouts: 6.62 us -> 0.01 us
    pallas_call x1, Pallas kernels: 3.1 us -> 4.23 us  [melt_rows(): pl.pallas_call(melt_kernel, grid=(steps,), out_shape=jax.ShapeDtypeStruct...]
  transfers between devices with their start and end apart: 5 -> 5, of which waited for: 1 -> 1; matrix products, arithmetic and copies ran while one was open for 0% -> 1% of each run, Pallas kernels for 32% -> 30%
where the time goes in v2:
time: 62.1 us; the launch traced here: 61.7 us
  Pallas kernels  39.9 us (64%)
  starting transfers between devices  20.4 us (33%)
  waiting for transfers between devices  0.8 us (1%)
    pallas_call x1, Pallas kernels, finish(): pl.pallas_call(functools.partial(final_kernel, pairs=pairs), out_shape=ja...  17.1 us
    pallas_call x1, Pallas kernels, stencil(): pl.pallas_call(stencil_kernel, out_shape=(pltpu.HBM(tracers.shape, F32),...  16.1 us
    all_to_all x1, starting transfers between devices, shards(): lax.all_to_all(melt, ('lon', 'lat'), split_axis=0, concat_axis=0, tiled=T...  10.5 us
    ppermute x4, starting transfers between devices, swap(): return lax.ppermute(value, axes, pairs + [(b, a) for a, b in pairs])  9.94 us
    pallas_call x1, Pallas kernels, melt_rows(): pl.pallas_call(melt_kernel, grid=(steps,), out_shape=jax.ShapeDtypeStruct...  4.23 us
    pallas_call x1, Pallas kernels, order(): pl.pallas_call(functools.partial(order_kernel, rows=rows, cols=cols, pair...  1.58 us
  transfers between devices with their start and end apart: 5, of which 1 were waited for; matrix products, arithmetic and copies ran while one was open for 1% of the time, Pallas kernels for 30%

profile of v2, /device:TPU:4, one launch (start us, length us, event | category | flops | bytes accessed | tf_op | source)
XLA Modules:
  0.0 61.7 jit_solution(4446637077347644603)
XLA Ops:
  0.0 4.2 %melt.1 = f32[128,16,128]{2,1,0:T(8,128)} custom-call(s32[128]{0:T(128)} %count_ref.1, f32[4096,128]{1,0:T(8,128)} %berg_ref.1, f32[50,128]{1,0:T(8,128)} %bitcast.6), custom_call_target="tpu_custom_call" | custom-call | tf_op jit(solution)/shard_map/melt/pallas_call | solution.py:78
  4.2 10.5 %all-to-all-start = ((f32[128,16,128]{2,1,0:T(8,128)}), f32[128,16,128]{2,1,0:T(8,128)S(1)}, u32[]{:S(2)}, u32[]{:S(2)}) async-start(f32[128,16,128]{2,1,0:T(8,128)} %melt.1), calls=%async_computation | async-start | bytes 2097152 | tf_op jit(solution)/shard_map/all_to_all | solution.py:553
  14.7 0.0 copy-start
  14.7 16.1 %stencil.1 = (f32[2,25,64,384]{3,2,1,0:T(8,128)}, f32[64,128]{1,0:T(8,128)S(1)}, f32[64,128]{1,0:T(8,128)S(1)}, f32[80,384]{1,0:T(8,128)S(1)}, f32[80,384]{1,0:T(8,128)S(1)}) custom-call(f32[2,25,64,384]{3,2,1,0:T(8,128)} %tr_hbm.1, f32[25,64,384]{2,1,0:T(8,128)} %ea_hbm.1, f32[25,64,384]{2,1,0:T(8,128)} %no_hbm.1, s32[64,384]{1,0:T(8,128)} %wet_ref.3), custom_call_target="tpu_custom_call" | custom-call | tf_op jit(solution)/shard_map/stencil/pallas_call | solution.py:225
  30.8 4.6 %collective-permute-start.2 = (f32[80,384]{1,0:T(8,128)S(1)}, f32[80,384]{1,0:T(8,128)S(1)}, u32[]{:S(2)}, u32[]{:S(2)}) collective-permute-start(f32[80,384]{1,0:T(8,128)S(1)} %get-tuple-element.23.ns_a), channel_id=1, source_target_pairs={{1,2},{3,4},{5,6},{9,10},{11,12},{13,14},{17,18},{19,20},{21,22},{... | collective-permute-start | bytes 368648 | tf_op jit(solution)/shard_map/ppermute | solution.py:543
  35.5 0.3 collective-permute-start.3
  35.7 0.0 collective-permute-start
  35.8 5.0 %collective-permute-start.1 = (f32[64,128]{1,0:T(8,128)S(1)}, f32[64,128]{1,0:T(8,128)S(1)}, u32[]{:S(2)}, u32[]{:S(2)}) collective-permute-start(f32[64,128]{1,0:T(8,128)S(1)} %get-tuple-element.22.ew_b), channel_id=1, source_target_pairs={{8,16},{24,32},{40,48},{56,64},{72,80},{88,96},{104,112},{120,0},{... | collective-permute-start | bytes 98312 | tf_op jit(solution)/shard_map/ppermute | solution.py:543
  40.8 0.0 copy-done
  40.8 0.6 reshape.15.fold_ref
  41.3 1.6 %order.1 = (s32[32,128]{1,0:T(8,128)S(1)}, s32[8,128]{1,0:T(8,128)S(1)}, f32[4096,128]{1,0:T(8,128)S(1)}) custom-call(s32[32,128]{1,0:T(8,128)} %bitcast.7), custom_call_target="tpu_custom_call" | custom-call | tf_op jit(solution)/shard_map/order/pallas_call | solution.py:379
  42.9 0.0 collective-permute-done.ew_a_in
  42.9 0.8 %collective-permute-done.1.ew_b_in = f32[64,128]{1,0:T(8,128)S(1)} collective-permute-done((f32[64,128]{1,0:T(8,128)S(1)}, f32[64,128]{1,0:T(8,128)S(1)}, u32[]{:S(2)}, u32[]{:S(2)}) %collective-permute-start.1) | collective-permute-done | bytes 32800 | tf_op jit(solution)/shard_map/ppermute | solution.py:543
  43.7 0.0 collective-permute-done.2.ns_a_in
  43.7 0.0 collective-permute-done.3.ns_b_in
  43.7 0.9 %fix.1 = (f32[64,128]{1,0:T(8,128)S(1)}, f32[64,128]{1,0:T(8,128)S(1)}, f32[50,384]{1,0:T(8,128)S(1)}, f32[50,384]{1,0:T(8,128)S(1)}) custom-call(s32[1,384]{1,0:T(1,128)} %reshape.15.fold_ref, f32[64,128]{1,0:T(8,128)S(1)} %get-tuple-element.21.ew_a, f32[64,128]{1,0:T(8,128)S(1)} %get-tuple-element.22.ew_b, f32[80,384]{1,0:T(8,128)S(1)} %get-tuple-element.23.ns_a, ...), custom_call_target="tpu_custom_call" | custom-call | tf_op jit(solution)/shard_map/fix/pallas_call | solution.py:319
  44.6 0.0 all-to-all-done
  44.6 17.1 %final.1 = f32[2,25,64,384]{3,2,1,0:T(8,128)} custom-call(s32[4096]{0:T(1024)S(1)} %bitcast.5, s32[8,128]{1,0:T(8,128)S(1)} %get-tuple-element.18.start_ref, f32[2048,128]{1,0:T(8,128)S(1)} %bitcast.4, f32[4096,128]{1,0:T(8,128)S(1)} %get-tuple-element.19.mark_ref, f32[2,25,64,384]{3,2,1,0:T(8,128)} %get-tuple-element.20.part_hbm, s32[64,384]{1,0:T(8,128)} %wet_ref.3, ...), custom_call_target="tpu_custom_call" | custom-call | tf_op jit(solution)/shard_map/final/pallas_call | solution.py:523
Async XLA Ops:
  4.2 40.4 %all-to-all-start = ((f32[128,16,128]{2,1,0:T(8,128)}), f32[128,16,128]{2,1,0:T(8,128)S(1)}, u32[]{:S(2)}, u32[]{:S(2)}) async-start(f32[128,16,128]{2,1,0:T(8,128)} %melt.1), calls=%async_computation | async-start | bytes 2097152 | tf_op jit(solution)/shard_map/all_to_all | solution.py:553
  14.7 26.0 %copy-start = (s32[384]{0:T(512)S(1)}, s32[384]{0:T(512)}, u32[]{:S(2)}) copy-start(s32[384]{0:T(512)} %param.13) | copy-start | bytes 4612
  30.8 12.9 %collective-permute-start.2 = (f32[80,384]{1,0:T(8,128)S(1)}, f32[80,384]{1,0:T(8,128)S(1)}, u32[]{:S(2)}, u32[]{:S(2)}) collective-permute-start(f32[80,384]{1,0:T(8,128)S(1)} %get-tuple-element.23.ns_a), channel_id=1, source_target_pairs={{1,2},{3,4},{5,6},{9,10},{11,12},{13,14},{17,18},{19,20},{21,22},{... | collective-permute-start | bytes 368648 | tf_op jit(solution)/shard_map/ppermute | solution.py:543
  35.5 8.2 %collective-permute-start.3 = (f32[80,384]{1,0:T(8,128)S(1)}, f32[80,384]{1,0:T(8,128)S(1)}, u32[]{:S(2)}, u32[]{:S(2)}) collective-permute-start(f32[80,384]{1,0:T(8,128)S(1)} %get-tuple-element.24.ns_b), channel_id=1, source_target_pairs={{0,1},{2,3},{4,5},{6,7},{1,0},{3,2},{5,4},{7,6},{8,9},{10,11},{12,... | collective-permute-start | bytes 368648 | tf_op jit(solution)/shard_map/ppermute | solution.py:543
  35.7 7.2 %collective-permute-start = (f32[64,128]{1,0:T(8,128)S(1)}, f32[64,128]{1,0:T(8,128)S(1)}, u32[]{:S(2)}, u32[]{:S(2)}) collective-permute-start(f32[64,128]{1,0:T(8,128)S(1)} %get-tuple-element.21.ew_a), channel_id=1, source_target_pairs={{0,8},{16,24},{32,40},{48,56},{64,72},{80,88},{96,104},{112,120},{... | collective-permute-start | bytes 98312 | tf_op jit(solution)/shard_map/ppermute | solution.py:543
  35.8 7.9 %collective-permute-start.1 = (f32[64,128]{1,0:T(8,128)S(1)}, f32[64,128]{1,0:T(8,128)S(1)}, u32[]{:S(2)}, u32[]{:S(2)}) collective-permute-start(f32[64,128]{1,0:T(8,128)S(1)} %get-tuple-element.22.ew_b), channel_id=1, source_target_pairs={{8,16},{24,32},{40,48},{56,64},{72,80},{88,96},{104,112},{120,0},{... | collective-permute-start | bytes 98312 | tf_op jit(solution)/shard_map/ppermute | solution.py:543

commit v3 on v2

--- a/solution.py
+++ b/solution.py
@@ -22,6 +22,7 @@
 TR_LANES = 32
 HALF = 64
 WET_LANE = 127
+AHEAD = 5
 WINDOW = 128
 CELL_LANE = 50
 
@@ -44,17 +45,22 @@
     return lax.dot_general(a, b, (((1,), (0,)), ((), ())), preferred_element_type=F32)
 
 
-def melt_kernel(count_ref, berg_ref, map_ref, out_ref, weight_ref):
+def melt_kernel(count_ref, berg_ref, map_ref, out_ref, weight_ref, both_ref):
     maps = map_ref.shape[0]
     width = berg_ref.shape[1]
     owners = out_ref.shape[0]
     pairs = out_ref.shape[1]
     rows = owners * pairs
-    weight_ref[...] = jnp.zeros_like(weight_ref)
-    weight_ref[0:maps, 0:width] = map_ref[...]
-    weight_ref[HALF : HALF + maps, width : 2 * width] = map_ref[...]
-    w_high, w_low = split(weight_ref[...])
-    w_both = jnp.concatenate([w_high, w_low], axis=0)
+
+    @pl.when(pl.program_id(0) == 0)
+    def _weights():
+        weight_ref[...] = jnp.zeros_like(weight_ref)
+        weight_ref[0:maps, 0:width] = map_ref[...]
+        weight_ref[HALF : HALF + maps, width : 2 * width] = map_ref[...]
+        both_ref[...] = jnp.concatenate(split(weight_ref[...]), axis=0)
+
+    w_both = both_ref[...]
+    w_high = w_both[:128]
     slots = berg_ref[...].reshape(owners, 2, pairs, width)
     both = jnp.concatenate([slots[:, h].reshape(rows, width) for h in range(2)], axis=1)
     b_high, b_low = split(both)
@@ -73,7 +79,7 @@
     owners = berg_count.shape[0]
     slots = bergs.shape[0] // owners
     width = bergs.shape[1]
-    steps = 4
+    steps = 8
     per = owners // steps
     return pl.pallas_call(
         melt_kernel,
@@ -85,7 +91,7 @@
             pl.BlockSpec(melt_map.shape[::-1], lambda i: (0, 0)),
         ],
         out_specs=pl.BlockSpec((per, slots // 2, 128), lambda i: (i, 0, 0)),
-        scratch_shapes=[VM((128, 2 * width), F32)],
+        scratch_shapes=[VM((128, 2 * width), F32), VM((256, 2 * width), BF16)],
         compiler_params=pltpu.CompilerParams(vmem_limit_bytes=LIMIT),
         name="melt",
     )(*in_hbm(berg_count, bergs, melt_map.T))
@@ -109,12 +115,9 @@
     def result(k):
         return pltpu.make_async_copy(ov.at[:, k], part_hbm.at[:, k], sem_o.at[k])
 
-    def start_level(k, _):
+    for k in range(AHEAD):
         for c in copies(k):
             c.start()
-        return _
-
-    lax.fori_loop(0, levels, start_level, 0)
     odd_lon = lax.rem(lax.axis_index("lon"), 2)
     odd_lat = lax.rem(lax.axis_index("lat"), 2)
     row_a = odd_lat * (rows - 1)
@@ -148,6 +151,11 @@
         packs = list(packs)
         above = jnp.minimum(k + 1, levels - 1)
         below = jnp.maximum(k - 1, 0)
+
+        @pl.when(k + AHEAD < levels)
+        def _start():
+            for c in copies(k + AHEAD):
+                c.start()
 
         @pl.when(k + 1 < levels)
         def _wait():
@@ -286,7 +294,7 @@
 
     @pl.when(lat_index == lat_count - 1)
     def _fold():
-        picks = fold_ref[...] - (lon_count - 1 - lon_index) * cols
+        picks = fold_ref[...].reshape(1, cols) - (lon_count - 1 - lon_index) * cols
         hot = (lax.broadcasted_iota(jnp.int32, (cols, cols), 0) == picks).astype(F32).astype(BF16)
         across = north[...]
         high, low = split(across)
@@ -329,7 +337,7 @@
         scratch_shapes=[VM(own[2].shape, F32), VM(own[2].shape, F32)],
         compiler_params=pltpu.CompilerParams(vmem_limit_bytes=LIMIT),
         name="fix",
-    )(*in_hbm(fold_partner.reshape(1, cols)), *own, *far)
+    )(*in_hbm(fold_partner), *own, *far)
 
 
 def order_kernel(cell_ref, place_ref, start_ref, mark_ref, base_ref, *, rows, cols, pairs):
@@ -438,9 +446,10 @@
 
     def spread(i, _):
         first = pl.multiple_of(i * pairs, pairs)
+        places = place_ref.at[pl.ds(2 * first, 2 * pairs)]
         for j in range(pairs):
             for h in range(2):
-                to = place_ref[2 * first + h * pairs + j]
+                to = places[h * pairs + j]
                 sorted_v[pl.ds(to, 1), :] = rows_v[pl.ds(h * n_rows + first + j, 1), :]
         return _
 
@@ -452,8 +461,8 @@
     def row_sources(r, at):
         at = pl.multiple_of(at, 8)
         lines = sorted_v[pl.ds(at, WINDOW), :]
-        lhs = lines.T.astype(BF16)
-        near = lines[:, CELL_LANE : CELL_LANE + 1] - (r * cols).astype(F32)
+        lhs = lines.astype(BF16).T
+        near = jnp.broadcast_to(lines[:, CELL_LANE : CELL_LANE + 1], (WINDOW, 128)) - (r * cols).astype(F32)
         hot = [jnp.where(near - float(128 * c) == lanef, 1.0, 0.0).astype(BF16) for c in range(tiles)]
         both = dot_nn(lhs, jnp.concatenate(hot, axis=1))
         return both[:HALF] + both[HALF:]
@@ -470,7 +479,8 @@
         for j in range(8):
             made = row_sources(8 * g + j, firsts[j])
             for c in range(tiles):
-                acc[c, j * HALF : (j + 1) * HALF, :] = made[:, c * 128 : (c + 1) * 128]
+                for m in range(0, maps, 8):
+                    acc[c, pl.ds(m * 9 + j, 8, stride=9), :] = made[m : m + 8, c * 128 : (c + 1) * 128]
         most = functools.reduce(jnp.maximum, windows)
 
         @pl.when(most > 1)
@@ -480,7 +490,10 @@
                 def again(i, _, j=j):
                     made = row_sources(8 * g + j, firsts[j] + i * WINDOW)
                     for c in range(tiles):
-                        acc[c, j * HALF : (j + 1) * HALF, :] += made[:, c * 128 : (c + 1) * 128]
+                        for m in range(0, maps, 8):
+                            acc[c, pl.ds(m * 9 + j, 8, stride=9), :] += made[
+                                m : m + 8, c * 128 : (c + 1) * 128
+                            ]
                     return _
 
                 lax.fori_loop(1, windows[j], again, 0)
@@ -503,7 +516,7 @@
             at = t * TR_LANES + levels - 1 - k
             for c in range(tiles):
                 lanes = slice(c * 128, (c + 1) * 128)
-                value = pv[t, k, here, lanes] + w[:, lanes] * acc[c, pl.ds(m, 8, stride=HALF), :]
+                value = pv[t, k, here, lanes] + w[:, lanes] * acc[c, 9 * m : 9 * m + 8, :]
                 if c == 0:
                     value += jnp.where(lane == 0, pltpu.roll(w_fix, (128 - at) % 128, 1), 0.0)
                 if c == tiles - 1:
@@ -530,7 +543,7 @@
             VM((2 * recv.shape[0] + WINDOW, 128), F32),
             VM(part.shape, F32),
             VM((rows, cols), F32),
-            VM((cols // 128, 8 * HALF, 128), F32),
+            VM((cols // 128, 9 * HALF, 128), F32),
             dma,
             dma,
         ],

time: 62.1 us -> 60.8 us (0.979)
  Pallas kernels: 39.9 us -> 38.5 us
    pallas_call x1, Pallas kernels: 17.1 us -> 13.2 us  [finish(): pl.pallas_call(functools.partial(final_kernel, pairs=pairs), out_shape=ja...]
    pallas_call x1, Pallas kernels: 4.23 us -> 6.4 us  [melt_rows(): pl.pallas_call(melt_kernel, grid=(steps,), out_shape=jax.ShapeDtypeStruct...]
  transfers between devices with their start and end apart: 5 -> 5, of which waited for: 1 -> 1; matrix products, arithmetic and copies ran while one was open for 1% -> 0% of each run, Pallas kernels for 30% -> 31%
where the time goes in v3:
time: 60.8 us; the launch traced here: 60.4 us
  Pallas kernels  38.5 us (63%)
  starting transfers between devices  20.4 us (34%)
  waiting for transfers between devices  1.36 us (2%)
    pallas_call x1, Pallas kernels, stencil(): pl.pallas_call(stencil_kernel, out_shape=(pltpu.HBM(tracers.shape, F32),...  16.4 us
    pallas_call x1, Pallas kernels, finish(): pl.pallas_call(functools.partial(final_kernel, pairs=pairs), out_shape=ja...  13.2 us
    all_to_all x1, starting transfers between devices, shards(): lax.all_to_all(melt, ('lon', 'lat'), split_axis=0, concat_axis=0, tiled=T...  10.5 us
    ppermute x4, starting transfers between devices, swap(): return lax.ppermute(value, axes, pairs + [(b, a) for a, b in pairs])  9.94 us
    pallas_call x1, Pallas kernels, melt_rows(): pl.pallas_call(melt_kernel, grid=(steps,), out_shape=jax.ShapeDtypeStruct...  6.4 us
    pallas_call x1, Pallas kernels, order(): pl.pallas_call(functools.partial(order_kernel, rows=rows, cols=cols, pair...  1.57 us
    ppermute x4, waiting for transfers between devices, swap(): return lax.ppermute(value, axes, pairs + [(b, a) for a, b in pairs])  1.36 us
  transfers between devices with their start and end apart: 5, of which 1 were waited for; matrix products, arithmetic and copies ran while one was open for 0% of the time, Pallas kernels for 31%

profile of v3, /device:TPU:4, one launch (start us, length us, event | category | flops | bytes accessed | tf_op | source)
XLA Modules:
  0.0 60.4 jit_solution(16708722681501596757)
XLA Ops:
  0.0 6.4 %melt.1 = f32[128,16,128]{2,1,0:T(8,128)} custom-call(s32[128]{0:T(128)} %count_ref.1, f32[4096,128]{1,0:T(8,128)} %berg_ref.1, f32[50,128]{1,0:T(8,128)} %bitcast.6), custom_call_target="tpu_custom_call" | custom-call | tf_op jit(solution)/shard_map/melt/pallas_call | solution.py:84
  6.4 10.5 %all-to-all-start = ((f32[128,16,128]{2,1,0:T(8,128)}), f32[128,16,128]{2,1,0:T(8,128)S(1)}, u32[]{:S(2)}, u32[]{:S(2)}) async-start(f32[128,16,128]{2,1,0:T(8,128)} %melt.1), calls=%async_computation | async-start | bytes 2097152 | tf_op jit(solution)/shard_map/all_to_all | solution.py:566
  16.9 16.4 %stencil.1 = (f32[2,25,64,384]{3,2,1,0:T(8,128)}, f32[64,128]{1,0:T(8,128)S(1)}, f32[64,128]{1,0:T(8,128)S(1)}, f32[80,384]{1,0:T(8,128)S(1)}, f32[80,384]{1,0:T(8,128)S(1)}) custom-call(f32[2,25,64,384]{3,2,1,0:T(8,128)} %tr_hbm.1, f32[25,64,384]{2,1,0:T(8,128)} %ea_hbm.1, f32[25,64,384]{2,1,0:T(8,128)} %no_hbm.1, s32[64,384]{1,0:T(8,128)} %wet_ref.3), custom_call_target="tpu_custom_call" | custom-call | tf_op jit(solution)/shard_map/stencil/pallas_call | solution.py:233
  33.3 4.6 %collective-permute-start.2 = (f32[80,384]{1,0:T(8,128)S(1)}, f32[80,384]{1,0:T(8,128)S(1)}, u32[]{:S(2)}, u32[]{:S(2)}) collective-permute-start(f32[80,384]{1,0:T(8,128)S(1)} %get-tuple-element.23.ns_a), channel_id=1, source_target_pairs={{1,2},{3,4},{5,6},{9,10},{11,12},{13,14},{17,18},{19,20},{21,22},{... | collective-permute-start | bytes 368648 | tf_op jit(solution)/shard_map/ppermute | solution.py:556
  38.0 0.3 collective-permute-start.3
  38.2 0.0 collective-permute-start
  38.2 5.0 %collective-permute-start.1 = (f32[64,128]{1,0:T(8,128)S(1)}, f32[64,128]{1,0:T(8,128)S(1)}, u32[]{:S(2)}, u32[]{:S(2)}) collective-permute-start(f32[64,128]{1,0:T(8,128)S(1)} %get-tuple-element.22.ew_b), channel_id=1, source_target_pairs={{8,16},{24,32},{40,48},{56,64},{72,80},{88,96},{104,112},{120,0},{... | collective-permute-start | bytes 98312 | tf_op jit(solution)/shard_map/ppermute | solution.py:556
  43.2 1.6 %order.1 = (s32[32,128]{1,0:T(8,128)S(1)}, s32[8,128]{1,0:T(8,128)S(1)}, f32[4096,128]{1,0:T(8,128)S(1)}) custom-call(s32[32,128]{1,0:T(8,128)} %bitcast.7), custom_call_target="tpu_custom_call" | custom-call | tf_op jit(solution)/shard_map/order/pallas_call | solution.py:387
  44.8 0.0 collective-permute-done.ew_a_in
  44.8 1.4 %collective-permute-done.1.ew_b_in = f32[64,128]{1,0:T(8,128)S(1)} collective-permute-done((f32[64,128]{1,0:T(8,128)S(1)}, f32[64,128]{1,0:T(8,128)S(1)}, u32[]{:S(2)}, u32[]{:S(2)}) %collective-permute-start.1) | collective-permute-done | bytes 32800 | tf_op jit(solution)/shard_map/ppermute | solution.py:556
  46.2 0.0 collective-permute-done.2.ns_a_in
  46.2 0.0 collective-permute-done.3.ns_b_in
  46.2 0.9 %fix.1 = (f32[64,128]{1,0:T(8,128)S(1)}, f32[64,128]{1,0:T(8,128)S(1)}, f32[50,384]{1,0:T(8,128)S(1)}, f32[50,384]{1,0:T(8,128)S(1)}) custom-call(s32[384]{0:T(512)} %fold_ref.1, f32[64,128]{1,0:T(8,128)S(1)} %get-tuple-element.21.ew_a, f32[64,128]{1,0:T(8,128)S(1)} %get-tuple-element.22.ew_b, f32[80,384]{1,0:T(8,128)S(1)} %get-tuple-element.23.ns_a, ...), custom_call_target="tpu_custom_call" | custom-call | tf_op jit(solution)/shard_map/fix/pallas_call | solution.py:327
  47.1 0.0 all-to-all-done
  47.2 13.2 %final.1 = f32[2,25,64,384]{3,2,1,0:T(8,128)} custom-call(s32[4096]{0:T(1024)S(1)} %bitcast.5, s32[8,128]{1,0:T(8,128)S(1)} %get-tuple-element.18.start_ref, f32[2048,128]{1,0:T(8,128)S(1)} %bitcast.4, f32[4096,128]{1,0:T(8,128)S(1)} %get-tuple-element.19.mark_ref, f32[2,25,64,384]{3,2,1,0:T(8,128)} %get-tuple-element.20.part_hbm, s32[64,384]{1,0:T(8,128)} %wet_ref.3, ...), custom_call_target="tpu_custom_call" | custom-call | tf_op jit(solution)/shard_map/final/pallas_call | solution.py:536
Async XLA Ops:
  6.4 40.7 %all-to-all-start = ((f32[128,16,128]{2,1,0:T(8,128)}), f32[128,16,128]{2,1,0:T(8,128)S(1)}, u32[]{:S(2)}, u32[]{:S(2)}) async-start(f32[128,16,128]{2,1,0:T(8,128)} %melt.1), calls=%async_computation | async-start | bytes 2097152 | tf_op jit(solution)/shard_map/all_to_all | solution.py:566
  33.3 12.9 %collective-permute-start.2 = (f32[80,384]{1,0:T(8,128)S(1)}, f32[80,384]{1,0:T(8,128)S(1)}, u32[]{:S(2)}, u32[]{:S(2)}) collective-permute-start(f32[80,384]{1,0:T(8,128)S(1)} %get-tuple-element.23.ns_a), channel_id=1, source_target_pairs={{1,2},{3,4},{5,6},{9,10},{11,12},{13,14},{17,18},{19,20},{21,22},{... | collective-permute-start | bytes 368648 | tf_op jit(solution)/shard_map/ppermute | solution.py:556
  38.0 8.2 %collective-permute-start.3 = (f32[80,384]{1,0:T(8,128)S(1)}, f32[80,384]{1,0:T(8,128)S(1)}, u32[]{:S(2)}, u32[]{:S(2)}) collective-permute-start(f32[80,384]{1,0:T(8,128)S(1)} %get-tuple-element.24.ns_b), channel_id=1, source_target_pairs={{0,1},{2,3},{4,5},{6,7},{1,0},{3,2},{5,4},{7,6},{8,9},{10,11},{12,... | collective-permute-start | bytes 368648 | tf_op jit(solution)/shard_map/ppermute | solution.py:556
  38.2 6.6 %collective-permute-start = (f32[64,128]{1,0:T(8,128)S(1)}, f32[64,128]{1,0:T(8,128)S(1)}, u32[]{:S(2)}, u32[]{:S(2)}) collective-permute-start(f32[64,128]{1,0:T(8,128)S(1)} %get-tuple-element.21.ew_a), channel_id=1, source_target_pairs={{0,8},{16,24},{32,40},{48,56},{64,72},{80,88},{96,104},{112,120},{... | collective-permute-start | bytes 98312 | tf_op jit(solution)/shard_map/ppermute | solution.py:556
  38.2 7.9 %collective-permute-start.1 = (f32[64,128]{1,0:T(8,128)S(1)}, f32[64,128]{1,0:T(8,128)S(1)}, u32[]{:S(2)}, u32[]{:S(2)}) collective-permute-start(f32[64,128]{1,0:T(8,128)S(1)} %get-tuple-element.22.ew_b), channel_id=1, source_target_pairs={{8,16},{24,32},{40,48},{56,64},{72,80},{88,96},{104,112},{120,0},{... | collective-permute-start | bytes 98312 | tf_op jit(solution)/shard_map/ppermute | solution.py:556

commit v4 on v3

--- a/solution.py
+++ b/solution.py
@@ -22,9 +22,11 @@
 TR_LANES = 32
 HALF = 64
 WET_LANE = 127
-AHEAD = 5
+MELT_STEPS = 4
+FIRSTS = (0, 1, 5, 13)
+PARTS = (0, 2)
 WINDOW = 128
-CELL_LANE = 50
+CELL_LANE = 25
 
 
 def in_hbm(*values):
@@ -45,53 +47,67 @@
     return lax.dot_general(a, b, (((1,), (0,)), ((), ())), preferred_element_type=F32)
 
 
-def melt_kernel(count_ref, berg_ref, map_ref, out_ref, weight_ref, both_ref):
+def melt_kernel(count_ref, berg_hbm, map_ref, out_hbm, berg_v, out_v, weight_ref, sem_i, sem_o):
     maps = map_ref.shape[0]
-    width = berg_ref.shape[1]
-    owners = out_ref.shape[0]
-    pairs = out_ref.shape[1]
-    rows = owners * pairs
-
-    @pl.when(pl.program_id(0) == 0)
-    def _weights():
-        weight_ref[...] = jnp.zeros_like(weight_ref)
-        weight_ref[0:maps, 0:width] = map_ref[...]
-        weight_ref[HALF : HALF + maps, width : 2 * width] = map_ref[...]
-        both_ref[...] = jnp.concatenate(split(weight_ref[...]), axis=0)
-
-    w_both = both_ref[...]
-    w_high = w_both[:128]
-    slots = berg_ref[...].reshape(owners, 2, pairs, width)
-    both = jnp.concatenate([slots[:, h].reshape(rows, width) for h in range(2)], axis=1)
-    b_high, b_low = split(both)
-    wide = dot_nt(b_high, w_both)
-    made = wide[:, :128] + (wide[:, 128:] + dot_nt(b_low, w_high))
+    width = berg_v.shape[1]
+    owners, pairs = out_v.shape[:2]
+    steps = MELT_STEPS
+    per = owners // steps
+    rows = per * pairs
+
+    def load(i):
+        span = pl.ds(i * 2 * rows, 2 * rows)
+        return pltpu.make_async_copy(berg_hbm.at[span], berg_v.at[span], sem_i.at[i])
+
+    def store(i):
+        span = pl.ds(i * per, per)
+        return pltpu.make_async_copy(out_v.at[span], out_hbm.at[span], sem_o)
+
+    for i in range(steps):
+        load(i).start()
+    weight_ref[...] = jnp.zeros_like(weight_ref)
+    for h in range(2):
+        for t in range(2):
+            place = h * HALF + t * TR_LANES
+            weight_ref[place : place + maps // 2, h * width : (h + 1) * width] = map_ref[
+                t * (maps // 2) : (t + 1) * (maps // 2), :
+            ]
+    w_high, w_low = split(weight_ref[...])
+    w_both = jnp.concatenate([w_high, w_low], axis=0)
     lane = lax.broadcasted_iota(jnp.int32, (pairs, 128), 1)
     slot = lax.broadcasted_iota(jnp.int32, (pairs, 128), 0) + jnp.where(lane >= HALF, pairs, 0)
-    first = pl.program_id(0) * owners
-    for o in range(owners):
-        out_ref[o] = jnp.where(
-            slot < count_ref[first + o], made[o * pairs : (o + 1) * pairs], 0.0
-        )
+    for i in range(steps):
+        load(i).wait()
+        slots = berg_v[i * 2 * rows : (i + 1) * 2 * rows, :].reshape(per, 2, pairs, width)
+        both = jnp.concatenate([slots[:, h].reshape(rows, width) for h in range(2)], axis=1)
+        b_high, b_low = split(both)
+        wide = dot_nt(b_high, w_both)
+        made = wide[:, :128] + (wide[:, 128:] + dot_nt(b_low, w_high))
+        for o in range(per):
+            out_v[i * per + o] = jnp.where(
+                slot < count_ref[i * per + o], made[o * pairs : (o + 1) * pairs], 0.0
+            )
+        store(i).start()
+    pltpu.make_async_copy(out_v, out_hbm, sem_o).wait()
 
 
 def melt_rows(bergs, berg_count, melt_map):
     owners = berg_count.shape[0]
-    slots = bergs.shape[0] // owners
+    pairs = bergs.shape[0] // owners // 2
     width = bergs.shape[1]
-    steps = 8
-    per = owners // steps
+    dma = pltpu.SemaphoreType.DMA((MELT_STEPS,))
     return pl.pallas_call(
         melt_kernel,
-        grid=(steps,),
-        out_shape=jax.ShapeDtypeStruct((owners, slots // 2, 128), F32),
-        in_specs=[
-            SMEM_SPEC,
-            pl.BlockSpec((per * slots, width), lambda i: (i, 0)),
-            pl.BlockSpec(melt_map.shape[::-1], lambda i: (0, 0)),
+        out_shape=jax.ShapeDtypeStruct((owners, pairs, 128), F32),
+        in_specs=[SMEM_SPEC, ANY_SPEC, VMEM_SPEC],
+        out_specs=ANY_SPEC,
+        scratch_shapes=[
+            VM(bergs.shape, F32),
+            VM((owners, pairs, 128), F32),
+            VM((128, 2 * width), F32),
+            dma,
+            pltpu.SemaphoreType.DMA,
         ],
-        out_specs=pl.BlockSpec((per, slots // 2, 128), lambda i: (i, 0, 0)),
-        scratch_shapes=[VM((128, 2 * width), F32), VM((256, 2 * width), BF16)],
         compiler_params=pltpu.CompilerParams(vmem_limit_bytes=LIMIT),
         name="melt",
     )(*in_hbm(berg_count, bergs, melt_map.T))
@@ -100,24 +116,29 @@
 def stencil_kernel(
     tr_hbm, ea_hbm, no_hbm, wet_ref,
     part_hbm, ew_a, ew_b, ns_a, ns_b,
-    tv, ev, nv, ov, m_e, m_n, wetf, sem_t, sem_e, sem_n, sem_o,
+    tv, ev, nv, ov, faces, wetf, packs, sem_t, sem_e, sem_n, sem_o,
 ):
     levels, rows, cols = ea_hbm.shape
     strips = rows // 8
 
-    def copies(k):
+    firsts = FIRSTS
+    lasts = firsts[1:] + (levels,)
+
+    def copies(c):
+        span = pl.ds(firsts[c], lasts[c] - firsts[c])
         return (
-            pltpu.make_async_copy(tr_hbm.at[:, k], tv.at[:, k], sem_t.at[k]),
-            pltpu.make_async_copy(ea_hbm.at[k], ev.at[k], sem_e.at[k]),
-            pltpu.make_async_copy(no_hbm.at[k], nv.at[k], sem_n.at[k]),
+            pltpu.make_async_copy(tr_hbm.at[:, span], tv.at[:, span], sem_t.at[c]),
+            pltpu.make_async_copy(ea_hbm.at[span], ev.at[span], sem_e.at[c]),
+            pltpu.make_async_copy(no_hbm.at[span], nv.at[span], sem_n.at[c]),
         )
 
-    def result(k):
-        return pltpu.make_async_copy(ov.at[:, k], part_hbm.at[:, k], sem_o.at[k])
-
-    for k in range(AHEAD):
-        for c in copies(k):
-            c.start()
+    def result(c):
+        span = pl.ds(firsts[c], lasts[c] - firsts[c])
+        return pltpu.make_async_copy(ov.at[:, span], part_hbm.at[:, span], sem_o)
+
+    for c in range(len(firsts)):
+        for copy in copies(c):
+            copy.start()
     odd_lon = lax.rem(lax.axis_index("lon"), 2)
     odd_lat = lax.rem(lax.axis_index("lat"), 2)
     row_a = odd_lat * (rows - 1)
@@ -127,8 +148,14 @@
     wetf[...] = wet
     col = lax.broadcasted_iota(jnp.int32, (rows, cols), 1)
     row = lax.broadcasted_iota(jnp.int32, (rows, cols), 0)
-    m_e[...] = jnp.where(col == cols - 1, 0.0, wet * pltpu.roll(wet, cols - 1, 1))
-    m_n[...] = jnp.where(row == rows - 1, 0.0, wet * pltpu.roll(wet, rows - 1, 0))
+    for at, face in enumerate(
+        (
+            jnp.where(col == cols - 1, 0.0, wet * pltpu.roll(wet, cols - 1, 1)),
+            jnp.where(row == rows - 1, 0.0, wet * pltpu.roll(wet, rows - 1, 0)),
+        )
+    ):
+        faces[2 * at] = (0.25 * time_step) * face
+        faces[2 * at + 1] = (diffuse_h * time_step) * face
     lane_all = lax.broadcasted_iota(jnp.int32, (rows, 128), 1)
     ns_a[...] = jnp.zeros_like(ns_a)
     ns_b[...] = jnp.zeros_like(ns_b)
@@ -137,99 +164,97 @@
 
     lane = lax.broadcasted_iota(jnp.int32, (8, 128), 1)
     top = lax.broadcasted_iota(jnp.int32, (8, cols), 0) == 0
-    marks = [lane == 0, lane == TR_LANES, lane == HALF]
-
-    def next_row(ref, lead, s):
-        if s < strips - 1:
-            return ref[lead + (pl.ds(8 * s + 1, 8), slice(None))]
-        return pltpu.roll(ref[lead + (pl.ds(8 * s, 8), slice(None))], 7, 0)
-
-    for c in copies(0):
-        c.wait()
-
-    def level(k, packs):
-        packs = list(packs)
+    last_lane = lane == 127
+    packs[...] = jnp.zeros_like(packs)
+
+    bottom = lax.broadcasted_iota(jnp.int32, (8, cols), 0) == 7
+
+    def level(k, _):
         above = jnp.minimum(k + 1, levels - 1)
         below = jnp.maximum(k - 1, 0)
-
-        @pl.when(k + AHEAD < levels)
-        def _start():
-            for c in copies(k + AHEAD):
-                c.start()
-
-        @pl.when(k + 1 < levels)
-        def _wait():
-            for c in copies(k + 1):
-                c.wait()
+        for c in range(len(firsts)):
+
+            @pl.when(k == max(firsts[c] - 1, 0))
+            def _wait(c=c):
+                for copy in copies(c):
+                    copy.wait()
 
         carried = [None, None]
+        fields = [tv.at[0, k], tv.at[1, k], nv.at[k]]
+        own = [f[0:8, :] for f in fields]
+        risen = [pltpu.roll(f, 7, 0) for f in own]
         for s in range(strips):
             here = pl.ds(8 * s, 8)
+            if s < strips - 1:
+                later = [f[8 * s + 8 : 8 * s + 16, :] for f in fields]
+                later_risen = [pltpu.roll(f, 7, 0) for f in later]
+                north = [jnp.where(bottom, b, a) for a, b in zip(risen, later_risen)]
+            else:
+                later, later_risen, north = own, risen, risen
             u = ev[k, here, :]
-            v = nv[k, here, :]
-            me = m_e[here, :]
-            mn = m_n[here, :]
+            v = own[2]
             w = wetf[here, :]
-            s_e = (0.25 * time_step * me) * (u + pltpu.roll(u, cols - 1, 1))
-            s_n = (0.25 * time_step * mn) * (v + next_row(nv, (k,), s))
-            d_e = (diffuse_h * time_step) * me
-            d_n = (diffuse_h * time_step) * mn
+            u_next = pltpu.roll(u, cols - 1, 1)
+            s_e = faces[0, here, :] * (u + u_next)
+            s_n = faces[2, here, :] * (v + north[2])
+            d_e = faces[1, here, :]
+            d_n = faces[3, here, :]
             a_e, b_e, a_n, b_n = s_e + d_e, s_e - d_e, s_n + d_n, s_n - d_n
-            edge = []
+            ends = [None, None, (u_next, u)]
             for t in range(2):
-                q = tv[t, k, here, :]
-                edge.append(q)
+                q = own[t]
                 up = tv[t, above, here, :]
                 dn = tv[t, below, here, :]
-                fe = q * a_e + pltpu.roll(q, cols - 1, 1) * b_e
-                fn = q * a_n + next_row(tv, (t, k), s) * b_n
+                q_next = pltpu.roll(q, cols - 1, 1)
+                ends[t] = (q_next, q)
+                fe = q * a_e + q_next * b_e
+                fn = q * a_n + north[t] * b_n
                 fw = pltpu.roll(fe, 1, 1)
                 turned = pltpu.roll(fn, 1, 0)
                 last = jnp.zeros_like(turned) if carried[t] is None else carried[t]
                 fs = jnp.where(top, last, turned)
                 carried[t] = turned
-                mix = (diffuse_v * time_step) * ((up - q) - (q - dn))
-                ov[t, k, here, :] = w * (q + ((mix - (fe - fw)) - (fn - fs)))
-            edge.append(u)
-            for side, lanes, shift in ((0, slice(0, 128), 0), (1, slice(cols - 128, cols), 1)):
-                old = pltpu.roll(packs[2 * s + side], 1, 1)
-                for at, (field, mark) in enumerate(zip(edge, marks)):
-                    turn = at * TR_LANES + shift
-                    moved = pltpu.roll(field[:, lanes], turn, 1) if turn else field[:, lanes]
-                    old = jnp.where(mark, moved, old)
-                packs[2 * s + side] = old
+                mix = (1 - 2 * diffuse_v * time_step) * q + (diffuse_v * time_step) * (up + dn)
+                ov[t, k, here, :] = w * ((mix - (fe - fw)) - (fn - fs))
+            for at in range(3):
+                for side in range(2):
+                    end = ends[at][side][:, cols - 128 :]
+                    packs[at, side, here, :] = jnp.where(
+                        last_lane, end, pltpu.roll(packs[at, side, here, :], 127, 1)
+                    )
+            own, risen = later, later_risen
         for ref, at in ((ns_a, row_a), (ns_b, row_b)):
             ref[pl.ds(k, 1), :] = tv[0, k, pl.ds(at, 1), :]
             ref[pl.ds(levels + k, 1), :] = tv[1, k, pl.ds(at, 1), :]
             ref[pl.ds(2 * levels + k, 1), :] = nv[k, pl.ds(at, 1), :]
-        result(k).start()
-        return tuple(packs)
-
-    packs = lax.fori_loop(0, levels, level, (jnp.zeros((8, 128), F32),) * (2 * strips))
-    west = jnp.concatenate(packs[0::2], axis=0)
-    east = jnp.concatenate(packs[1::2], axis=0)
-
-    def again(value, mask):
-        speed = (lane_all >= HALF + TR_LANES) & (lane_all < HALF + TR_LANES + levels)
-        value = jnp.where(speed, pltpu.roll(value, TR_LANES, 1), value)
-        return jnp.where(lane_all == WET_LANE, mask, value)
+        for c in range(len(firsts)):
+
+            @pl.when(k == lasts[c] - 1)
+            def _send(c=c):
+                result(c).start()
+
+        return _
+
+    lax.fori_loop(0, levels, level, 0)
+
+    def packed(side, mask):
+        value = jnp.where(lane_all == WET_LANE, mask, 0.0)
+        for at, place in ((0, 0), (1, TR_LANES), (2, HALF), (2, HALF + TR_LANES)):
+            here = (lane_all >= place) & (lane_all < place + levels)
+            value = jnp.where(here, pltpu.roll(packs[at, side], levels + place, 1), value)
+        return value
 
     is_odd = odd_lon == 1
-    west_all, east_all = again(west, wetf[:, 0:1]), again(east, wetf[:, cols - 1 : cols])
-    ew_a[...] = jnp.where(is_odd, west_all, east_all)
-    ew_b[...] = jnp.where(is_odd, east_all, west_all)
-
-    def done(k, _):
-        result(k).wait()
-        return _
-
-    lax.fori_loop(0, levels, done, 0)
+    west, east = packed(0, wetf[:, 0:1]), packed(1, wetf[:, cols - 1 : cols])
+    ew_a[...] = jnp.where(is_odd, west, east)
+    ew_b[...] = jnp.where(is_odd, east, west)
+    pltpu.make_async_copy(ov, part_hbm, sem_o).wait()
 
 
 def stencil(tracers, east_speed, north_speed, wet):
     count, levels, rows, cols = tracers.shape
     edge_rows = -(-(3 * levels + 1) // 8) * 8
-    dma = pltpu.SemaphoreType.DMA((levels,))
+    dma = pltpu.SemaphoreType.DMA((len(FIRSTS),))
     return pl.pallas_call(
         stencil_kernel,
         out_shape=(
@@ -246,13 +271,13 @@
             VM(east_speed.shape, F32),
             VM(north_speed.shape, F32),
             VM(tracers.shape, F32),
+            VM((4, rows, cols), F32),
             VM((rows, cols), F32),
-            VM((rows, cols), F32),
-            VM((rows, cols), F32),
+            VM((3, 2, rows, 128), F32),
             dma,
             dma,
             dma,
-            dma,
+            pltpu.SemaphoreType.DMA,
         ],
         compiler_params=pltpu.CompilerParams(vmem_limit_bytes=20 << 20),
         name="stencil",
@@ -261,7 +286,7 @@
 
 def fix_kernel(
     fold_ref, ew_a, ew_b, ns_a, ns_b, ew_a_in, ew_b_in, ns_a_in, ns_b_in,
-    fix_e, fix_w, fix_n, fix_s, north, south,
+    fix_c, fix_n, fix_s, north, south,
 ):
     levels = fix_n.shape[0] // 2
     cols = ns_a.shape[1]
@@ -286,8 +311,16 @@
     west_own = column(pick(odd_lon, ew_a[...], ew_b[...]))
     east_far = column(pick(odd_lon, ew_b_in[...], ew_a_in[...]))
     west_far = column(pick(odd_lon, ew_a_in[...], ew_b_in[...]))
-    fix_e[...] = -(east_own[2] * faces(*east_own, *east_far))
-    fix_w[...] = west_own[2] * faces(*west_far, *west_own)
+    lane = lax.broadcasted_iota(jnp.int32, ew_a.shape, 1)
+    first = lax.broadcasted_iota(jnp.int32, ew_a.shape, 0) * cols
+    for at, value, cell in (
+        (0, -(east_own[2] * faces(*east_own, *east_far)), first + (cols - 1)),
+        (1, west_own[2] * faces(*west_far, *west_own), first),
+    ):
+        high = value.astype(BF16).astype(F32)
+        body = jnp.where(lane < HALF, high, pltpu.roll(value - high, HALF, 1))
+        fix_c[at] = jnp.where(lane == CELL_LANE, cell.astype(F32), body)
+
 
     north[...] = pick(odd_lat, ns_a_in[...], ns_b_in[...])
     south[...] = pick(odd_lat, ns_b_in[...], ns_a_in[...])
@@ -327,13 +360,12 @@
     return pl.pallas_call(
         fix_kernel,
         out_shape=(
-            jax.ShapeDtypeStruct((rows, 128), F32),
-            jax.ShapeDtypeStruct((rows, 128), F32),
+            jax.ShapeDtypeStruct((2, rows, 128), F32),
             jax.ShapeDtypeStruct((2 * levels, cols), F32),
             jax.ShapeDtypeStruct((2 * levels, cols), F32),
         ),
         in_specs=[VMEM_SPEC] * 9,
-        out_specs=(VMEM_SPEC,) * 4,
+        out_specs=(VMEM_SPEC,) * 3,
         scratch_shapes=[VM(own[2].shape, F32), VM(own[2].shape, F32)],
         compiler_params=pltpu.CompilerParams(vmem_limit_bytes=LIMIT),
         name="fix",
@@ -365,15 +397,17 @@
         base_ref[c * 128 : (c + 1) * 128, :] = base
         spot = base + within[c * 128 : (c + 1) * 128]
         for j in range(per):
-            place = place + hot[c * per + j] * spot[j * blocks : (j + 1) * blocks]
+            extra = 2.0 * (c * per + j + 1)
+            place = place + hot[c * per + j] * (spot[j * blocks : (j + 1) * blocks] + extra)
     place_ref[...] = place.astype(jnp.int32)
     starts = base_ref[pl.ds(0, rows, stride=blocks), :]
     high = jnp.floor(starts * (1.0 / 128))
     low = starts - 128 * high
     first = jnp.where(along[:8] == 0, 1.0, 0.0).astype(BF16)
     starts = 128 * dot_nt(first, high.astype(BF16)) + dot_nt(first, low.astype(BF16))
-    start_ref[...] = jnp.full(start_ref.shape, count, jnp.int32)
-    start_ref[:, 0:rows] = starts.astype(jnp.int32)
+    extra = 2.0 * lax.broadcasted_iota(jnp.int32, starts.shape, 1).astype(F32)
+    start_ref[...] = jnp.full(start_ref.shape, count + 2 * rows, jnp.int32)
+    start_ref[:, 0:rows] = (starts + extra).astype(jnp.int32)
     for i in range(blocks):
         turned = jnp.broadcast_to(cell[i : i + 1], (128, 128)).T
         for j in range(128 // pairs):
@@ -400,7 +434,7 @@
 
 
 def final_kernel(
-    place_ref, start_ref, recv_ref, mark_ref, part_hbm, wet_ref, fix_e, fix_w, fix_n, fix_s,
+    place_ref, start_ref, recv_ref, mark_ref, part_hbm, wet_ref, fix_c, fix_n, fix_s,
     out_hbm,
     rows_v, sorted_v, pv, wetf, acc, sem_i, sem_o, *, pairs,
 ):
@@ -409,18 +443,18 @@
     tiles = cols // 128
     maps = 2 * levels
     n_rows = recv_ref.shape[0]
-    count = 2 * n_rows
-
-    def load(g):
-        here = pl.ds(pl.multiple_of(8 * g, 8), 8)
-        return pltpu.make_async_copy(part_hbm.at[:, :, here], pv.at[:, :, here], sem_i.at[g])
+    count = 2 * (n_rows + rows)
+
+    def load(i):
+        here = pl.ds(8 * PARTS[i], 8 * ((PARTS[1:] + (groups,))[i] - PARTS[i]))
+        return pltpu.make_async_copy(part_hbm.at[:, :, here], pv.at[:, :, here], sem_i.at[i])
 
     def store(g):
         here = pl.ds(pl.multiple_of(8 * g, 8), 8)
-        return pltpu.make_async_copy(pv.at[:, :, here], out_hbm.at[:, :, here], sem_o.at[g])
-
-    for g in range(groups):
-        load(g).start()
+        return pltpu.make_async_copy(pv.at[:, :, here], out_hbm.at[:, :, here], sem_o)
+
+    for i in range(len(PARTS)):
+        load(i).start()
     lane_all = lax.broadcasted_iota(jnp.int32, (128, 128), 1)
     low_half = lane_all < HALF
     cell_lane = lane_all == CELL_LANE
@@ -454,8 +488,11 @@
         return _
 
     lax.fori_loop(0, n_rows // pairs, spread, 0)
-
-    lane = lax.broadcasted_iota(jnp.int32, (8, 128), 1)
+    for r in range(rows):
+        first = start_ref[0, r]
+        for h in range(2):
+            sorted_v[pl.ds(first + h, 1), :] = fix_c[h, r : r + 1, :]
+
     lanef = lax.broadcasted_iota(jnp.int32, (WINDOW, 128), 1).astype(F32)
 
     def row_sources(r, at):
@@ -479,7 +516,7 @@
         for j in range(8):
             made = row_sources(8 * g + j, firsts[j])
             for c in range(tiles):
-                for m in range(0, maps, 8):
+                for m in range(0, HALF, 8):
                     acc[c, pl.ds(m * 9 + j, 8, stride=9), :] = made[m : m + 8, c * 128 : (c + 1) * 128]
         most = functools.reduce(jnp.maximum, windows)
 
@@ -490,7 +527,7 @@
                 def again(i, _, j=j):
                     made = row_sources(8 * g + j, firsts[j] + i * WINDOW)
                     for c in range(tiles):
-                        for m in range(0, maps, 8):
+                        for m in range(0, HALF, 8):
                             acc[c, pl.ds(m * 9 + j, 8, stride=9), :] += made[
                                 m : m + 8, c * 128 : (c + 1) * 128
                             ]
@@ -498,10 +535,13 @@
 
                 lax.fori_loop(1, windows[j], again, 0)
 
-        load(g).wait()
+        for i in range(len(PARTS)):
+
+            @pl.when(g == PARTS[i])
+            def _wait(i=i):
+                load(i).wait()
+
         w = wetf[here, :]
-        e_fix = fix_e[here, :]
-        w_fix = fix_w[here, :]
 
         for edge, ref, at in ((groups - 1, fix_n, rows - 1), (0, fix_s, 0)):
 
@@ -513,39 +553,32 @@
 
         for m in range(maps):
             t, k = m // levels, m % levels
-            at = t * TR_LANES + levels - 1 - k
+            at = 9 * (t * TR_LANES + k)
             for c in range(tiles):
                 lanes = slice(c * 128, (c + 1) * 128)
-                value = pv[t, k, here, lanes] + w[:, lanes] * acc[c, 9 * m : 9 * m + 8, :]
-                if c == 0:
-                    value += jnp.where(lane == 0, pltpu.roll(w_fix, (128 - at) % 128, 1), 0.0)
-                if c == tiles - 1:
-                    value += jnp.where(lane == 127, pltpu.roll(e_fix, 127 - at, 1), 0.0)
-                pv[t, k, here, lanes] = value
+                pv[t, k, here, lanes] += w[:, lanes] * acc[c, at : at + 8, :]
         store(g).start()
         return _
 
     lax.fori_loop(0, groups, group, 0)
-    for g in range(groups):
-        store(g).wait()
+    pltpu.make_async_copy(pv, out_hbm, sem_o).wait()
 
 
 def finish(place, start, recv, mark, part, wet, fix, pairs):
     _, levels, rows, cols = part.shape
-    dma = pltpu.SemaphoreType.DMA((rows // 8,))
     return pl.pallas_call(
         functools.partial(final_kernel, pairs=pairs),
         out_shape=jax.ShapeDtypeStruct(part.shape, F32),
-        in_specs=[SMEM_SPEC] * 2 + [VMEM_SPEC] * 2 + [ANY_SPEC] + [VMEM_SPEC] * 5,
+        in_specs=[SMEM_SPEC] * 2 + [VMEM_SPEC] * 2 + [ANY_SPEC] + [VMEM_SPEC] * 4,
         out_specs=ANY_SPEC,
         scratch_shapes=[
             VM((2 * recv.shape[0], 128), F32),
-            VM((2 * recv.shape[0] + WINDOW, 128), F32),
+            VM((2 * recv.shape[0] + 2 * rows + WINDOW, 128), F32),
             VM(part.shape, F32),
             VM((rows, cols), F32),
             VM((cols // 128, 9 * HALF, 128), F32),
-            dma,
-            dma,
+            pltpu.SemaphoreType.DMA((len(PARTS),)),
+            pltpu.SemaphoreType.DMA,
         ],
         compiler_params=pltpu.CompilerParams(vmem_limit_bytes=24 << 20),
         name="final",

time: 60.8 us -> 57.5 us (0.946)
  Pallas kernels: 38.5 us -> 35.2 us
    pallas_call x2, Pallas kernels: 7.34 us -> 4.89 us  [the longest x1 3.87 us: melt_rows(): pl.pallas_call(melt_kernel, out_shape=jax.ShapeDtypeStruct((owners, pairs...]
    pallas_call x1, Pallas kernels: 13.2 us -> 12.2 us  [finish(): pl.pallas_call(functools.partial(final_kernel, pairs=pairs), out_shape=ja...]
  transfers between devices with their start and end apart: 5 -> 5, of which waited for: 1 -> 1; matrix products, arithmetic and copies ran while one was open for 0% -> 0% of each run, Pallas kernels for 31% -> 33%
where the time goes in v4:
time: 57.5 us; the launch traced here: 57.1 us
  Pallas kernels  35.2 us (61%)
  starting transfers between devices  20.4 us (35%)
  waiting for transfers between devices  1.43 us (2%)
    pallas_call x1, Pallas kernels, stencil(): pl.pallas_call(stencil_kernel, out_shape=(pltpu.HBM(tracers.shape, F32),...  16.6 us
    pallas_call x1, Pallas kernels, finish(): pl.pallas_call(functools.partial(final_kernel, pairs=pairs), out_shape=ja...  12.2 us
    all_to_all x1, starting transfers between devices, shards(): lax.all_to_all(melt, ('lon', 'lat'), split_axis=0, concat_axis=0, tiled=T...  10.5 us
    ppermute x4, starting transfers between devices, swap(): return lax.ppermute(value, axes, pairs + [(b, a) for a, b in pairs])  9.92 us
    pallas_call x1, Pallas kernels, melt_rows(): pl.pallas_call(melt_kernel, out_shape=jax.ShapeDtypeStruct((owners, pairs...  3.87 us
    pallas_call x1, Pallas kernels, order(): pl.pallas_call(functools.partial(order_kernel, rows=rows, cols=cols, pair...  1.52 us
    ppermute x4, waiting for transfers between devices, swap(): return lax.ppermute(value, axes, pairs + [(b, a) for a, b in pairs])  1.42 us
  transfers between devices with their start and end apart: 5, of which 1 were waited for; matrix products, arithmetic and copies ran while one was open for 0% of the time, Pallas kernels for 33%

profile of v4, /device:TPU:4, one launch (start us, length us, event | category | flops | bytes accessed | tf_op | source)
XLA Modules:
  0.0 57.1 jit_solution(2741100396951116813)
XLA Ops:
  0.0 3.9 %melt.1 = f32[128,16,128]{2,1,0:T(8,128)} custom-call(s32[128]{0:T(128)} %count_ref.1, f32[4096,128]{1,0:T(8,128)} %berg_hbm.1, f32[50,128]{1,0:T(8,128)} %bitcast.6), custom_call_target="tpu_custom_call" | custom-call | tf_op jit(solution)/shard_map/melt/pallas_call | solution.py:99
  3.9 10.5 %all-to-all-start = ((f32[128,16,128]{2,1,0:T(8,128)}), f32[128,16,128]{2,1,0:T(8,128)S(1)}, u32[]{:S(2)}, u32[]{:S(2)}) async-start(f32[128,16,128]{2,1,0:T(8,128)} %melt.1), calls=%async_computation | async-start | bytes 2097152 | tf_op jit(solution)/shard_map/all_to_all | solution.py:599
  14.4 16.6 %stencil.1 = (f32[2,25,64,384]{3,2,1,0:T(8,128)}, f32[64,128]{1,0:T(8,128)S(1)}, f32[64,128]{1,0:T(8,128)S(1)}, f32[80,384]{1,0:T(8,128)S(1)}, f32[80,384]{1,0:T(8,128)S(1)}) custom-call(f32[2,25,64,384]{3,2,1,0:T(8,128)} %tr_hbm.1, f32[25,64,384]{2,1,0:T(8,128)} %ea_hbm.1, f32[25,64,384]{2,1,0:T(8,128)} %no_hbm.1, s32[64,384]{1,0:T(8,128)} %wet_ref.3), custom_call_target="tpu_custom_call" | custom-call | tf_op jit(solution)/shard_map/stencil/pallas_call | solution.py:258
  31.0 4.6 %collective-permute-start.2 = (f32[80,384]{1,0:T(8,128)S(1)}, f32[80,384]{1,0:T(8,128)S(1)}, u32[]{:S(2)}, u32[]{:S(2)}) collective-permute-start(f32[80,384]{1,0:T(8,128)S(1)} %get-tuple-element.22.ns_a), channel_id=1, source_target_pairs={{1,2},{3,4},{5,6},{9,10},{11,12},{13,14},{17,18},{19,20},{21,22},{... | collective-permute-start | bytes 368648 | tf_op jit(solution)/shard_map/ppermute | solution.py:589
  35.6 0.3 collective-permute-start.3
  35.9 0.0 collective-permute-start
  35.9 5.0 %collective-permute-start.1 = (f32[64,128]{1,0:T(8,128)S(1)}, f32[64,128]{1,0:T(8,128)S(1)}, u32[]{:S(2)}, u32[]{:S(2)}) collective-permute-start(f32[64,128]{1,0:T(8,128)S(1)} %get-tuple-element.21.ew_b), channel_id=1, source_target_pairs={{8,16},{24,32},{40,48},{56,64},{72,80},{88,96},{104,112},{120,0},{... | collective-permute-start | bytes 98312 | tf_op jit(solution)/shard_map/ppermute | solution.py:589
  40.9 1.5 %order.1 = (s32[32,128]{1,0:T(8,128)S(1)}, s32[8,128]{1,0:T(8,128)S(1)}, f32[4096,128]{1,0:T(8,128)S(1)}) custom-call(s32[32,128]{1,0:T(8,128)} %bitcast.7), custom_call_target="tpu_custom_call" | custom-call | tf_op jit(solution)/shard_map/order/pallas_call | solution.py:421
  42.4 0.0 collective-permute-done.ew_a_in
  42.4 1.4 %collective-permute-done.1.ew_b_in = f32[64,128]{1,0:T(8,128)S(1)} collective-permute-done((f32[64,128]{1,0:T(8,128)S(1)}, f32[64,128]{1,0:T(8,128)S(1)}, u32[]{:S(2)}, u32[]{:S(2)}) %collective-permute-start.1) | collective-permute-done | bytes 32800 | tf_op jit(solution)/shard_map/ppermute | solution.py:589
  43.9 0.0 collective-permute-done.2.ns_a_in
  43.9 0.0 collective-permute-done.3.ns_b_in
  43.9 1.0 %fix.1 = (f32[2,64,128]{2,1,0:T(8,128)S(1)}, f32[50,384]{1,0:T(8,128)S(1)}, f32[50,384]{1,0:T(8,128)S(1)}) custom-call(s32[384]{0:T(512)} %fold_ref.1, f32[64,128]{1,0:T(8,128)S(1)} %get-tuple-element.20.ew_a, f32[64,128]{1,0:T(8,128)S(1)} %get-tuple-element.21.ew_b, f32[80,384]{1,0:T(8,128)S(1)} %get-tuple-element.22.ns_a, ...), custom_call_target="tpu_custom_call" | custom-call | tf_op jit(solution)/shard_map/fix/pallas_call | solution.py:360
  44.9 0.0 all-to-all-done
  44.9 12.2 %final.1 = f32[2,25,64,384]{3,2,1,0:T(8,128)} custom-call(s32[4096]{0:T(1024)S(1)} %bitcast.5, s32[8,128]{1,0:T(8,128)S(1)} %get-tuple-element.17.start_ref, f32[2048,128]{1,0:T(8,128)S(1)} %bitcast.4, f32[4096,128]{1,0:T(8,128)S(1)} %get-tuple-element.18.mark_ref, f32[2,25,64,384]{3,2,1,0:T(8,128)} %get-tuple-element.19.part_hbm, s32[64,384]{1,0:T(8,128)} %wet_ref.3, ...), custom_call_target="tpu_custom_call" | custom-call | tf_op jit(solution)/shard_map/final/pallas_call | solution.py:569
Async XLA Ops:
  3.9 41.0 %all-to-all-start = ((f32[128,16,128]{2,1,0:T(8,128)}), f32[128,16,128]{2,1,0:T(8,128)S(1)}, u32[]{:S(2)}, u32[]{:S(2)}) async-start(f32[128,16,128]{2,1,0:T(8,128)} %melt.1), calls=%async_computation | async-start | bytes 2097152 | tf_op jit(solution)/shard_map/all_to_all | solution.py:599
  31.0 12.9 %collective-permute-start.2 = (f32[80,384]{1,0:T(8,128)S(1)}, f32[80,384]{1,0:T(8,128)S(1)}, u32[]{:S(2)}, u32[]{:S(2)}) collective-permute-start(f32[80,384]{1,0:T(8,128)S(1)} %get-tuple-element.22.ns_a), channel_id=1, source_target_pairs={{1,2},{3,4},{5,6},{9,10},{11,12},{13,14},{17,18},{19,20},{21,22},{... | collective-permute-start | bytes 368648 | tf_op jit(solution)/shard_map/ppermute | solution.py:589
  35.6 8.2 %collective-permute-start.3 = (f32[80,384]{1,0:T(8,128)S(1)}, f32[80,384]{1,0:T(8,128)S(1)}, u32[]{:S(2)}, u32[]{:S(2)}) collective-permute-start(f32[80,384]{1,0:T(8,128)S(1)} %get-tuple-element.23.ns_b), channel_id=1, source_target_pairs={{0,1},{2,3},{4,5},{6,7},{1,0},{3,2},{5,4},{7,6},{8,9},{10,11},{12,... | collective-permute-start | bytes 368648 | tf_op jit(solution)/shard_map/ppermute | solution.py:589
  35.9 6.5 %collective-permute-start = (f32[64,128]{1,0:T(8,128)S(1)}, f32[64,128]{1,0:T(8,128)S(1)}, u32[]{:S(2)}, u32[]{:S(2)}) collective-permute-start(f32[64,128]{1,0:T(8,128)S(1)} %get-tuple-element.20.ew_a), channel_id=1, source_target_pairs={{0,8},{16,24},{32,40},{48,56},{64,72},{80,88},{96,104},{112,120},{... | collective-permute-start | bytes 98312 | tf_op jit(solution)/shard_map/ppermute | solution.py:589
  35.9 7.9 %collective-permute-start.1 = (f32[64,128]{1,0:T(8,128)S(1)}, f32[64,128]{1,0:T(8,128)S(1)}, u32[]{:S(2)}, u32[]{:S(2)}) collective-permute-start(f32[64,128]{1,0:T(8,128)S(1)} %get-tuple-element.21.ew_b), channel_id=1, source_target_pairs={{8,16},{24,32},{40,48},{56,64},{72,80},{88,96},{104,112},{120,0},{... | collective-permute-start | bytes 98312 | tf_op jit(solution)/shard_map/ppermute | solution.py:589

commit v5 on v4

--- a/solution.py
+++ b/solution.py
@@ -19,14 +19,14 @@
 ANY_SPEC = pl.BlockSpec(memory_space=pl.ANY)
 LIMIT = 12 << 20
 
-TR_LANES = 32
-HALF = 64
-WET_LANE = 127
+EAST_WET = 126
+WEST_WET = 127
 MELT_STEPS = 4
-FIRSTS = (0, 1, 5, 13)
+FIRSTS = (0, 1, 4, 9, 16)
+SENDS = (6, 12, 18, 22, 24)
 PARTS = (0, 2)
 WINDOW = 128
-CELL_LANE = 25
+CELL_LANE = 100
 
 
 def in_hbm(*values):
@@ -47,8 +47,11 @@
     return lax.dot_general(a, b, (((1,), (0,)), ((), ())), preferred_element_type=F32)
 
 
-def melt_kernel(count_ref, berg_hbm, map_ref, out_hbm, berg_v, out_v, weight_ref, sem_i, sem_o):
-    maps = map_ref.shape[0]
+def melt_kernel(
+    count_hbm, berg_hbm, map_hbm, out_hbm,
+    berg_v, out_v, weight_ref, map_v, count_ref, sem_i, sem_o, sem_s,
+):
+    maps = map_v.shape[0]
     width = berg_v.shape[1]
     owners, pairs = out_v.shape[:2]
     steps = MELT_STEPS
@@ -63,19 +66,23 @@
         span = pl.ds(i * per, per)
         return pltpu.make_async_copy(out_v.at[span], out_hbm.at[span], sem_o)
 
+    small = (
+        pltpu.make_async_copy(map_hbm, map_v, sem_s.at[0]),
+        pltpu.make_async_copy(count_hbm, count_ref, sem_s.at[1]),
+    )
+    for copy in small:
+        copy.start()
     for i in range(steps):
         load(i).start()
+    for copy in small:
+        copy.wait()
     weight_ref[...] = jnp.zeros_like(weight_ref)
     for h in range(2):
-        for t in range(2):
-            place = h * HALF + t * TR_LANES
-            weight_ref[place : place + maps // 2, h * width : (h + 1) * width] = map_ref[
-                t * (maps // 2) : (t + 1) * (maps // 2), :
-            ]
-    w_high, w_low = split(weight_ref[...])
+        weight_ref[h, pl.ds(h, maps, stride=2), :] = map_v[...]
+    w_high, w_low = split(jnp.concatenate([weight_ref[0], weight_ref[1]], axis=1))
     w_both = jnp.concatenate([w_high, w_low], axis=0)
     lane = lax.broadcasted_iota(jnp.int32, (pairs, 128), 1)
-    slot = lax.broadcasted_iota(jnp.int32, (pairs, 128), 0) + jnp.where(lane >= HALF, pairs, 0)
+    slot = lax.broadcasted_iota(jnp.int32, (pairs, 128), 0) + pairs * jnp.bitwise_and(lane, 1)
     for i in range(steps):
         load(i).wait()
         slots = berg_v[i * 2 * rows : (i + 1) * 2 * rows, :].reshape(per, 2, pairs, width)
@@ -99,14 +106,17 @@
     return pl.pallas_call(
         melt_kernel,
         out_shape=jax.ShapeDtypeStruct((owners, pairs, 128), F32),
-        in_specs=[SMEM_SPEC, ANY_SPEC, VMEM_SPEC],
+        in_specs=[ANY_SPEC] * 3,
         out_specs=ANY_SPEC,
         scratch_shapes=[
             VM(bergs.shape, F32),
             VM((owners, pairs, 128), F32),
-            VM((128, 2 * width), F32),
+            VM((2, 128, width), F32),
+            VM(melt_map.shape[::-1], F32),
+            pltpu.SMEM((owners,), jnp.int32),
             dma,
             pltpu.SemaphoreType.DMA,
+            pltpu.SemaphoreType.DMA((2,)),
         ],
         compiler_params=pltpu.CompilerParams(vmem_limit_bytes=LIMIT),
         name="melt",
@@ -114,15 +124,16 @@
 
 
 def stencil_kernel(
-    tr_hbm, ea_hbm, no_hbm, wet_ref,
-    part_hbm, ew_a, ew_b, ns_a, ns_b,
-    tv, ev, nv, ov, faces, wetf, packs, sem_t, sem_e, sem_n, sem_o,
+    tr_hbm, ea_hbm, no_hbm, wet_hbm,
+    part_hbm, ew, ns_a, ns_b,
+    tv, ev, nv, ov, faces, wetf, wet_v, sem_t, sem_e, sem_n, sem_o, sem_w,
 ):
     levels, rows, cols = ea_hbm.shape
     strips = rows // 8
 
     firsts = FIRSTS
     lasts = firsts[1:] + (levels,)
+    sent = (0,) + SENDS + (levels,)
 
     def copies(c):
         span = pl.ds(firsts[c], lasts[c] - firsts[c])
@@ -133,18 +144,20 @@
         )
 
     def result(c):
-        span = pl.ds(firsts[c], lasts[c] - firsts[c])
+        span = pl.ds(sent[c], sent[c + 1] - sent[c])
         return pltpu.make_async_copy(ov.at[:, span], part_hbm.at[:, span], sem_o)
 
+    mask_copy = pltpu.make_async_copy(wet_hbm, wet_v, sem_w)
+    mask_copy.start()
     for c in range(len(firsts)):
         for copy in copies(c):
             copy.start()
-    odd_lon = lax.rem(lax.axis_index("lon"), 2)
+    mask_copy.wait()
     odd_lat = lax.rem(lax.axis_index("lat"), 2)
     row_a = odd_lat * (rows - 1)
     row_b = (1 - odd_lat) * (rows - 1)
 
-    wet = wet_ref[...].astype(F32)
+    wet = wet_v[...].astype(F32)
     wetf[...] = wet
     col = lax.broadcasted_iota(jnp.int32, (rows, cols), 1)
     row = lax.broadcasted_iota(jnp.int32, (rows, cols), 0)
@@ -164,8 +177,6 @@
 
     lane = lax.broadcasted_iota(jnp.int32, (8, 128), 1)
     top = lax.broadcasted_iota(jnp.int32, (8, cols), 0) == 0
-    last_lane = lane == 127
-    packs[...] = jnp.zeros_like(packs)
 
     bottom = lax.broadcasted_iota(jnp.int32, (8, cols), 0) == 7
 
@@ -200,13 +211,11 @@
             d_e = faces[1, here, :]
             d_n = faces[3, here, :]
             a_e, b_e, a_n, b_n = s_e + d_e, s_e - d_e, s_n + d_n, s_n - d_n
-            ends = [None, None, (u_next, u)]
             for t in range(2):
                 q = own[t]
                 up = tv[t, above, here, :]
                 dn = tv[t, below, here, :]
                 q_next = pltpu.roll(q, cols - 1, 1)
-                ends[t] = (q_next, q)
                 fe = q * a_e + q_next * b_e
                 fn = q * a_n + north[t] * b_n
                 fw = pltpu.roll(fe, 1, 1)
@@ -216,20 +225,14 @@
                 carried[t] = turned
                 mix = (1 - 2 * diffuse_v * time_step) * q + (diffuse_v * time_step) * (up + dn)
                 ov[t, k, here, :] = w * ((mix - (fe - fw)) - (fn - fs))
-            for at in range(3):
-                for side in range(2):
-                    end = ends[at][side][:, cols - 128 :]
-                    packs[at, side, here, :] = jnp.where(
-                        last_lane, end, pltpu.roll(packs[at, side, here, :], 127, 1)
-                    )
             own, risen = later, later_risen
         for ref, at in ((ns_a, row_a), (ns_b, row_b)):
             ref[pl.ds(k, 1), :] = tv[0, k, pl.ds(at, 1), :]
             ref[pl.ds(levels + k, 1), :] = tv[1, k, pl.ds(at, 1), :]
             ref[pl.ds(2 * levels + k, 1), :] = nv[k, pl.ds(at, 1), :]
-        for c in range(len(firsts)):
-
-            @pl.when(k == lasts[c] - 1)
+        for c in range(len(sent) - 1):
+
+            @pl.when(k == sent[c + 1] - 1)
             def _send(c=c):
                 result(c).start()
 
@@ -237,17 +240,34 @@
 
     lax.fori_loop(0, levels, level, 0)
 
-    def packed(side, mask):
-        value = jnp.where(lane_all == WET_LANE, mask, 0.0)
-        for at, place in ((0, 0), (1, TR_LANES), (2, HALF), (2, HALF + TR_LANES)):
-            here = (lane_all >= place) & (lane_all < place + levels)
-            value = jnp.where(here, pltpu.roll(packs[at, side], levels + place, 1), value)
-        return value
-
-    is_odd = odd_lon == 1
-    west, east = packed(0, wetf[:, 0:1]), packed(1, wetf[:, cols - 1 : cols])
-    ew_a[...] = jnp.where(is_odd, west, east)
-    ew_b[...] = jnp.where(is_odd, east, west)
+    west_lanes = lane < 64
+    ends = (lane == 0) | (lane == 127)
+
+    def inserted(packs, field):
+        made = []
+        for s, pack in enumerate(packs):
+            here = pl.ds(8 * s, 8)
+            both = jnp.where(west_lanes, field[here, 0:128], field[here, cols - 128 : cols])
+            made.append(jnp.where(ends, both, pltpu.roll(pack, 2, 1)))
+        return tuple(made)
+
+    def second(i, packs):
+        return inserted(packs, tv.at[1, levels - 1 - i])
+
+    def first(i, packs):
+        k = levels - 1 - i
+        return inserted(packs[0], tv.at[0, k]), inserted(packs[1], ev.at[k])
+
+    blank = (jnp.zeros((8, 128), F32),) * strips
+    fields = lax.fori_loop(0, levels, second, blank)
+    fields, speeds = lax.fori_loop(0, levels, first, (fields, blank))
+    fields = pltpu.roll(jnp.concatenate(fields, axis=0), 1, 1)
+    fields = jnp.where(lane_all == EAST_WET, wetf[:, cols - 1 : cols], fields)
+    ew[:, 0:128] = jnp.where(lane_all == WEST_WET, wetf[:, 0:1], fields)
+    speeds = jnp.concatenate(speeds, axis=0)
+    ew[:, 128:256] = jnp.where(
+        lane_all < 2 * levels, pltpu.roll(speeds, 1, 1), pltpu.roll(speeds, 2 * levels + 1, 1)
+    )
     pltpu.make_async_copy(ov, part_hbm, sem_o).wait()
 
 
@@ -259,13 +279,12 @@
         stencil_kernel,
         out_shape=(
             pltpu.HBM(tracers.shape, F32),
-            jax.ShapeDtypeStruct((rows, 128), F32),
-            jax.ShapeDtypeStruct((rows, 128), F32),
+            jax.ShapeDtypeStruct((rows, 256), F32),
             jax.ShapeDtypeStruct((edge_rows, cols), F32),
             jax.ShapeDtypeStruct((edge_rows, cols), F32),
         ),
-        in_specs=[ANY_SPEC] * 3 + [VMEM_SPEC],
-        out_specs=(ANY_SPEC,) + (VMEM_SPEC,) * 4,
+        in_specs=[ANY_SPEC] * 4,
+        out_specs=(ANY_SPEC,) + (VMEM_SPEC,) * 3,
         scratch_shapes=[
             VM(tracers.shape, F32),
             VM(east_speed.shape, F32),
@@ -273,10 +292,11 @@
             VM(tracers.shape, F32),
             VM((4, rows, cols), F32),
             VM((rows, cols), F32),
-            VM((3, 2, rows, 128), F32),
+            VM((rows, cols), jnp.int32),
             dma,
             dma,
             dma,
+            pltpu.SemaphoreType.DMA,
             pltpu.SemaphoreType.DMA,
         ],
         compiler_params=pltpu.CompilerParams(vmem_limit_bytes=20 << 20),
@@ -285,7 +305,7 @@
 
 
 def fix_kernel(
-    fold_ref, ew_a, ew_b, ns_a, ns_b, ew_a_in, ew_b_in, ns_a_in, ns_b_in,
+    fold_ref, ew, ns_a, ns_b, ew_a_in, ew_b_in, ns_a_in, ns_b_in,
     fix_c, fix_n, fix_s, north, south,
 ):
     levels = fix_n.shape[0] // 2
@@ -304,23 +324,31 @@
     def pick(odd, a, b):
         return jnp.where(odd, a, b)
 
-    def column(value):
-        return value, pltpu.roll(value, HALF, 1), value[:, WET_LANE : WET_LANE + 1]
-
-    east_own = column(pick(odd_lon, ew_b[...], ew_a[...]))
-    west_own = column(pick(odd_lon, ew_a[...], ew_b[...]))
-    east_far = column(pick(odd_lon, ew_b_in[...], ew_a_in[...]))
-    west_far = column(pick(odd_lon, ew_a_in[...], ew_b_in[...]))
-    lane = lax.broadcasted_iota(jnp.int32, ew_a.shape, 1)
-    first = lax.broadcasted_iota(jnp.int32, ew_a.shape, 0) * cols
+    def column(value, turn, mask):
+        field, speed = value[:, 0:128], value[:, 128:256]
+        if turn:
+            field, speed = pltpu.roll(field, turn, 1), pltpu.roll(speed, turn, 1)
+        return field, speed, value[:, mask : mask + 1]
+
+    own, far_a, far_b = ew[...], ew_a_in[...], ew_b_in[...]
+    east_own = column(own, 0, EAST_WET)
+    west_own = column(own, 0, WEST_WET)
+    east_far = column(pick(odd_lon, far_b, far_a), 127, WEST_WET)
+    west_far = column(pick(odd_lon, far_a, far_b), 1, EAST_WET)
+    lane = lax.broadcasted_iota(jnp.int32, (own.shape[0], 128), 1)
+    even = jnp.bitwise_and(lane, 1) == 0
+    first = lax.broadcasted_iota(jnp.int32, lane.shape, 0) * cols
     for at, value, cell in (
         (0, -(east_own[2] * faces(*east_own, *east_far)), first + (cols - 1)),
         (1, west_own[2] * faces(*west_far, *west_own), first),
     ):
         high = value.astype(BF16).astype(F32)
-        body = jnp.where(lane < HALF, high, pltpu.roll(value - high, HALF, 1))
+        low = value - high
+        if at:
+            body = jnp.where(even, pltpu.roll(high, 127, 1), low)
+        else:
+            body = jnp.where(even, high, pltpu.roll(low, 1, 1))
         fix_c[at] = jnp.where(lane == CELL_LANE, cell.astype(F32), body)
-
 
     north[...] = pick(odd_lat, ns_a_in[...], ns_b_in[...])
     south[...] = pick(odd_lat, ns_b_in[...], ns_a_in[...])
@@ -356,7 +384,7 @@
 
 
 def fixes(fold_partner, own, far, levels):
-    rows, cols = own[0].shape[0], own[2].shape[1]
+    rows, cols = own[0].shape[0], own[1].shape[1]
     return pl.pallas_call(
         fix_kernel,
         out_shape=(
@@ -364,9 +392,9 @@
             jax.ShapeDtypeStruct((2 * levels, cols), F32),
             jax.ShapeDtypeStruct((2 * levels, cols), F32),
         ),
-        in_specs=[VMEM_SPEC] * 9,
+        in_specs=[VMEM_SPEC] * 8,
         out_specs=(VMEM_SPEC,) * 3,
-        scratch_shapes=[VM(own[2].shape, F32), VM(own[2].shape, F32)],
+        scratch_shapes=[VM(own[1].shape, F32), VM(own[1].shape, F32)],
         compiler_params=pltpu.CompilerParams(vmem_limit_bytes=LIMIT),
         name="fix",
     )(*in_hbm(fold_partner), *own, *far)
@@ -434,9 +462,9 @@
 
 
 def final_kernel(
-    place_ref, start_ref, recv_ref, mark_ref, part_hbm, wet_ref, fix_c, fix_n, fix_s,
+    place_in, start_in, recv_ref, mark_ref, part_hbm, wet_hbm, fix_c, fix_n, fix_s,
     out_hbm,
-    rows_v, sorted_v, pv, wetf, acc, sem_i, sem_o, *, pairs,
+    rows_v, sorted_v, pv, wet_v, wetf, acc, place_ref, start_ref, sem_i, sem_o, sem_s, *, pairs,
 ):
     _, levels, rows, cols = pv.shape
     groups = rows // 8
@@ -453,10 +481,17 @@
         here = pl.ds(pl.multiple_of(8 * g, 8), 8)
         return pltpu.make_async_copy(pv.at[:, :, here], out_hbm.at[:, :, here], sem_o)
 
+    small = (
+        pltpu.make_async_copy(place_in, place_ref, sem_s.at[0]),
+        pltpu.make_async_copy(start_in, start_ref, sem_s.at[1]),
+        pltpu.make_async_copy(wet_hbm, wet_v, sem_s.at[2]),
+    )
+    for copy in small:
+        copy.start()
     for i in range(len(PARTS)):
         load(i).start()
     lane_all = lax.broadcasted_iota(jnp.int32, (128, 128), 1)
-    low_half = lane_all < HALF
+    even = jnp.bitwise_and(lane_all, 1) == 0
     cell_lane = lane_all == CELL_LANE
 
     def halves(i, _):
@@ -466,8 +501,8 @@
         low = both - high
         for h, body in enumerate(
             (
-                jnp.where(low_half, high, pltpu.roll(low, HALF, 1)),
-                jnp.where(low_half, pltpu.roll(high, HALF, 1), low),
+                jnp.where(even, high, pltpu.roll(low, 1, 1)),
+                jnp.where(even, pltpu.roll(high, 127, 1), low),
             )
         ):
             there = pl.ds(pl.multiple_of(h * n_rows + at, 128), 128)
@@ -475,19 +510,20 @@
         return _
 
     lax.fori_loop(0, n_rows // 128, halves, 0)
-    wetf[...] = wet_ref[...].astype(F32)
+    for copy in small:
+        copy.wait()
+    wetf[...] = wet_v[...].astype(F32)
     sorted_v[count:, :] = jnp.full((WINDOW, 128), -1.0, F32)
 
     def spread(i, _):
-        first = pl.multiple_of(i * pairs, pairs)
-        places = place_ref.at[pl.ds(2 * first, 2 * pairs)]
-        for j in range(pairs):
-            for h in range(2):
-                to = places[h * pairs + j]
-                sorted_v[pl.ds(to, 1), :] = rows_v[pl.ds(h * n_rows + first + j, 1), :]
+        first = pl.multiple_of(i * 64, 64)
+        for j in range(128):
+            source, h, pair = j // (2 * pairs), j // pairs % 2, j % pairs
+            line = rows_v[pl.ds(h * n_rows + first + source * pairs + pair, 1), :]
+            sorted_v[pl.ds(place_ref[i, j], 1), :] = line
         return _
 
-    lax.fori_loop(0, n_rows // pairs, spread, 0)
+    lax.fori_loop(0, place_ref.shape[0], spread, 0)
     for r in range(rows):
         first = start_ref[0, r]
         for h in range(2):
@@ -501,8 +537,7 @@
         lhs = lines.astype(BF16).T
         near = jnp.broadcast_to(lines[:, CELL_LANE : CELL_LANE + 1], (WINDOW, 128)) - (r * cols).astype(F32)
         hot = [jnp.where(near - float(128 * c) == lanef, 1.0, 0.0).astype(BF16) for c in range(tiles)]
-        both = dot_nn(lhs, jnp.concatenate(hot, axis=1))
-        return both[:HALF] + both[HALF:]
+        return dot_nn(lhs, jnp.concatenate(hot, axis=1))
 
     def group(g, _):
         here = pl.ds(pl.multiple_of(8 * g, 8), 8)
@@ -516,7 +551,7 @@
         for j in range(8):
             made = row_sources(8 * g + j, firsts[j])
             for c in range(tiles):
-                for m in range(0, HALF, 8):
+                for m in range(0, 2 * maps, 8):
                     acc[c, pl.ds(m * 9 + j, 8, stride=9), :] = made[m : m + 8, c * 128 : (c + 1) * 128]
         most = functools.reduce(jnp.maximum, windows)
 
@@ -527,7 +562,7 @@
                 def again(i, _, j=j):
                     made = row_sources(8 * g + j, firsts[j] + i * WINDOW)
                     for c in range(tiles):
-                        for m in range(0, HALF, 8):
+                        for m in range(0, 2 * maps, 8):
                             acc[c, pl.ds(m * 9 + j, 8, stride=9), :] += made[
                                 m : m + 8, c * 128 : (c + 1) * 128
                             ]
@@ -553,10 +588,10 @@
 
         for m in range(maps):
             t, k = m // levels, m % levels
-            at = 9 * (t * TR_LANES + k)
+            at = 18 * m
             for c in range(tiles):
                 lanes = slice(c * 128, (c + 1) * 128)
-                pv[t, k, here, lanes] += w[:, lanes] * acc[c, at : at + 8, :]
+                pv[t, k, here, lanes] += w[:, lanes] * (acc[c, at : at + 8, :] + acc[c, at + 9 : at + 17, :])
         store(g).start()
         return _
 
@@ -569,16 +604,20 @@
     return pl.pallas_call(
         functools.partial(final_kernel, pairs=pairs),
         out_shape=jax.ShapeDtypeStruct(part.shape, F32),
-        in_specs=[SMEM_SPEC] * 2 + [VMEM_SPEC] * 2 + [ANY_SPEC] + [VMEM_SPEC] * 4,
+        in_specs=[VMEM_SPEC] * 4 + [ANY_SPEC] * 2 + [VMEM_SPEC] * 3,
         out_specs=ANY_SPEC,
         scratch_shapes=[
             VM((2 * recv.shape[0], 128), F32),
             VM((2 * recv.shape[0] + 2 * rows + WINDOW, 128), F32),
             VM(part.shape, F32),
+            VM((rows, cols), jnp.int32),
             VM((rows, cols), F32),
-            VM((cols // 128, 9 * HALF, 128), F32),
+            VM((cols // 128, 9 * 128, 128), F32),
+            pltpu.SMEM(place.shape, jnp.int32),
+            pltpu.SMEM(start.shape, jnp.int32),
             pltpu.SemaphoreType.DMA((len(PARTS),)),
             pltpu.SemaphoreType.DMA,
+            pltpu.SemaphoreType.DMA((3,)),
         ],
         compiler_params=pltpu.CompilerParams(vmem_limit_bytes=24 << 20),
         name="final",
@@ -598,7 +637,7 @@
     melt = melt_rows(bergs, berg_count, melt_map)
     recv = lax.all_to_all(melt, ("lon", "lat"), split_axis=0, concat_axis=0, tiled=True)
     part, *own = stencil(tracers, east_speed, north_speed, wet)
-    ew_a, ew_b, ns_a, ns_b = own
+    ew, ns_a, ns_b = own
 
     lon_even = [(i, i + 1) for i in range(0, lon_count, 2)]
     lon_odd = [(i, (i + 1) % lon_count) for i in range(1, lon_count, 2)]
@@ -613,8 +652,8 @@
     ]
     lat_even = [(j, j + 1) for j in range(0, lat_count, 2)]
     far = (
-        swap(ew_a, "lon", lon_even),
-        swap(ew_b, "lon", lon_odd),
+        swap(ew, "lon", lon_even),
+        swap(ew, "lon", lon_odd),
         swap(ns_a, ("lon", "lat"), lat_odd),
         swap(ns_b, "lat", lat_even),
     )
@@ -622,7 +661,7 @@
     pairs = melt.shape[1]
     spots, start, mark = order(berg_cell, tracers.shape[2], cols, pairs)
     recv = recv.reshape(-1, 128)
-    return finish(spots.reshape(-1), start, recv, mark, part, wet, fix, pairs)
+    return finish(spots, start, recv, mark, part, wet, fix, pairs)
 
 
 def solution(mesh):

time: 57.5 us -> 54.4 us (0.946)
  Pallas kernels: 35.2 us -> 31.5 us
  waiting for transfers between devices: 1.43 us -> 2.77 us
  starting transfers between devices: 20.4 us -> 19.8 us
    pallas_call x1, Pallas kernels: 16.6 us -> 14.6 us  [stencil(): pl.pallas_call(stencil_kernel, out_shape=(pltpu.HBM(tracers.shape, F32),...]
    ppermute x4, waiting for transfers between devices: 1.42 us -> 2.77 us  [swap(): return lax.ppermute(value, axes, pairs + [(b, a) for a, b in pairs])]
    pallas_call x1, Pallas kernels: 12.2 us -> 11.1 us  [finish(): pl.pallas_call(functools.partial(final_kernel, pairs=pairs), out_shape=ja...]
    pallas_call x1, Pallas kernels: 3.87 us -> 3.18 us  [melt_rows(): pl.pallas_call(melt_kernel, out_shape=jax.ShapeDtypeStruct((owners, pairs...]
    ppermute x4, starting transfers between devices: 9.92 us -> 9.29 us  [swap(): return lax.ppermute(value, axes, pairs + [(b, a) for a, b in pairs])]
  transfers between devices with their start and end apart: 5 -> 5, of which waited for: 1 -> 1; matrix products, arithmetic and copies ran while one was open for 0% -> 0% of each run, Pallas kernels for 33% -> 32%
where the time goes in v5:
time: 54.4 us; the launch traced here: 54.1 us
  Pallas kernels  31.5 us (58%)
  starting transfers between devices  19.8 us (36%)
  waiting for transfers between devices  2.77 us (5%)
    pallas_call x1, Pallas kernels, stencil(): pl.pallas_call(stencil_kernel, out_shape=(pltpu.HBM(tracers.shape, F32),...  14.6 us
    pallas_call x1, Pallas kernels, finish(): pl.pallas_call(functools.partial(final_kernel, pairs=pairs), out_shape=ja...  11.1 us
    all_to_all x1, starting transfers between devices, shards(): lax.all_to_all(melt, ('lon', 'lat'), split_axis=0, concat_axis=0, tiled=T...  10.5 us
    ppermute x4, starting transfers between devices, swap(): return lax.ppermute(value, axes, pairs + [(b, a) for a, b in pairs])  9.29 us
    pallas_call x1, Pallas kernels, melt_rows(): pl.pallas_call(melt_kernel, out_shape=jax.ShapeDtypeStruct((owners, pairs...  3.18 us
    ppermute x4, waiting for transfers between devices, swap(): return lax.ppermute(value, axes, pairs + [(b, a) for a, b in pairs])  2.77 us
    pallas_call x1, Pallas kernels, order(): pl.pallas_call(functools.partial(order_kernel, rows=rows, cols=cols, pair...  1.52 us
  transfers between devices with their start and end apart: 5, of which 1 were waited for; matrix products, arithmetic and copies ran while one was open for 0% of the time, Pallas kernels for 32%

profile of v5, /device:TPU:4, one launch (start us, length us, event | category | flops | bytes accessed | tf_op | source)
XLA Modules:
  0.0 54.1 jit_solution(16302585070175154571)
XLA Ops:
  0.0 3.2 %melt.1 = f32[128,16,128]{2,1,0:T(8,128)} custom-call(s32[128]{0:T(128)} %count_hbm.1, f32[4096,128]{1,0:T(8,128)} %berg_hbm.1, f32[50,128]{1,0:T(8,128)} %bitcast.4), custom_call_target="tpu_custom_call" | custom-call | tf_op jit(solution)/shard_map/melt/pallas_call | solution.py:106
  3.2 10.5 %all-to-all-start = ((f32[128,16,128]{2,1,0:T(8,128)}), f32[128,16,128]{2,1,0:T(8,128)S(1)}, u32[]{:S(2)}, u32[]{:S(2)}) async-start(f32[128,16,128]{2,1,0:T(8,128)} %melt.1), calls=%async_computation | async-start | bytes 2097152 | tf_op jit(solution)/shard_map/all_to_all | solution.py:638
  13.7 14.6 %stencil.1 = (f32[2,25,64,384]{3,2,1,0:T(8,128)}, f32[64,256]{1,0:T(8,128)S(1)}, f32[80,384]{1,0:T(8,128)S(1)}, f32[80,384]{1,0:T(8,128)S(1)}) custom-call(f32[2,25,64,384]{3,2,1,0:T(8,128)} %tr_hbm.1, f32[25,64,384]{2,1,0:T(8,128)} %ea_hbm.1, f32[25,64,384]{2,1,0:T(8,128)} %no_hbm.1, s32[64,384]{1,0:T(8,128)} %wet_hbm.3), custom_call_target="tpu_custom_call" | custom-call | tf_op jit(solution)/shard_map/stencil/pallas_call | solution.py:278
  28.3 4.6 %collective-permute-start.2 = (f32[80,384]{1,0:T(8,128)S(1)}, f32[80,384]{1,0:T(8,128)S(1)}, u32[]{:S(2)}, u32[]{:S(2)}) collective-permute-start(f32[80,384]{1,0:T(8,128)S(1)} %get-tuple-element.20.ns_a), channel_id=1, source_target_pairs={{1,2},{3,4},{5,6},{9,10},{11,12},{13,14},{17,18},{19,20},{21,22},{... | collective-permute-start | bytes 368648 | tf_op jit(solution)/shard_map/ppermute | solution.py:628
  32.9 0.3 collective-permute-start.3
  33.2 4.4 %collective-permute-start.1 = (f32[64,256]{1,0:T(8,128)S(1)}, f32[64,256]{1,0:T(8,128)S(1)}, u32[]{:S(2)}, u32[]{:S(2)}) collective-permute-start(f32[64,256]{1,0:T(8,128)S(1)} %get-tuple-element.19.ew), channel_id=1, source_target_pairs={{8,16},{24,32},{40,48},{56,64},{72,80},{88,96},{104,112},{120,0},{... | collective-permute-start | bytes 196616 | tf_op jit(solution)/shard_map/ppermute | solution.py:628
  37.6 0.0 collective-permute-start
  37.6 1.5 %order.1 = (s32[32,128]{1,0:T(8,128)S(1)}, s32[8,128]{1,0:T(8,128)S(1)}, f32[4096,128]{1,0:T(8,128)S(1)}) custom-call(s32[32,128]{1,0:T(8,128)} %bitcast.5), custom_call_target="tpu_custom_call" | custom-call | tf_op jit(solution)/shard_map/order/pallas_call | solution.py:449
  39.1 2.8 %collective-permute-done.1.ew_b_in = f32[64,256]{1,0:T(8,128)S(1)} collective-permute-done((f32[64,256]{1,0:T(8,128)S(1)}, f32[64,256]{1,0:T(8,128)S(1)}, u32[]{:S(2)}, u32[]{:S(2)}) %collective-permute-start.1) | collective-permute-done | bytes 65568 | tf_op jit(solution)/shard_map/ppermute | solution.py:628
  41.8 0.0 collective-permute-done.ew_a_in
  41.8 0.0 collective-permute-done.2.ns_a_in
  41.9 0.0 collective-permute-done.3.ns_b_in
  41.9 1.1 %fix.1 = (f32[2,64,128]{2,1,0:T(8,128)S(1)}, f32[50,384]{1,0:T(8,128)S(1)}, f32[50,384]{1,0:T(8,128)S(1)}) custom-call(s32[384]{0:T(512)} %fold_ref.1, f32[64,256]{1,0:T(8,128)S(1)} %get-tuple-element.19.ew, f32[80,384]{1,0:T(8,128)S(1)} %get-tuple-element.20.ns_a, f32[80,384]{1,0:T(8,128)S(1)} %get-tuple-element.21.ns_b, ...), custom_call_target="tpu_custom_call" | custom-call | tf_op jit(solution)/shard_map/fix/pallas_call | solution.py:388
  43.0 0.0 all-to-all-done
  43.0 11.1 %final.1 = f32[2,25,64,384]{3,2,1,0:T(8,128)} custom-call(s32[32,128]{1,0:T(8,128)S(1)} %get-tuple-element.15.place_in, s32[8,128]{1,0:T(8,128)S(1)} %get-tuple-element.16.start_in, f32[2048,128]{1,0:T(8,128)S(1)} %bitcast.3, f32[4096,128]{1,0:T(8,128)S(1)} %get-tuple-element.17.mark_ref, f32[2,25,64,384]{3,2,1,0:T(8,128)} %get-tuple-element.18.part_hbm, ...), custom_call_target="tpu_custom_call" | custom-call | tf_op jit(solution)/shard_map/final/pallas_call | solution.py:604
Async XLA Ops:
  3.2 39.8 %all-to-all-start = ((f32[128,16,128]{2,1,0:T(8,128)}), f32[128,16,128]{2,1,0:T(8,128)S(1)}, u32[]{:S(2)}, u32[]{:S(2)}) async-start(f32[128,16,128]{2,1,0:T(8,128)} %melt.1), calls=%async_computation | async-start | bytes 2097152 | tf_op jit(solution)/shard_map/all_to_all | solution.py:638
  28.3 13.6 %collective-permute-start.2 = (f32[80,384]{1,0:T(8,128)S(1)}, f32[80,384]{1,0:T(8,128)S(1)}, u32[]{:S(2)}, u32[]{:S(2)}) collective-permute-start(f32[80,384]{1,0:T(8,128)S(1)} %get-tuple-element.20.ns_a), channel_id=1, source_target_pairs={{1,2},{3,4},{5,6},{9,10},{11,12},{13,14},{17,18},{19,20},{21,22},{... | collective-permute-start | bytes 368648 | tf_op jit(solution)/shard_map/ppermute | solution.py:628
  32.9 8.9 %collective-permute-start.3 = (f32[80,384]{1,0:T(8,128)S(1)}, f32[80,384]{1,0:T(8,128)S(1)}, u32[]{:S(2)}, u32[]{:S(2)}) collective-permute-start(f32[80,384]{1,0:T(8,128)S(1)} %get-tuple-element.21.ns_b), channel_id=1, source_target_pairs={{0,1},{2,3},{4,5},{6,7},{1,0},{3,2},{5,4},{7,6},{8,9},{10,11},{12,... | collective-permute-start | bytes 368648 | tf_op jit(solution)/shard_map/ppermute | solution.py:628
  33.2 8.6 %collective-permute-start.1 = (f32[64,256]{1,0:T(8,128)S(1)}, f32[64,256]{1,0:T(8,128)S(1)}, u32[]{:S(2)}, u32[]{:S(2)}) collective-permute-start(f32[64,256]{1,0:T(8,128)S(1)} %get-tuple-element.19.ew), channel_id=1, source_target_pairs={{8,16},{24,32},{40,48},{56,64},{72,80},{88,96},{104,112},{120,0},{... | collective-permute-start | bytes 196616 | tf_op jit(solution)/shard_map/ppermute | solution.py:628
  37.6 4.3 %collective-permute-start = (f32[64,256]{1,0:T(8,128)S(1)}, f32[64,256]{1,0:T(8,128)S(1)}, u32[]{:S(2)}, u32[]{:S(2)}) collective-permute-start(f32[64,256]{1,0:T(8,128)S(1)} %get-tuple-element.19.ew), channel_id=1, source_target_pairs={{0,8},{16,24},{32,40},{48,56},{64,72},{80,88},{96,104},{112,120},{... | collective-permute-start | bytes 196616 | tf_op jit(solution)/shard_map/ppermute | solution.py:628

commit v6 on v5

--- a/solution.py
+++ b/solution.py
@@ -22,7 +22,8 @@
 EAST_WET = 126
 WEST_WET = 127
 MELT_STEPS = 4
-FIRSTS = (0, 1, 4, 9, 16)
+FIRSTS = (0, 1, 3, 6, 10, 15, 20)
+AHEAD = 3
 SENDS = (6, 12, 18, 22, 24)
 PARTS = (0, 2)
 WINDOW = 128
@@ -124,11 +125,11 @@
 
 
 def stencil_kernel(
-    tr_hbm, ea_hbm, no_hbm, wet_hbm,
+    tr_hbm, ev, no_hbm, wet_hbm,
     part_hbm, ew, ns_a, ns_b,
-    tv, ev, nv, ov, faces, wetf, wet_v, sem_t, sem_e, sem_n, sem_o, sem_w,
+    tv, nv, ov, faces, wetf, wet_v, sem_t, sem_n, sem_o, sem_w,
 ):
-    levels, rows, cols = ea_hbm.shape
+    levels, rows, cols = no_hbm.shape
     strips = rows // 8
 
     firsts = FIRSTS
@@ -139,7 +140,6 @@
         span = pl.ds(firsts[c], lasts[c] - firsts[c])
         return (
             pltpu.make_async_copy(tr_hbm.at[:, span], tv.at[:, span], sem_t.at[c]),
-            pltpu.make_async_copy(ea_hbm.at[span], ev.at[span], sem_e.at[c]),
             pltpu.make_async_copy(no_hbm.at[span], nv.at[span], sem_n.at[c]),
         )
 
@@ -149,7 +149,7 @@
 
     mask_copy = pltpu.make_async_copy(wet_hbm, wet_v, sem_w)
     mask_copy.start()
-    for c in range(len(firsts)):
+    for c in range(AHEAD):
         for copy in copies(c):
             copy.start()
     mask_copy.wait()
@@ -189,6 +189,9 @@
             def _wait(c=c):
                 for copy in copies(c):
                     copy.wait()
+                if c + AHEAD < len(firsts):
+                    for copy in copies(c + AHEAD):
+                        copy.start()
 
         carried = [None, None]
         fields = [tv.at[0, k], tv.at[1, k], nv.at[k]]
@@ -283,11 +286,10 @@
             jax.ShapeDtypeStruct((edge_rows, cols), F32),
             jax.ShapeDtypeStruct((edge_rows, cols), F32),
         ),
-        in_specs=[ANY_SPEC] * 4,
+        in_specs=[ANY_SPEC, VMEM_SPEC, ANY_SPEC, ANY_SPEC],
         out_specs=(ANY_SPEC,) + (VMEM_SPEC,) * 3,
         scratch_shapes=[
             VM(tracers.shape, F32),
-            VM(east_speed.shape, F32),
             VM(north_speed.shape, F32),
             VM(tracers.shape, F32),
             VM((4, rows, cols), F32),
@@ -295,13 +297,12 @@
             VM((rows, cols), jnp.int32),
             dma,
             dma,
-            dma,
             pltpu.SemaphoreType.DMA,
             pltpu.SemaphoreType.DMA,
         ],
         compiler_params=pltpu.CompilerParams(vmem_limit_bytes=20 << 20),
         name="stencil",
-    )(*in_hbm(tracers, east_speed, north_speed, wet))
+    )(*in_hbm(tracers), east_speed, *in_hbm(north_speed, wet))
 
 
 def fix_kernel(
@@ -515,15 +516,12 @@
     wetf[...] = wet_v[...].astype(F32)
     sorted_v[count:, :] = jnp.full((WINDOW, 128), -1.0, F32)
 
-    def spread(i, _):
-        first = pl.multiple_of(i * 64, 64)
+    for i in range(place_ref.shape[0]):
+        first = i * 64
         for j in range(128):
             source, h, pair = j // (2 * pairs), j // pairs % 2, j % pairs
             line = rows_v[pl.ds(h * n_rows + first + source * pairs + pair, 1), :]
             sorted_v[pl.ds(place_ref[i, j], 1), :] = line
-        return _
-
-    lax.fori_loop(0, place_ref.shape[0], spread, 0)
     for r in range(rows):
         first = start_ref[0, r]
         for h in range(2):

time: 54.4 us -> 52 us (0.956)
  Pallas kernels: 31.5 us -> 29 us
    pallas_call x1, Pallas kernels: 14.6 us -> 13.2 us  [stencil(): pl.pallas_call(stencil_kernel, out_shape=(pltpu.HBM(tracers.shape, F32),...]
    pallas_call x1, Pallas kernels: 11.1 us -> 9.87 us  [finish(): pl.pallas_call(functools.partial(final_kernel, pairs=pairs), out_shape=ja...]
  transfers between devices with their start and end apart: 5 -> 5, of which waited for: 1 -> 1; matrix products, arithmetic and copies ran while one was open for 0% -> 0% of each run, Pallas kernels for 32% -> 31%
where the time goes in v6:
time: 52 us; the launch traced here: 51.6 us
  Pallas kernels  29 us (56%)
  starting transfers between devices  19.8 us (38%)
  waiting for transfers between devices  2.78 us (5%)
    pallas_call x1, Pallas kernels, stencil(): pl.pallas_call(stencil_kernel, out_shape=(pltpu.HBM(tracers.shape, F32),...  13.2 us
    all_to_all x1, starting transfers between devices, shards(): lax.all_to_all(melt, ('lon', 'lat'), split_axis=0, concat_axis=0, tiled=T...  10.5 us
    pallas_call x1, Pallas kernels, finish(): pl.pallas_call(functools.partial(final_kernel, pairs=pairs), out_shape=ja...  9.87 us
    ppermute x4, starting transfers between devices, swap(): return lax.ppermute(value, axes, pairs + [(b, a) for a, b in pairs])  9.29 us
    pallas_call x1, Pallas kernels, melt_rows(): pl.pallas_call(melt_kernel, out_shape=jax.ShapeDtypeStruct((owners, pairs...  3.34 us
    ppermute x4, waiting for transfers between devices, swap(): return lax.ppermute(value, axes, pairs + [(b, a) for a, b in pairs])  2.77 us
    pallas_call x1, Pallas kernels, order(): pl.pallas_call(functools.partial(order_kernel, rows=rows, cols=cols, pair...  1.52 us
    pallas_call x1, Pallas kernels, fixes(): pl.pallas_call(fix_kernel, out_shape=(jax.ShapeDtypeStruct((2, rows, 128)...  1.09 us
  transfers between devices with their start and end apart: 5, of which 1 were waited for; matrix products, arithmetic and copies ran while one was open for 0% of the time, Pallas kernels for 31%

profile of v6, /device:TPU:4, one launch (start us, length us, event | category | flops | bytes accessed | tf_op | source)
XLA Modules:
  0.0 51.6 jit_solution(1019102135754742757)
XLA Ops:
  0.0 0.0 copy-start
  0.0 3.3 %melt.1 = f32[128,16,128]{2,1,0:T(8,128)} custom-call(s32[128]{0:T(128)} %count_hbm.1, f32[4096,128]{1,0:T(8,128)} %berg_hbm.1, f32[50,128]{1,0:T(8,128)} %bitcast.4), custom_call_target="tpu_custom_call" | custom-call | tf_op jit(solution)/shard_map/melt/pallas_call | solution.py:107
  3.3 10.5 %all-to-all-start = ((f32[128,16,128]{2,1,0:T(8,128)}), f32[128,16,128]{2,1,0:T(8,128)S(1)}, u32[]{:S(2)}, u32[]{:S(2)}) async-start(f32[128,16,128]{2,1,0:T(8,128)} %melt.1), calls=%async_computation | async-start | bytes 2097152 | tf_op jit(solution)/shard_map/all_to_all | solution.py:636
  13.9 0.0 copy-done
  13.9 13.2 %stencil.1 = (f32[2,25,64,384]{3,2,1,0:T(8,128)}, f32[64,256]{1,0:T(8,128)S(1)}, f32[80,384]{1,0:T(8,128)S(1)}, f32[80,384]{1,0:T(8,128)S(1)}) custom-call(f32[2,25,64,384]{3,2,1,0:T(8,128)} %tr_hbm.1, f32[25,64,384]{2,1,0:T(8,128)S(1)} %copy-done, f32[25,64,384]{2,1,0:T(8,128)} %no_hbm.1, s32[64,384]{1,0:T(8,128)} %wet_hbm.3), custom_call_target="tpu_custom_call" | custom-call | tf_op jit(solution)/shard_map/stencil/pallas_call | solution.py:281
  27.1 4.6 %collective-permute-start.2 = (f32[80,384]{1,0:T(8,128)S(1)}, f32[80,384]{1,0:T(8,128)S(1)}, u32[]{:S(2)}, u32[]{:S(2)}) collective-permute-start(f32[80,384]{1,0:T(8,128)S(1)} %get-tuple-element.20.ns_a), channel_id=1, source_target_pairs={{1,2},{3,4},{5,6},{9,10},{11,12},{13,14},{17,18},{19,20},{21,22},{... | collective-permute-start | bytes 368648 | tf_op jit(solution)/shard_map/ppermute | solution.py:626
  31.7 0.3 collective-permute-start.3
  32.0 4.4 %collective-permute-start.1 = (f32[64,256]{1,0:T(8,128)S(1)}, f32[64,256]{1,0:T(8,128)S(1)}, u32[]{:S(2)}, u32[]{:S(2)}) collective-permute-start(f32[64,256]{1,0:T(8,128)S(1)} %get-tuple-element.19.ew), channel_id=1, source_target_pairs={{8,16},{24,32},{40,48},{56,64},{72,80},{88,96},{104,112},{120,0},{... | collective-permute-start | bytes 196616 | tf_op jit(solution)/shard_map/ppermute | solution.py:626
  36.4 0.0 collective-permute-start
  36.4 1.5 %order.1 = (s32[32,128]{1,0:T(8,128)S(1)}, s32[8,128]{1,0:T(8,128)S(1)}, f32[4096,128]{1,0:T(8,128)S(1)}) custom-call(s32[32,128]{1,0:T(8,128)} %bitcast.5), custom_call_target="tpu_custom_call" | custom-call | tf_op jit(solution)/shard_map/order/pallas_call | solution.py:450
  37.9 2.8 %collective-permute-done.1.ew_b_in = f32[64,256]{1,0:T(8,128)S(1)} collective-permute-done((f32[64,256]{1,0:T(8,128)S(1)}, f32[64,256]{1,0:T(8,128)S(1)}, u32[]{:S(2)}, u32[]{:S(2)}) %collective-permute-start.1) | collective-permute-done | bytes 65568 | tf_op jit(solution)/shard_map/ppermute | solution.py:626
  40.6 0.0 collective-permute-done.ew_a_in
  40.7 0.0 collective-permute-done.2.ns_a_in
  40.7 0.0 collective-permute-done.3.ns_b_in
  40.7 1.1 %fix.1 = (f32[2,64,128]{2,1,0:T(8,128)S(1)}, f32[50,384]{1,0:T(8,128)S(1)}, f32[50,384]{1,0:T(8,128)S(1)}) custom-call(s32[384]{0:T(512)} %fold_ref.1, f32[64,256]{1,0:T(8,128)S(1)} %get-tuple-element.19.ew, f32[80,384]{1,0:T(8,128)S(1)} %get-tuple-element.20.ns_a, f32[80,384]{1,0:T(8,128)S(1)} %get-tuple-element.21.ns_b, ...), custom_call_target="tpu_custom_call" | custom-call | tf_op jit(solution)/shard_map/fix/pallas_call | solution.py:389
  41.8 0.0 all-to-all-done
  41.8 9.9 %final.1 = f32[2,25,64,384]{3,2,1,0:T(8,128)} custom-call(s32[32,128]{1,0:T(8,128)S(1)} %get-tuple-element.15.place_in, s32[8,128]{1,0:T(8,128)S(1)} %get-tuple-element.16.start_in, f32[2048,128]{1,0:T(8,128)S(1)} %bitcast.3, f32[4096,128]{1,0:T(8,128)S(1)} %get-tuple-element.17.mark_ref, f32[2,25,64,384]{3,2,1,0:T(8,128)} %get-tuple-element.18.part_hbm, ...), custom_call_target="tpu_custom_call" | custom-call | tf_op jit(solution)/shard_map/final/pallas_call | solution.py:602
Async XLA Ops:
  0.0 13.9 %copy-start = (f32[25,64,384]{2,1,0:T(8,128)S(1)}, f32[25,64,384]{2,1,0:T(8,128)}, u32[]{:S(2)}) copy-start(f32[25,64,384]{2,1,0:T(8,128)} %ev.1) | copy-start | bytes 7372804
  3.3 38.4 %all-to-all-start = ((f32[128,16,128]{2,1,0:T(8,128)}), f32[128,16,128]{2,1,0:T(8,128)S(1)}, u32[]{:S(2)}, u32[]{:S(2)}) async-start(f32[128,16,128]{2,1,0:T(8,128)} %melt.1), calls=%async_computation | async-start | bytes 2097152 | tf_op jit(solution)/shard_map/all_to_all | solution.py:636
  27.1 13.6 %collective-permute-start.2 = (f32[80,384]{1,0:T(8,128)S(1)}, f32[80,384]{1,0:T(8,128)S(1)}, u32[]{:S(2)}, u32[]{:S(2)}) collective-permute-start(f32[80,384]{1,0:T(8,128)S(1)} %get-tuple-element.20.ns_a), channel_id=1, source_target_pairs={{1,2},{3,4},{5,6},{9,10},{11,12},{13,14},{17,18},{19,20},{21,22},{... | collective-permute-start | bytes 368648 | tf_op jit(solution)/shard_map/ppermute | solution.py:626
  31.7 8.9 %collective-permute-start.3 = (f32[80,384]{1,0:T(8,128)S(1)}, f32[80,384]{1,0:T(8,128)S(1)}, u32[]{:S(2)}, u32[]{:S(2)}) collective-permute-start(f32[80,384]{1,0:T(8,128)S(1)} %get-tuple-element.21.ns_b), channel_id=1, source_target_pairs={{0,1},{2,3},{4,5},{6,7},{1,0},{3,2},{5,4},{7,6},{8,9},{10,11},{12,... | collective-permute-start | bytes 368648 | tf_op jit(solution)/shard_map/ppermute | solution.py:626
  32.0 8.6 %collective-permute-start.1 = (f32[64,256]{1,0:T(8,128)S(1)}, f32[64,256]{1,0:T(8,128)S(1)}, u32[]{:S(2)}, u32[]{:S(2)}) collective-permute-start(f32[64,256]{1,0:T(8,128)S(1)} %get-tuple-element.19.ew), channel_id=1, source_target_pairs={{8,16},{24,32},{40,48},{56,64},{72,80},{88,96},{104,112},{120,0},{... | collective-permute-start | bytes 196616 | tf_op jit(solution)/shard_map/ppermute | solution.py:626
  36.4 4.3 %collective-permute-start = (f32[64,256]{1,0:T(8,128)S(1)}, f32[64,256]{1,0:T(8,128)S(1)}, u32[]{:S(2)}, u32[]{:S(2)}) collective-permute-start(f32[64,256]{1,0:T(8,128)S(1)} %get-tuple-element.19.ew), channel_id=1, source_target_pairs={{0,8},{16,24},{32,40},{48,56},{64,72},{80,88},{96,104},{112,120},{... | collective-permute-start | bytes 196616 | tf_op jit(solution)/shard_map/ppermute | solution.py:626

commit v7 on v6

--- a/solution.py
+++ b/solution.py
@@ -125,8 +125,8 @@
 
 
 def stencil_kernel(
-    tr_hbm, ev, no_hbm, wet_hbm,
-    part_hbm, ew, ns_a, ns_b,
+    tr_hbm, ev, no_hbm, wet_hbm, cell_hbm, fold_hbm,
+    part_hbm, ew, ns_a, ns_b, cell_v, fold_v,
     tv, nv, ov, faces, wetf, wet_v, sem_t, sem_n, sem_o, sem_w,
 ):
     levels, rows, cols = no_hbm.shape
@@ -147,11 +147,17 @@
         span = pl.ds(sent[c], sent[c + 1] - sent[c])
         return pltpu.make_async_copy(ov.at[:, span], part_hbm.at[:, span], sem_o)
 
-    mask_copy = pltpu.make_async_copy(wet_hbm, wet_v, sem_w)
+    mask_copy = pltpu.make_async_copy(wet_hbm, wet_v, sem_w.at[0])
     mask_copy.start()
+    passed = (
+        pltpu.make_async_copy(cell_hbm, cell_v, sem_w.at[1]),
+        pltpu.make_async_copy(fold_hbm, fold_v, sem_w.at[2]),
+    )
     for c in range(AHEAD):
         for copy in copies(c):
             copy.start()
+    for copy in passed:
+        copy.start()
     mask_copy.wait()
     odd_lat = lax.rem(lax.axis_index("lat"), 2)
     row_a = odd_lat * (rows - 1)
@@ -271,10 +277,12 @@
     ew[:, 128:256] = jnp.where(
         lane_all < 2 * levels, pltpu.roll(speeds, 1, 1), pltpu.roll(speeds, 2 * levels + 1, 1)
     )
+    for copy in passed:
+        copy.wait()
     pltpu.make_async_copy(ov, part_hbm, sem_o).wait()
 
 
-def stencil(tracers, east_speed, north_speed, wet):
+def stencil(tracers, east_speed, north_speed, wet, cells, fold_partner):
     count, levels, rows, cols = tracers.shape
     edge_rows = -(-(3 * levels + 1) // 8) * 8
     dma = pltpu.SemaphoreType.DMA((len(FIRSTS),))
@@ -285,9 +293,11 @@
             jax.ShapeDtypeStruct((rows, 256), F32),
             jax.ShapeDtypeStruct((edge_rows, cols), F32),
             jax.ShapeDtypeStruct((edge_rows, cols), F32),
+            jax.ShapeDtypeStruct(cells.shape, cells.dtype),
+            jax.ShapeDtypeStruct(fold_partner.shape, fold_partner.dtype),
         ),
-        in_specs=[ANY_SPEC, VMEM_SPEC, ANY_SPEC, ANY_SPEC],
-        out_specs=(ANY_SPEC,) + (VMEM_SPEC,) * 3,
+        in_specs=[ANY_SPEC, VMEM_SPEC] + [ANY_SPEC] * 4,
+        out_specs=(ANY_SPEC,) + (VMEM_SPEC,) * 5,
         scratch_shapes=[
             VM(tracers.shape, F32),
             VM(north_speed.shape, F32),
@@ -298,11 +308,11 @@
             dma,
             dma,
             pltpu.SemaphoreType.DMA,
-            pltpu.SemaphoreType.DMA,
+            pltpu.SemaphoreType.DMA((3,)),
         ],
         compiler_params=pltpu.CompilerParams(vmem_limit_bytes=20 << 20),
         name="stencil",
-    )(*in_hbm(tracers), east_speed, *in_hbm(north_speed, wet))
+    )(*in_hbm(tracers), east_speed, *in_hbm(north_speed, wet, cells, fold_partner))
 
 
 def fix_kernel(
@@ -398,7 +408,7 @@
         scratch_shapes=[VM(own[1].shape, F32), VM(own[1].shape, F32)],
         compiler_params=pltpu.CompilerParams(vmem_limit_bytes=LIMIT),
         name="fix",
-    )(*in_hbm(fold_partner), *own, *far)
+    )(fold_partner, *own, *far)
 
 
 def order_kernel(cell_ref, place_ref, start_ref, mark_ref, base_ref, *, rows, cols, pairs):
@@ -444,8 +454,8 @@
             mark_ref[at : at + pairs, :] = turned[j * pairs : (j + 1) * pairs]
 
 
-def order(berg_cell, rows, cols, pairs):
-    count = berg_cell.shape[0]
+def order(cells, rows, cols, pairs):
+    count = cells.size
     blocks = count // 128
     return pl.pallas_call(
         functools.partial(order_kernel, rows=rows, cols=cols, pairs=pairs),
@@ -459,7 +469,7 @@
         scratch_shapes=[VM((blocks * rows, 128), F32)],
         compiler_params=pltpu.CompilerParams(vmem_limit_bytes=LIMIT),
         name="order",
-    )(*in_hbm(berg_cell.reshape(blocks, 128)))
+    )(cells)
 
 
 def final_kernel(
@@ -634,7 +644,10 @@
 
     melt = melt_rows(bergs, berg_count, melt_map)
     recv = lax.all_to_all(melt, ("lon", "lat"), split_axis=0, concat_axis=0, tiled=True)
-    part, *own = stencil(tracers, east_speed, north_speed, wet)
+    cells = berg_cell.reshape(-1, 128)
+    part, *own, cells, fold_partner = stencil(
+        tracers, east_speed, north_speed, wet, cells, fold_partner
+    )
     ew, ns_a, ns_b = own
 
     lon_even = [(i, i + 1) for i in range(0, lon_count, 2)]
@@ -657,7 +670,7 @@
     )
     fix = fixes(fold_partner, own, far, levels)
     pairs = melt.shape[1]
-    spots, start, mark = order(berg_cell, tracers.shape[2], cols, pairs)
+    spots, start, mark = order(cells, tracers.shape[2], cols, pairs)
     recv = recv.reshape(-1, 128)
     return finish(spots, start, recv, mark, part, wet, fix, pairs)
 

time: 52 us -> 51.1 us (0.983)
  Pallas kernels: 29 us -> 27.5 us
  waiting for transfers between devices: 2.78 us -> 3.49 us
    pallas_call x1, Pallas kernels: 1.52 us -> 0.8 us  [order(): pl.pallas_call(functools.partial(order_kernel, rows=rows, cols=cols, pair...]
    ppermute x4, waiting for transfers between devices: 2.77 us -> 3.49 us  [swap(): return lax.ppermute(value, axes, pairs + [(b, a) for a, b in pairs])]
    pallas_call x1, Pallas kernels: 1.09 us -> 0.41 us  [fixes(): pl.pallas_call(fix_kernel, out_shape=(jax.ShapeDtypeStruct((2, rows, 128)...]
  transfers between devices with their start and end apart: 5 -> 5, of which waited for: 1 -> 1; matrix products, arithmetic and copies ran while one was open for 0% -> 0% of each run, Pallas kernels for 31% -> 28%
where the time goes in v7:
time: 51.1 us; the launch traced here: 50.9 us
  Pallas kernels  27.5 us (54%)
  starting transfers between devices  19.8 us (39%)
  waiting for transfers between devices  3.49 us (7%)
    pallas_call x1, Pallas kernels, stencil(): pl.pallas_call(stencil_kernel, out_shape=(pltpu.HBM(tracers.shape, F32),...  13.1 us
    all_to_all x1, starting transfers between devices, shards(): lax.all_to_all(melt, ('lon', 'lat'), split_axis=0, concat_axis=0, tiled=T...  10.5 us
    pallas_call x1, Pallas kernels, finish(): pl.pallas_call(functools.partial(final_kernel, pairs=pairs), out_shape=ja...  9.87 us
    ppermute x4, starting transfers between devices, swap(): return lax.ppermute(value, axes, pairs + [(b, a) for a, b in pairs])  9.29 us
    ppermute x4, waiting for transfers between devices, swap(): return lax.ppermute(value, axes, pairs + [(b, a) for a, b in pairs])  3.49 us
    pallas_call x1, Pallas kernels, melt_rows(): pl.pallas_call(melt_kernel, out_shape=jax.ShapeDtypeStruct((owners, pairs...  3.34 us
  transfers between devices with their start and end apart: 5, of which 1 were waited for; matrix products, arithmetic and copies ran while one was open for 0% of the time, Pallas kernels for 28%

profile of v7, /device:TPU:4, one launch (start us, length us, event | category | flops | bytes accessed | tf_op | source)
XLA Modules:
  0.0 50.9 jit_solution(2256759643117032388)
XLA Ops:
  0.0 0.0 copy-start
  0.0 3.3 %melt.1 = f32[128,16,128]{2,1,0:T(8,128)} custom-call(s32[128]{0:T(128)} %count_hbm.1, f32[4096,128]{1,0:T(8,128)} %berg_hbm.1, f32[50,128]{1,0:T(8,128)} %bitcast.4), custom_call_target="tpu_custom_call" | custom-call | tf_op jit(solution)/shard_map/melt/pallas_call | solution.py:107
  3.3 10.5 %all-to-all-start = ((f32[128,16,128]{2,1,0:T(8,128)}), f32[128,16,128]{2,1,0:T(8,128)S(1)}, u32[]{:S(2)}, u32[]{:S(2)}) async-start(f32[128,16,128]{2,1,0:T(8,128)} %melt.1), calls=%async_computation | async-start | bytes 2097152 | tf_op jit(solution)/shard_map/all_to_all | solution.py:646
  13.9 0.0 copy-done
  13.9 13.1 %stencil.1 = (f32[2,25,64,384]{3,2,1,0:T(8,128)}, f32[64,256]{1,0:T(8,128)S(1)}, f32[80,384]{1,0:T(8,128)S(1)}, f32[80,384]{1,0:T(8,128)S(1)}, s32[32,128]{1,0:T(8,128)S(1)}, /*index=5*/s32[384]{0:T(512)S(1)}) custom-call(f32[2,25,64,384]{3,2,1,0:T(8,128)} %tr_hbm.1, f32[25,64,384]{2,1,0:T(8,128)S(1)} %copy-done, f32[25,64,384]{2,1,0:T(8,128)} %no_hbm.1, ...), custom_call_target="tpu_custom_call" | custom-call | tf_op jit(solution)/shard_map/stencil/pallas_call | solution.py:289
  27.0 4.6 %collective-permute-start.2 = (f32[80,384]{1,0:T(8,128)S(1)}, f32[80,384]{1,0:T(8,128)S(1)}, u32[]{:S(2)}, u32[]{:S(2)}) collective-permute-start(f32[80,384]{1,0:T(8,128)S(1)} %get-tuple-element.24.ns_a), channel_id=1, source_target_pairs={{1,2},{3,4},{5,6},{9,10},{11,12},{13,14},{17,18},{19,20},{21,22},{... | collective-permute-start | bytes 368648 | tf_op jit(solution)/shard_map/ppermute | solution.py:636
  31.6 0.3 collective-permute-start.3
  31.9 4.3 %collective-permute-start.1 = (f32[64,256]{1,0:T(8,128)S(1)}, f32[64,256]{1,0:T(8,128)S(1)}, u32[]{:S(2)}, u32[]{:S(2)}) collective-permute-start(f32[64,256]{1,0:T(8,128)S(1)} %get-tuple-element.23.ew), channel_id=1, source_target_pairs={{8,16},{24,32},{40,48},{56,64},{72,80},{88,96},{104,112},{120,0},{... | collective-permute-start | bytes 196616 | tf_op jit(solution)/shard_map/ppermute | solution.py:636
  36.3 0.0 collective-permute-start
  36.3 0.8 %order.1 = (s32[32,128]{1,0:T(8,128)S(1)}, s32[8,128]{1,0:T(8,128)S(1)}, f32[4096,128]{1,0:T(8,128)S(1)}) custom-call(s32[32,128]{1,0:T(8,128)S(1)} %get-tuple-element.17.cell_ref), custom_call_target="tpu_custom_call" | custom-call | tf_op jit(solution)/shard_map/order/pallas_call | solution.py:460
  37.1 3.5 %collective-permute-done.1.ew_b_in = f32[64,256]{1,0:T(8,128)S(1)} collective-permute-done((f32[64,256]{1,0:T(8,128)S(1)}, f32[64,256]{1,0:T(8,128)S(1)}, u32[]{:S(2)}, u32[]{:S(2)}) %collective-permute-start.1) | collective-permute-done | bytes 65568 | tf_op jit(solution)/shard_map/ppermute | solution.py:636
  40.6 0.0 collective-permute-done.ew_a_in
  40.6 0.0 collective-permute-done.2.ns_a_in
  40.6 0.0 collective-permute-done.3.ns_b_in
  40.6 0.4 fix.1
  41.0 0.0 all-to-all-done
  41.0 9.9 %final.1 = f32[2,25,64,384]{3,2,1,0:T(8,128)} custom-call(s32[32,128]{1,0:T(8,128)S(1)} %get-tuple-element.18.place_in, s32[8,128]{1,0:T(8,128)S(1)} %get-tuple-element.19.start_in, f32[2048,128]{1,0:T(8,128)S(1)} %bitcast.3, f32[4096,128]{1,0:T(8,128)S(1)} %get-tuple-element.20.mark_ref, f32[2,25,64,384]{3,2,1,0:T(8,128)} %get-tuple-element.21.part_hbm, ...), custom_call_target="tpu_custom_call" | custom-call | tf_op jit(solution)/shard_map/final/pallas_call | solution.py:612
Async XLA Ops:
  0.0 13.9 %copy-start = (f32[25,64,384]{2,1,0:T(8,128)S(1)}, f32[25,64,384]{2,1,0:T(8,128)}, u32[]{:S(2)}) copy-start(f32[25,64,384]{2,1,0:T(8,128)} %ev.1) | copy-start | bytes 7372804
  3.3 37.6 %all-to-all-start = ((f32[128,16,128]{2,1,0:T(8,128)}), f32[128,16,128]{2,1,0:T(8,128)S(1)}, u32[]{:S(2)}, u32[]{:S(2)}) async-start(f32[128,16,128]{2,1,0:T(8,128)} %melt.1), calls=%async_computation | async-start | bytes 2097152 | tf_op jit(solution)/shard_map/all_to_all | solution.py:646
  27.0 13.6 %collective-permute-start.2 = (f32[80,384]{1,0:T(8,128)S(1)}, f32[80,384]{1,0:T(8,128)S(1)}, u32[]{:S(2)}, u32[]{:S(2)}) collective-permute-start(f32[80,384]{1,0:T(8,128)S(1)} %get-tuple-element.24.ns_a), channel_id=1, source_target_pairs={{1,2},{3,4},{5,6},{9,10},{11,12},{13,14},{17,18},{19,20},{21,22},{... | collective-permute-start | bytes 368648 | tf_op jit(solution)/shard_map/ppermute | solution.py:636
  31.6 8.9 %collective-permute-start.3 = (f32[80,384]{1,0:T(8,128)S(1)}, f32[80,384]{1,0:T(8,128)S(1)}, u32[]{:S(2)}, u32[]{:S(2)}) collective-permute-start(f32[80,384]{1,0:T(8,128)S(1)} %get-tuple-element.25.ns_b), channel_id=1, source_target_pairs={{0,1},{2,3},{4,5},{6,7},{1,0},{3,2},{5,4},{7,6},{8,9},{10,11},{12,... | collective-permute-start | bytes 368648 | tf_op jit(solution)/shard_map/ppermute | solution.py:636
  31.9 8.6 %collective-permute-start.1 = (f32[64,256]{1,0:T(8,128)S(1)}, f32[64,256]{1,0:T(8,128)S(1)}, u32[]{:S(2)}, u32[]{:S(2)}) collective-permute-start(f32[64,256]{1,0:T(8,128)S(1)} %get-tuple-element.23.ew), channel_id=1, source_target_pairs={{8,16},{24,32},{40,48},{56,64},{72,80},{88,96},{104,112},{120,0},{... | collective-permute-start | bytes 196616 | tf_op jit(solution)/shard_map/ppermute | solution.py:636
  36.3 4.3 %collective-permute-start = (f32[64,256]{1,0:T(8,128)S(1)}, f32[64,256]{1,0:T(8,128)S(1)}, u32[]{:S(2)}, u32[]{:S(2)}) collective-permute-start(f32[64,256]{1,0:T(8,128)S(1)} %get-tuple-element.23.ew), channel_id=1, source_target_pairs={{0,8},{16,24},{32,40},{48,56},{64,72},{80,88},{96,104},{112,120},{... | collective-permute-start | bytes 196616 | tf_op jit(solution)/shard_map/ppermute | solution.py:636

commit v8 on v7

--- a/solution.py
+++ b/solution.py
@@ -411,7 +411,10 @@
     )(fold_partner, *own, *far)
 
 
-def order_kernel(cell_ref, place_ref, start_ref, mark_ref, base_ref, *, rows, cols, pairs):
+def order_kernel(
+    cell_ref, recv_ref, sorted_v, start_ref,
+    mark_ref, base_ref, rows_v, place_v, place_ref, sem, *, rows, cols, pairs,
+):
     blocks = cell_ref.shape[0]
     count = blocks * 128
     half = count // 2
@@ -438,7 +441,9 @@
         for j in range(per):
             extra = 2.0 * (c * per + j + 1)
             place = place + hot[c * per + j] * (spot[j * blocks : (j + 1) * blocks] + extra)
-    place_ref[...] = place.astype(jnp.int32)
+    place_v[...] = place.astype(jnp.int32)
+    to_scalars = pltpu.make_async_copy(place_v, place_ref, sem)
+    to_scalars.start()
     starts = base_ref[pl.ds(0, rows, stride=blocks), :]
     high = jnp.floor(starts * (1.0 / 128))
     low = starts - 128 * high
@@ -452,55 +457,7 @@
         for j in range(128 // pairs):
             at = (j % 2) * half + (i * (128 // pairs) + j) // 2 * pairs
             mark_ref[at : at + pairs, :] = turned[j * pairs : (j + 1) * pairs]
-
-
-def order(cells, rows, cols, pairs):
-    count = cells.size
-    blocks = count // 128
-    return pl.pallas_call(
-        functools.partial(order_kernel, rows=rows, cols=cols, pairs=pairs),
-        out_shape=(
-            jax.ShapeDtypeStruct((blocks, 128), jnp.int32),
-            jax.ShapeDtypeStruct((8, 128), jnp.int32),
-            jax.ShapeDtypeStruct((count, 128), F32),
-        ),
-        in_specs=[VMEM_SPEC],
-        out_specs=(VMEM_SPEC,) * 3,
-        scratch_shapes=[VM((blocks * rows, 128), F32)],
-        compiler_params=pltpu.CompilerParams(vmem_limit_bytes=LIMIT),
-        name="order",
-    )(cells)
-
-
-def final_kernel(
-    place_in, start_in, recv_ref, mark_ref, part_hbm, wet_hbm, fix_c, fix_n, fix_s,
-    out_hbm,
-    rows_v, sorted_v, pv, wet_v, wetf, acc, place_ref, start_ref, sem_i, sem_o, sem_s, *, pairs,
-):
-    _, levels, rows, cols = pv.shape
-    groups = rows // 8
-    tiles = cols // 128
-    maps = 2 * levels
-    n_rows = recv_ref.shape[0]
-    count = 2 * (n_rows + rows)
-
-    def load(i):
-        here = pl.ds(8 * PARTS[i], 8 * ((PARTS[1:] + (groups,))[i] - PARTS[i]))
-        return pltpu.make_async_copy(part_hbm.at[:, :, here], pv.at[:, :, here], sem_i.at[i])
-
-    def store(g):
-        here = pl.ds(pl.multiple_of(8 * g, 8), 8)
-        return pltpu.make_async_copy(pv.at[:, :, here], out_hbm.at[:, :, here], sem_o)
-
-    small = (
-        pltpu.make_async_copy(place_in, place_ref, sem_s.at[0]),
-        pltpu.make_async_copy(start_in, start_ref, sem_s.at[1]),
-        pltpu.make_async_copy(wet_hbm, wet_v, sem_s.at[2]),
-    )
-    for copy in small:
-        copy.start()
-    for i in range(len(PARTS)):
-        load(i).start()
+    n_rows = half
     lane_all = lax.broadcasted_iota(jnp.int32, (128, 128), 1)
     even = jnp.bitwise_and(lane_all, 1) == 0
     cell_lane = lane_all == CELL_LANE
@@ -521,17 +478,72 @@
         return _
 
     lax.fori_loop(0, n_rows // 128, halves, 0)
-    for copy in small:
-        copy.wait()
-    wetf[...] = wet_v[...].astype(F32)
-    sorted_v[count:, :] = jnp.full((WINDOW, 128), -1.0, F32)
-
+    filled = count + 2 * rows
+    sorted_v[filled:, :] = jnp.full((WINDOW, 128), -1.0, F32)
+    to_scalars.wait()
     for i in range(place_ref.shape[0]):
         first = i * 64
         for j in range(128):
             source, h, pair = j // (2 * pairs), j // pairs % 2, j % pairs
             line = rows_v[pl.ds(h * n_rows + first + source * pairs + pair, 1), :]
             sorted_v[pl.ds(place_ref[i, j], 1), :] = line
+
+
+def order(cells, recv, rows, cols, pairs):
+    count = cells.size
+    blocks = count // 128
+    return pl.pallas_call(
+        functools.partial(order_kernel, rows=rows, cols=cols, pairs=pairs),
+        out_shape=(
+            jax.ShapeDtypeStruct((count + 2 * rows + WINDOW, 128), F32),
+            jax.ShapeDtypeStruct((8, 128), jnp.int32),
+        ),
+        in_specs=[VMEM_SPEC] * 2,
+        out_specs=(VMEM_SPEC,) * 2,
+        scratch_shapes=[
+            VM((count, 128), F32),
+            VM((blocks * rows, 128), F32),
+            VM((count, 128), F32),
+            VM((blocks, 128), jnp.int32),
+            pltpu.SMEM((blocks, 128), jnp.int32),
+            pltpu.SemaphoreType.DMA,
+        ],
+        compiler_params=pltpu.CompilerParams(vmem_limit_bytes=LIMIT),
+        name="order",
+    )(cells, recv)
+
+
+def final_kernel(
+    sorted_in, start_in, part_hbm, wet_hbm, fix_c, fix_n, fix_s,
+    out_hbm,
+    sorted_v, pv, wet_v, wetf, acc, start_ref, sem_i, sem_o, sem_s,
+):
+    _, levels, rows, cols = pv.shape
+    groups = rows // 8
+    tiles = cols // 128
+    maps = 2 * levels
+
+    def load(i):
+        here = pl.ds(8 * PARTS[i], 8 * ((PARTS[1:] + (groups,))[i] - PARTS[i]))
+        return pltpu.make_async_copy(part_hbm.at[:, :, here], pv.at[:, :, here], sem_i.at[i])
+
+    def store(g):
+        here = pl.ds(pl.multiple_of(8 * g, 8), 8)
+        return pltpu.make_async_copy(pv.at[:, :, here], out_hbm.at[:, :, here], sem_o)
+
+    small = (
+        pltpu.make_async_copy(start_in, start_ref, sem_s.at[0]),
+        pltpu.make_async_copy(wet_hbm, wet_v, sem_s.at[1]),
+    )
+    for copy in small:
+        copy.start()
+    for i in range(len(PARTS)):
+        load(i).start()
+    sorted_v[...] = sorted_in[...]
+    for copy in small:
+        copy.wait()
+    wetf[...] = wet_v[...].astype(F32)
+
     for r in range(rows):
         first = start_ref[0, r]
         for h in range(2):
@@ -607,29 +619,27 @@
     pltpu.make_async_copy(pv, out_hbm, sem_o).wait()
 
 
-def finish(place, start, recv, mark, part, wet, fix, pairs):
+def finish(lines, start, part, wet, fix):
     _, levels, rows, cols = part.shape
     return pl.pallas_call(
-        functools.partial(final_kernel, pairs=pairs),
+        final_kernel,
         out_shape=jax.ShapeDtypeStruct(part.shape, F32),
-        in_specs=[VMEM_SPEC] * 4 + [ANY_SPEC] * 2 + [VMEM_SPEC] * 3,
+        in_specs=[VMEM_SPEC] * 2 + [ANY_SPEC] * 2 + [VMEM_SPEC] * 3,
         out_specs=ANY_SPEC,
         scratch_shapes=[
-            VM((2 * recv.shape[0], 128), F32),
-            VM((2 * recv.shape[0] + 2 * rows + WINDOW, 128), F32),
+            VM(lines.shape, F32),
             VM(part.shape, F32),
             VM((rows, cols), jnp.int32),
             VM((rows, cols), F32),
             VM((cols // 128, 9 * 128, 128), F32),
-            pltpu.SMEM(place.shape, jnp.int32),
             pltpu.SMEM(start.shape, jnp.int32),
             pltpu.SemaphoreType.DMA((len(PARTS),)),
             pltpu.SemaphoreType.DMA,
-            pltpu.SemaphoreType.DMA((3,)),
+            pltpu.SemaphoreType.DMA((2,)),
         ],
         compiler_params=pltpu.CompilerParams(vmem_limit_bytes=24 << 20),
         name="final",
-    )(place, start, recv, mark, *in_hbm(part, wet), *fix)
+    )(lines, start, *in_hbm(part, wet), *fix)
 
 
 def swap(value, axes, pairs):
@@ -668,11 +678,11 @@
         swap(ns_a, ("lon", "lat"), lat_odd),
         swap(ns_b, "lat", lat_even),
     )
+    recv = recv.reshape(-1, 128)
+    lines, start = order(cells, recv, tracers.shape[2], cols, melt.shape[1])
+    far, start = lax.optimization_barrier((far, start))
     fix = fixes(fold_partner, own, far, levels)
-    pairs = melt.shape[1]
-    spots, start, mark = order(cells, tracers.shape[2], cols, pairs)
-    recv = recv.reshape(-1, 128)
-    return finish(spots, start, recv, mark, part, wet, fix, pairs)
+    return finish(lines, start, part, wet, fix)
 
 
 def solution(mesh):

time: 51.1 us -> 51.3 us (level); the launches traced: 50.9 us -> 50.4 us
  waiting for transfers between devices: 3.49 us -> 0.01 us
  Pallas kernels: 27.5 us -> 30.5 us
    pallas_call x1, Pallas kernels: 0.8 us -> 4.55 us  [order(): pl.pallas_call(functools.partial(order_kernel, rows=rows, cols=cols, pair...]
    ppermute x4, waiting for transfers between devices: 3.49 us -> 0.01 us  [swap(): return lax.ppermute(value, axes, pairs + [(b, a) for a, b in pairs])]
    pallas_call x1, Pallas kernels: 9.87 us -> 7.39 us  [finish(): pl.pallas_call(final_kernel, out_shape=jax.ShapeDtypeStruct(part.shape, F...]
    pallas_call x1, Pallas kernels: 0.41 us -> 1.39 us  [fixes(): pl.pallas_call(fix_kernel, out_shape=(jax.ShapeDtypeStruct((2, rows, 128)...]
    pallas_call x1, Pallas kernels: 13.1 us -> 13.8 us  [stencil(): pl.pallas_call(stencil_kernel, out_shape=(pltpu.HBM(tracers.shape, F32),...]
  transfers between devices with their start and end apart: 5 -> 5, of which waited for: 1 -> 0; matrix products, arithmetic and copies ran while one was open for 0% -> 0% of each run, Pallas kernels for 28% -> 36%
where the time goes in v8:
time: 51.3 us; the launch traced here: 50.4 us
  Pallas kernels  30.5 us (59%)
  starting transfers between devices  19.8 us (39%)
    pallas_call x1, Pallas kernels, stencil(): pl.pallas_call(stencil_kernel, out_shape=(pltpu.HBM(tracers.shape, F32),...  13.8 us
    all_to_all x1, starting transfers between devices, shards(): lax.all_to_all(melt, ('lon', 'lat'), split_axis=0, concat_axis=0, tiled=T...  10.5 us
    ppermute x4, starting transfers between devices, swap(): return lax.ppermute(value, axes, pairs + [(b, a) for a, b in pairs])  9.28 us
    pallas_call x1, Pallas kernels, finish(): pl.pallas_call(final_kernel, out_shape=jax.ShapeDtypeStruct(part.shape, F...  7.39 us
    pallas_call x1, Pallas kernels, order(): pl.pallas_call(functools.partial(order_kernel, rows=rows, cols=cols, pair...  4.55 us
    pallas_call x1, Pallas kernels, melt_rows(): pl.pallas_call(melt_kernel, out_shape=jax.ShapeDtypeStruct((owners, pairs...  3.34 us
    pallas_call x1, Pallas kernels, fixes(): pl.pallas_call(fix_kernel, out_shape=(jax.ShapeDtypeStruct((2, rows, 128)...  1.39 us
  transfers between devices with their start and end apart: 5, of which 0 were waited for; matrix products, arithmetic and copies ran while one was open for 0% of the time, Pallas kernels for 36%

profile of v8, /device:TPU:4, one launch (start us, length us, event | category | flops | bytes accessed | tf_op | source)
XLA Modules:
  0.0 50.4 jit_solution(14624509083386739002)
XLA Ops:
  0.0 0.0 copy-start
  0.0 3.3 %melt.1 = f32[128,16,128]{2,1,0:T(8,128)} custom-call(s32[128]{0:T(128)} %count_hbm.1, f32[4096,128]{1,0:T(8,128)} %berg_hbm.1, f32[50,128]{1,0:T(8,128)} %bitcast.4), custom_call_target="tpu_custom_call" | custom-call | tf_op jit(solution)/shard_map/melt/pallas_call | solution.py:107
  3.3 10.5 %all-to-all-start = ((f32[128,16,128]{2,1,0:T(8,128)}), f32[128,16,128]{2,1,0:T(8,128)S(1)}, u32[]{:S(2)}, u32[]{:S(2)}) async-start(f32[128,16,128]{2,1,0:T(8,128)} %melt.1), calls=%async_computation | async-start | bytes 2097152 | tf_op jit(solution)/shard_map/all_to_all | solution.py:656
  13.9 0.0 copy-done
  13.9 13.8 %stencil.1 = (f32[2,25,64,384]{3,2,1,0:T(8,128)}, f32[64,256]{1,0:T(8,128)}, f32[80,384]{1,0:T(8,128)}, f32[80,384]{1,0:T(8,128)}, s32[32,128]{1,0:T(8,128)S(1)}, /*index=5*/s32[384]{0:T(512)S(1)}) custom-call(f32[2,25,64,384]{3,2,1,0:T(8,128)} %tr_hbm.1, f32[25,64,384]{2,1,0:T(8,128)S(1)} %copy-done, f32[25,64,384]{2,1,0:T(8,128)} %no_hbm.1, ...), custom_call_target="tpu_custom_call" | custom-call | tf_op jit(solution)/shard_map/stencil/pallas_call | solution.py:289
  27.7 4.6 %collective-permute-start.2 = (f32[80,384]{1,0:T(8,128)}, f32[80,384]{1,0:T(8,128)S(1)}, u32[]{:S(2)}, u32[]{:S(2)}) collective-permute-start(f32[80,384]{1,0:T(8,128)} %get-tuple-element.24.ns_a), channel_id=1, source_target_pairs={{1,2},{3,4},{5,6},{9,10},{11,12},{13,14},{17,18},{19,20},{21,22},{... | collective-permute-start | bytes 368648 | tf_op jit(solution)/shard_map/ppermute | solution.py:646
  32.3 0.3 collective-permute-start.3
  32.6 4.3 %collective-permute-start.1 = (f32[64,256]{1,0:T(8,128)}, f32[64,256]{1,0:T(8,128)S(1)}, u32[]{:S(2)}, u32[]{:S(2)}) collective-permute-start(f32[64,256]{1,0:T(8,128)} %get-tuple-element.23.ew), channel_id=1, source_target_pairs={{8,16},{24,32},{40,48},{56,64},{72,80},{88,96},{104,112},{120,0},{... | collective-permute-start | bytes 196616 | tf_op jit(solution)/shard_map/ppermute | solution.py:646
  37.0 0.0 collective-permute-start
  37.0 0.0 all-to-all-done
  37.0 4.5 %order.1 = (f32[4352,128]{1,0:T(8,128)S(1)}, s32[8,128]{1,0:T(8,128)S(1)}) custom-call(s32[32,128]{1,0:T(8,128)S(1)} %get-tuple-element.21.cell_ref, f32[2048,128]{1,0:T(8,128)S(1)} %bitcast.3), custom_call_target="tpu_custom_call" | custom-call | tf_op jit(solution)/shard_map/order/pallas_call | solution.py:495
  41.5 0.0 collective-permute-done.1.ew_b_in
  41.5 0.0 collective-permute-done.ew_a_in
  41.5 0.0 collective-permute-done.2.ns_a_in
  41.6 0.0 collective-permute-done.3.ns_b_in
  41.6 1.4 %fix.1 = (f32[2,64,128]{2,1,0:T(8,128)S(1)}, f32[50,384]{1,0:T(8,128)S(1)}, f32[50,384]{1,0:T(8,128)S(1)}) custom-call(s32[384]{0:T(512)S(1)} %get-tuple-element.29.fold_ref, f32[64,256]{1,0:T(8,128)} %get-tuple-element.23.ew, f32[80,384]{1,0:T(8,128)} %get-tuple-element.24.ns_a, f32[80,384]{1,0:T(8,128)} %get-tuple-element.25.ns_b, ...), custom_call_target="tpu_custom_call" | custom-call | tf_op jit(solution)/shard_map/fix/pallas_call | solution.py:399
  43.0 7.4 %final.1 = f32[2,25,64,384]{3,2,1,0:T(8,128)} custom-call(f32[4352,128]{1,0:T(8,128)S(1)} %get-tuple-element.22.sorted_in, s32[8,128]{1,0:T(8,128)S(1)} %get-tuple-element.27.start_in, f32[2,25,64,384]{3,2,1,0:T(8,128)} %get-tuple-element.28.part_hbm, s32[64,384]{1,0:T(8,128)} %wet_hbm.3, f32[2,64,128]{2,1,0:T(8,128)S(1)} %get-tuple-element.34.fix_c, ...), custom_call_target="tpu_custom_call" | custom-call | tf_op jit(solution)/shard_map/final/pallas_call | solution.py:624
Async XLA Ops:
  0.0 13.9 %copy-start = (f32[25,64,384]{2,1,0:T(8,128)S(1)}, f32[25,64,384]{2,1,0:T(8,128)}, u32[]{:S(2)}) copy-start(f32[25,64,384]{2,1,0:T(8,128)} %ev.1) | copy-start | bytes 7372804
  3.3 33.6 %all-to-all-start = ((f32[128,16,128]{2,1,0:T(8,128)}), f32[128,16,128]{2,1,0:T(8,128)S(1)}, u32[]{:S(2)}, u32[]{:S(2)}) async-start(f32[128,16,128]{2,1,0:T(8,128)} %melt.1), calls=%async_computation | async-start | bytes 2097152 | tf_op jit(solution)/shard_map/all_to_all | solution.py:656
  27.7 13.9 %collective-permute-start.2 = (f32[80,384]{1,0:T(8,128)}, f32[80,384]{1,0:T(8,128)S(1)}, u32[]{:S(2)}, u32[]{:S(2)}) collective-permute-start(f32[80,384]{1,0:T(8,128)} %get-tuple-element.24.ns_a), channel_id=1, source_target_pairs={{1,2},{3,4},{5,6},{9,10},{11,12},{13,14},{17,18},{19,20},{21,22},{... | collective-permute-start | bytes 368648 | tf_op jit(solution)/shard_map/ppermute | solution.py:646
  32.3 9.2 %collective-permute-start.3 = (f32[80,384]{1,0:T(8,128)}, f32[80,384]{1,0:T(8,128)S(1)}, u32[]{:S(2)}, u32[]{:S(2)}) collective-permute-start(f32[80,384]{1,0:T(8,128)} %get-tuple-element.25.ns_b), channel_id=1, source_target_pairs={{0,1},{2,3},{4,5},{6,7},{1,0},{3,2},{5,4},{7,6},{8,9},{10,11},{12,... | collective-permute-start | bytes 368648 | tf_op jit(solution)/shard_map/ppermute | solution.py:646
  32.6 8.9 %collective-permute-start.1 = (f32[64,256]{1,0:T(8,128)}, f32[64,256]{1,0:T(8,128)S(1)}, u32[]{:S(2)}, u32[]{:S(2)}) collective-permute-start(f32[64,256]{1,0:T(8,128)} %get-tuple-element.23.ew), channel_id=1, source_target_pairs={{8,16},{24,32},{40,48},{56,64},{72,80},{88,96},{104,112},{120,0},{... | collective-permute-start | bytes 196616 | tf_op jit(solution)/shard_map/ppermute | solution.py:646
  37.0 4.6 %collective-permute-start = (f32[64,256]{1,0:T(8,128)}, f32[64,256]{1,0:T(8,128)S(1)}, u32[]{:S(2)}, u32[]{:S(2)}) collective-permute-start(f32[64,256]{1,0:T(8,128)} %get-tuple-element.23.ew), channel_id=1, source_target_pairs={{0,8},{16,24},{32,40},{48,56},{64,72},{80,88},{96,104},{112,120},{... | collective-permute-start | bytes 196616 | tf_op jit(solution)/shard_map/ppermute | solution.py:646
